TPU v7x, 32 devices: a whole 2x2x4 slice. The times are simulated.
32 devices in a mesh: az: 4 (over z), rad: 2 (over x), ax: 4 (over y, core).
Axes of the slice: x: 2, y: 2, z: 4, core: 2. Of those that a mesh axis runs over, the one named last changes fastest.
Arguments:
- cycle: float32 [4, 5, 512, 4096], P(None, None, ('rad', 'ax'), 'az'), may hold values from -6 to 6
- field: float32 [5, 64, 8, 4096], P(None, 'rad', 'ax', 'az'), may hold values from -6 to 6
- shift: int32 [1], replicated, may hold values from 0 to 4095
- owner: int32 [64, 8], P('rad', 'ax'), may hold values 0 or 1
Outputs:
- field_next: float32 [5, 64, 8, 4096], P(None, 'rad', 'ax', 'az')
- shifted_cycle: float32 [4, 5, 512, 4096], P(None, None, ('rad', 'ax'), 'az')
All inputs are finite; a program needn't handle non-finite values. No bound on the sum of `owner` on one device may be relied on, other than what follows from the above.
Results may differ from a plain program's by a relative error of at most 0.00007.
Values sent between devices are 32-bit elements; how exact they have to be, the bound alone decides.
A program may use at most 192 MiB of HBM per device.

v0:
```python
import math

import jax
import jax.numpy as jnp
from jax import lax
from jax.sharding import PartitionSpec as P

KR = 8


LAYER_WEIGHTS = (0.4, 0.3, 0.2, 0.1)
AXIAL_SPEEDS = (0.35, 0.2, 0.3, 0.25, 0.4)
DIFFUSION = 0.15
SWIRL_SPEED = 0.1


def padded(array, sides, width):
    for axis, dim in sides:
        devices, length = (lax.axis_size(axis), array.shape[dim])
        up = [(i, (i + 1) % devices) for i in range(devices - 1)]
        down = [(j, i) for i, j in up]
        last = lax.slice_in_dim(array, length - width, length, axis=dim)
        leading = lax.slice_in_dim(array, 0, width, axis=dim)
        before = lax.ppermute(last, axis, up)
        after = lax.ppermute(leading, axis, down)
        array = jnp.concatenate([before, array, after], axis=dim)
    return array


def turn_table(first, second, modulus):
    product = jnp.remainder(first[:, None] * second[None, :], modulus).astype(jnp.float32)
    angle = product * (2.0 * math.pi / modulus)
    return (jnp.cos(angle), jnp.sin(angle))


def spectral_shift(rows, shift_value):
    count, length = rows.shape
    half_bits = (length.bit_length() - 1) // 2
    outer = 2**half_bits
    inner = length // outer
    hp = lax.Precision.HIGHEST
    outer_index = jnp.arange(outer, dtype=jnp.int32)
    inner_index = jnp.arange(inner, dtype=jnp.int32)
    cos_outer, sin_outer = turn_table(outer_index, outer_index, outer)
    cos_inner, sin_inner = turn_table(inner_index, inner_index, inner)
    cos_twist, sin_twist = turn_table(outer_index, inner_index, length)
    grid = rows.reshape(count, outer, inner)
    section_re = jnp.einsum("bpq,pk->bkq", grid, cos_outer, precision=hp)
    section_im = -jnp.einsum("bpq,pk->bkq", grid, sin_outer, precision=hp)
    twist_re = section_re * cos_twist + section_im * sin_twist
    twist_im = section_im * cos_twist - section_re * sin_twist
    spec_re = jnp.einsum("bkq,qm->bkm", twist_re, cos_inner, precision=hp) + jnp.einsum(
        "bkq,qm->bkm", twist_im, sin_inner, precision=hp
    )
    spec_im = jnp.einsum("bkq,qm->bkm", twist_im, cos_inner, precision=hp) - jnp.einsum(
        "bkq,qm->bkm", twist_re, sin_inner, precision=hp
    )
    wave = outer_index[:, None] + outer * inner_index[None, :]
    folded = jnp.minimum(wave, length - wave)
    filt = (3 * folded < length).astype(jnp.float32)
    phase = jnp.remainder(wave * shift_value, length).astype(jnp.float32) * (2.0 * math.pi / length)
    gain_re = filt * jnp.cos(phase)
    gain_im = -filt * jnp.sin(phase)
    mixed_re = spec_re * gain_re - spec_im * gain_im
    mixed_im = spec_re * gain_im + spec_im * gain_re
    back_re = jnp.einsum("bkm,qm->bkq", mixed_re, cos_inner, precision=hp) - jnp.einsum(
        "bkm,qm->bkq", mixed_im, sin_inner, precision=hp
    )
    back_im = jnp.einsum("bkm,qm->bkq", mixed_im, cos_inner, precision=hp) + jnp.einsum(
        "bkm,qm->bkq", mixed_re, sin_inner, precision=hp
    )
    turn_re = back_re * cos_twist - back_im * sin_twist
    turn_im = back_im * cos_twist + back_re * sin_twist
    result = jnp.einsum("bkq,pk->bpq", turn_re, cos_outer, precision=hp) - jnp.einsum(
        "bkq,pk->bpq", turn_im, sin_outer, precision=hp
    )
    return (result / length).reshape(count, length)


def on_device(cycle, field, shift, owner):
    layers, variables, radial, sector = cycle.shape
    stacked = cycle.reshape(layers * variables, radial, sector)
    shift_value = shift[0]
    piece = lax.all_to_all(stacked, "az", split_axis=1, concat_axis=2, tiled=True)
    moved = spectral_shift(piece.reshape(-1, piece.shape[2]), shift_value).reshape(piece.shape)
    shifted_flat = lax.all_to_all(moved, "az", split_axis=2, concat_axis=1, tiled=True)
    shifted_cycle = shifted_flat.reshape(layers, variables, radial, sector)
    weights = jnp.array(LAYER_WEIGHTS, jnp.float32)
    depth, count, rows, width = shifted_cycle.shape
    grouped = shifted_cycle.reshape(depth, count, rows // KR, KR, width)
    ghost = lax.all_gather(
        jnp.einsum("l,lvrkt->vrt", weights, grouped, precision=lax.Precision.HIGHEST) / KR,
        "ax",
        axis=1,
        tiled=True,
    )
    mask = owner.astype(jnp.float32)[None, :, :, None]
    speeds = jnp.array(AXIAL_SPEEDS, jnp.float32)[:, None, None, None]
    at_inlet = lax.axis_index("ax") == 0

    def rates(state):
        radial_pad = padded(state, (("rad", 1),), 1)
        axial_pad = padded(state, (("ax", 2),), 1)
        lower = jnp.where(at_inlet, ghost, axial_pad[:, :, 0])
        outward = radial_pad[:, 2:]
        inward = radial_pad[:, :-2]
        above = axial_pad[:, :, 2:]
        below = jnp.concatenate([lower[:, :, None], axial_pad[:, :, 1:-2]], axis=2)
        return mask * (
            DIFFUSION * (outward + inward + above + below - 4.0 * state)
            - 0.5 * speeds * (above - below)
            - 0.5 * SWIRL_SPEED * (outward - inward)
        )

    first = rates(field)
    second = rates(field + 0.5 * first)
    third = rates(field + 0.5 * second)
    fourth = rates(field + third)
    field_next = field + (first + 2.0 * second + 2.0 * third + fourth) / 6.0
    return (field_next, shifted_cycle)


def solution(mesh):
    in_specs = (P(None, None, ("rad", "ax"), "az"), P(None, "rad", "ax", "az"), P(), P("rad", "ax"))
    out_specs = (P(None, "rad", "ax", "az"), P(None, None, ("rad", "ax"), "az"))
    return jax.shard_map(
        on_device, mesh=mesh, in_specs=in_specs, out_specs=out_specs, check_vma=False
    )
```

profile of v0, /device:TPU:0, one launch (start us, length us, event | category | flops | bytes accessed | tf_op | source)
XLA Modules:
  0.0 714.0 jit_solution(15796967327889109579)
XLA Ops:
  0.6 8.2 %copy.187 = f32[20,64,1024]{2,0,1:T(8,128)} copy(f32[20,64,1024]{2,1,0:T(8,128)} %bitcast.97) | data formatting | bytes 10485760 | tf_op jit(solution)/shard_map/reshape | solution.py:82
  8.8 6.5 all-to-all-start
  15.4 0.1 fusion.62
  16.3 0.2 cosine_select_fusion
  16.5 137.6 %all-to-all-done = f32[20,64,1024]{2,0,1:T(8,128)} async-done(((f32[20,64,1024]{2,0,1:T(8,128)}), f32[20,64,1024]{2,0,1:T(8,128)}, u32[]{:S(2)}, u32[]{:S(2)}) %all-to-all-start) | async-done | bytes 5242912 | tf_op jit(solution)/shard_map/all_to_all | solution.py:84
  154.1 8.5 %copy.189 = f32[20,16,4,1024]{3,2,1,0:T(4,128)} copy(f32[20,16,4,1024]{3,0,1,2:T(8,128)} %bitcast.5) | data formatting | bytes 10485760 | tf_op jit(solution)/shard_map/all_to_all | solution.py:84
  162.6 9.6 %reshape_reshape.9 = f32[320,64,64]{2,1,0:T(8,128)} reshape(f32[20,16,4,1024]{3,2,1,0:T(4,128)} %copy.189) | data formatting | bytes 10485760 | tf_op jit(solution)/shard_map/reshape;reshape | solution.py:47
  172.2 11.8 %copy.191 = f32[320,64,64]{0,1,2:T(8,128)} copy(f32[320,64,64]{2,1,0:T(8,128)} %reshape_reshape.9) | data formatting | bytes 10485760 | tf_op jit(solution)/shard_map/reshape;reshape | solution.py:47
  184.1 8.7 %fusion.44 = f32[64,320,64]{1,0,2:T(8,128)S(1)} fusion(f32[320,64,64]{0,1,2:T(8,128)} %copy.191), kind=kOutput, calls=%fused_computation.85 | convolution fusion | flops 1006690304 | bytes 10485760 | tf_op jit(solution)/shard_map/bpq,pk->bkq/dot_general | solution.py:49
  192.8 7.6 %add_bitcast_fusion = (f32[320,64,64]{0,1,2:T(8,128)S(1)}, f32[320,64,64]{0,1,2:T(8,128)S(1)}) fusion(f32[64,320,64]{1,0,2:T(8,128)S(1)} %fusion.44, f32[64,64]{0,1:T(8,128)S(1)} %copy.195, f32[64,64]{0,1:T(8,128)S(1)} %copy.192, f32[320,64,64]{0,1,2:T(8,128)S(1)} %copy-done.2), kind=kOutput, calls=%fused_computation.10 | convolution fusion | flops 1015865344 | bytes 21004288 | tf_op jit(solution)/shard_map/bpq,pk->bkq/dot_general | solution.py:48
  200.4 14.0 %fusion.10 = f32[320,64,64]{0,2,1:T(8,128)} fusion(f32[320,64,64]{0,1,2:T(8,128)S(1)} %get-tuple-element.16), kind=kOutput, calls=%fused_computation.17 | convolution fusion | flops 1006690304 | bytes 10485760 | tf_op jit(solution)/shard_map/bkq,qm->bkm/dot_general | solution.py:52
  214.4 13.2 %fusion.8 = f32[320,64,64]{0,2,1:T(8,128)} fusion(f32[320,64,64]{0,1,2:T(8,128)S(1)} %get-tuple-element.16), kind=kOutput, calls=%fused_computation.15 | convolution fusion | flops 1006690304 | bytes 10485760 | tf_op jit(solution)/shard_map/bkq,qm->bkm/dot_general | solution.py:55
  227.6 13.3 %fusion.6 = f32[320,64,64]{0,2,1:T(8,128)} fusion(f32[320,64,64]{0,1,2:T(8,128)S(1)} %get-tuple-element.17), kind=kOutput, calls=%fused_computation.13 | convolution fusion | flops 1006690304 | bytes 10485760 | tf_op jit(solution)/shard_map/bkq,qm->bkm/dot_general | solution.py:52
  240.9 19.1 %multiply_subtract_fusion.1 = (f32[320,64,64]{0,2,1:T(8,128)}, f32[320,64,64]{0,2,1:T(8,128)S(1)}) fusion(f32[64,64]{1,0:T(8,128)S(1)} %get-tuple-element.35, f32[64,64]{1,0:T(8,128)S(1)} %get-tuple-element.34, f32[320,64,64]{0,2,1:T(8,128)} %fusion.8, f32[320,64,64]{0,2,1:T(8,128)} %fusion.10, f32[320,64,64]{0,2,1:T(8,128)} %fusion.6, ...), kind=kOutput, calls=%fused_computation.8 | convolution fusion | flops 1017176064 | bytes 31490048 | tf_op jit(solution)/shard_map/bkq,qm->bkm/dot_general | solution.py:55
  260.0 10.3 %fusion.38 = f32[320,64,64]{0,2,1:T(8,128)} fusion(f32[320,64,64]{0,2,1:T(8,128)} %get-tuple-element.14), kind=kOutput, calls=%fused_computation.79 | convolution fusion | flops 1006690304 | bytes 10485760 | tf_op jit(solution)/shard_map/bkm,qm->bkq/dot_general | solution.py:69
  270.3 7.8 %fusion.53 = f32[320,64,64]{0,2,1:T(8,128)} fusion(f32[320,64,64]{0,2,1:T(8,128)S(1)} %copy-done), kind=kOutput, calls=%fused_computation.94 | convolution fusion | flops 1006690304 | bytes 10485760 | tf_op jit(solution)/shard_map/bkm,qm->bkq/dot_general | solution.py:66
  278.1 7.9 %fusion.40 = f32[320,64,64]{0,2,1:T(8,128)} fusion(f32[320,64,64]{0,2,1:T(8,128)S(1)} %get-tuple-element.15), kind=kOutput, calls=%fused_computation.81 | convolution fusion | flops 1006690304 | bytes 10485760 | tf_op jit(solution)/shard_map/bkm,qm->bkq/dot_general | solution.py:66
  286.0 15.2 %multiply_subtract_fusion = (f32[320,64,64]{0,2,1:T(8,128)}, f32[320,64,64]{0,2,1:T(8,128)}) fusion(f32[64,64]{1,0:T(8,128)S(1)} %get-tuple-element.36, f32[64,64]{1,0:T(8,128)S(1)} %get-tuple-element.37, f32[320,64,64]{0,2,1:T(8,128)} %fusion.38, f32[320,64,64]{0,2,1:T(8,128)} %fusion.53, f32[320,64,64]{0,2,1:T(8,128)} %fusion.40, ...), kind=kOutput, calls=%fused_computation.6 | convolution fusion | flops 1017176064 | bytes 31490048 | tf_op jit(solution)/shard_map/bkm,qm->bkq/dot_general | solution.py:69
  301.2 12.4 %fusion = f32[64,320,64]{1,0,2:T(8,128)S(1)} fusion(f32[320,64,64]{0,2,1:T(8,128)} %get-tuple-element.13), kind=kOutput, calls=%fused_computation | convolution fusion | flops 1006690304 | bytes 10485760 | tf_op jit(solution)/shard_map/bkq,pk->bpq/dot_general | solution.py:74
  313.6 11.2 %multiply_bitcast_fusion = f32[320,64,64]{0,1,2:T(8,128)} fusion(f32[64,320,64]{1,0,2:T(8,128)S(1)} %fusion, f32[320,64,64]{0,2,1:T(8,128)S(1)} %copy-done.3), kind=kOutput, calls=%fused_computation.4 | convolution fusion | flops 1009311744 | bytes 15728640 | tf_op jit(solution)/shard_map/bkq,pk->bpq/dot_general | solution.py:74
  324.8 12.6 %copy.206 = f32[320,64,64]{2,1,0:T(8,128)} copy(f32[320,64,64]{0,1,2:T(8,128)} %multiply_bitcast_fusion) | data formatting | bytes 10485760 | tf_op jit(solution)/shard_map/div | solution.py:77
  337.4 9.7 %reshape_reshape.10 = f32[20,16,4096]{2,1,0:T(8,128)} reshape(f32[320,64,64]{2,1,0:T(8,128)} %copy.206) | data formatting | bytes 10485760 | tf_op jit(solution)/shard_map/reshape;reshape | solution.py:85
  347.1 18.7 %copy.207 = f32[20,16,4096]{0,1,2:T(8,128)} copy(f32[20,16,4096]{2,1,0:T(8,128)} %reshape_reshape.10) | data formatting | bytes 10485760 | tf_op jit(solution)/shard_map/reshape;reshape | solution.py:85
  365.9 56.1 %reshape.131 = f32[4,1,327680]{2,1,0:T(1,128)} reshape(f32[4096,16,20]{2,1,0:T(8,128)} %bitcast.92) | data formatting | bytes 10485760
  422.0 5.2 all-to-all-start.1
  427.2 0.4 copy.215
  427.7 1.0 fusion.132
  428.6 2.2 collective-permute-start.3
  430.8 1.3 collective-permute-start.2
  432.2 1.3 collective-permute-start
  433.5 4.5 collective-permute-start.1
  438.1 104.5 %all-to-all-done.1 = f32[4,1,327680]{2,1,0:T(1,128)} async-done(((f32[4,1,327680]{2,1,0:T(1,128)}), f32[4,1,327680]{2,1,0:T(1,128)}, u32[]{:S(2)}, u32[]{:S(2)}) %all-to-all-start.1) | async-done | bytes 5242912 | tf_op jit(solution)/shard_map/all_to_all | solution.py:86
  542.6 0.6 broadcast.363
  543.2 18.3 %reduce = f32[4,327680]{1,0:T(4,128)} reduce(f32[4,1,327680]{2,1,0:T(1,128)} %all-to-all-done.1, f32[]{:T(128)} %broadcast.363), dimensions={1}, to_apply=%all_to_all.25.reduce_sub_computation | reduce | bytes 10485764 | tf_op jit(solution)/shard_map/all_to_all | solution.py:86
  561.5 52.9 %reshape.132 = f32[4096,16,20]{2,1,0:T(8,128)} reshape(f32[4,327680]{1,0:T(4,128)} %reduce) | data formatting | bytes 10485760
  614.4 22.4 %copy.234 = f32[20,16,4,1024]{3,2,1,0:T(4,128)} copy(f32[20,16,4,1024]{0,1,3,2:T(8,128)} %bitcast.93) | data formatting | bytes 10485760 | tf_op jit(solution)/shard_map/all_to_all | solution.py:86
  636.8 9.2 %copy.209 = f32[20,4,16,1024]{3,2,1,0:T(8,128)} copy(f32[20,4,16,1024]{3,1,2,0:T(4,128)} %bitcast.94) | data formatting | bytes 10485760 | tf_op jit(solution)/shard_map/all_to_all | solution.py:86
  646.0 4.6 reduce_sum.9
  650.5 2.7 fusion.26
  653.3 7.7 %all_gather.3 = f32[5,32,1024]{2,1,0:T(8,128)S(1)} all-gather(f32[5,8,1024]{2,1,0:T(8,128)S(1)} %bitcast_multiply_fusion), channel_id=1, replica_groups=mesh['az'=4,'rad'=2,'ax'=4] {'ax'}, dimensions={1}, use_global_device_ids=true | all-gather | bytes 819200 | tf_op jit(solution)/shard_map/all_gather | solution.py:91
  661.0 1.2 fusion.25
  662.2 2.0 multiply_add_fusion.4
  664.3 2.3 collective-permute-start.7
  666.6 1.3 collective-permute-start.6
  668.0 1.3 collective-permute-start.4
  669.3 4.5 collective-permute-start.5
  674.0 0.2 collective-permute-done.4
  674.2 1.5 collective-permute-done.5
  675.7 1.1 multiply_add_fusion.3
  676.9 5.3 collective-permute-start.11
  682.2 1.3 collective-permute-start.10
  683.6 1.3 collective-permute-start.8
  684.9 4.8 collective-permute-start.9
  689.8 1.4 collective-permute-done.9
  691.2 1.0 copy_add_fusion
  692.3 0.1 fusion.127
  692.4 4.8 collective-permute-start.15
  697.2 1.3 collective-permute-start.14
  698.6 1.3 collective-permute-start.12
  699.9 4.5 collective-permute-start.13
  704.5 0.2 collective-permute-done.12
  704.7 1.5 collective-permute-done.13
  706.2 5.5 multiply_add_fusion.2
  711.7 2.1 copy.217
  (43 shorter events, 1.1 us)
Async XLA Ops:
  8.8 145.2 %all-to-all-start = ((f32[20,64,1024]{2,0,1:T(8,128)}), f32[20,64,1024]{2,0,1:T(8,128)}, u32[]{:S(2)}, u32[]{:S(2)}) async-start(f32[20,64,1024]{2,0,1:T(8,128)} %copy.187), calls=%async_computation | async-start | bytes 12582912 | tf_op jit(solution)/shard_map/all_to_all | solution.py:84
  184.1 8.7 %copy-start.2 = (f32[320,64,64]{0,1,2:T(8,128)S(1)}, f32[320,64,64]{0,1,2:T(8,128)}, u32[]{:S(2)}) copy-start(f32[320,64,64]{0,1,2:T(8,128)} %copy.191) | copy-start | bytes 15728644
  200.4 27.2 %copy-start.1 = (f32[320,64,64]{0,1,2:T(8,128)}, f32[320,64,64]{0,1,2:T(8,128)S(1)}, u32[]{:S(2)}) copy-start(f32[320,64,64]{0,1,2:T(8,128)S(1)} %get-tuple-element.17) | copy-start | bytes 15728644
  260.0 10.3 %copy-start = (f32[320,64,64]{0,2,1:T(8,128)S(1)}, f32[320,64,64]{0,2,1:T(8,128)}, u32[]{:S(2)}) copy-start(f32[320,64,64]{0,2,1:T(8,128)} %get-tuple-element.14) | copy-start | bytes 15728644
  301.2 12.4 %copy-start.3 = (f32[320,64,64]{0,2,1:T(8,128)S(1)}, f32[320,64,64]{0,2,1:T(8,128)}, u32[]{:S(2)}) copy-start(f32[320,64,64]{0,2,1:T(8,128)} %get-tuple-element.12) | copy-start | bytes 15728644
  422.0 5.2 copy-start.4
  422.0 120.6 %all-to-all-start.1 = ((f32[4,1,327680]{2,1,0:T(1,128)}), f32[4,1,327680]{2,1,0:T(1,128)}, u32[]{:S(2)}, u32[]{:S(2)}) async-start(f32[4,1,327680]{2,1,0:T(1,128)} %reshape.131), calls=%async_computation.1 | async-start | bytes 10485760 | tf_op jit(solution)/shard_map/all_to_all | solution.py:86
  427.7 10.4 %copy-start.6 = (s32[32,2]{0,1:T(2,128)S(1)}, s32[32,2]{0,1:T(2,128)}, u32[]{:S(2)}) copy-start(s32[32,2]{0,1:T(2,128)} %param.9) | copy-start | bytes 772
  428.6 232.4 %collective-permute-start.3 = (f32[5,32,1,1024]{3,1,0,2:T(8,128)}, f32[5,32,1,1024]{3,1,0,2:T(8,128)}, u32[]{:S(2)}, u32[]{:S(2)}) collective-permute-start(f32[5,32,1,1024]{3,1,0,2:T(8,128)} %get-tuple-element.30), channel_id=1, source_target_pairs={{0,1},{1,2},{2,3},{4,5},{5,6},{6,7},{8,9},{9,10},{10,11},{12,13},{... | collective-permute-start | bytes 1966088 | tf_op jit(solution)/shard_map/ppermute | solution.py:24
  430.8 231.4 %collective-permute-start.2 = (f32[5,32,1,1024]{3,1,0,2:T(8,128)S(1)}, f32[5,32,1,1024]{3,1,0,2:T(8,128)}, u32[]{:S(2)}, u32[]{:S(2)}) collective-permute-start(f32[5,32,1,1024]{3,1,0,2:T(8,128)S(1)} %get-tuple-element.31), channel_id=1, source_target_pairs={{1,0},{2,1},{3,2},{5,4},{6,5},{7,6},{9,8},{10,9},{11,10},{13,12},{... | collective-permute-start | bytes 1966088 | tf_op jit(solution)/shard_map/ppermute | solution.py:25
  432.2 230.0 %collective-permute-start = (f32[5,1,2,1024]{3,1,0,2:T(1,128)S(1)}, f32[5,1,2,1024]{3,1,0,2:T(1,128)S(1)}, u32[]{:S(2)}, u32[]{:S(2)}) collective-permute-start(f32[5,1,2,1024]{3,1,0,2:T(1,128)S(1)} %copy.181), channel_id=1, source_target_pairs={{4,0},{5,1},{6,2},{7,3},{12,8},{13,9},{14,10},{15,11},{20,16},{21,... | collective-permute-start | bytes 122888 | tf_op jit(solution)/shard_map/ppermute | solution.py:25
  433.5 228.7 %collective-permute-start.1 = (f32[5,1,2,1024]{3,1,0,2:T(1,128)S(1)}, f32[5,1,2,1024]{3,1,0,2:T(1,128)S(1)}, u32[]{:S(2)}, u32[]{:S(2)}) collective-permute-start(f32[5,1,2,1024]{3,1,0,2:T(1,128)S(1)} %copy.183), channel_id=1, source_target_pairs={{0,4},{1,5},{2,6},{3,7},{8,12},{9,13},{10,14},{11,15},{16,20},{17,... | collective-permute-start | bytes 122888 | tf_op jit(solution)/shard_map/ppermute | solution.py:24
  646.0 4.6 copy-start.7
  653.3 8.9 %copy-start.5 = (f32[5]{0:T(128)S(1)}, f32[5]{0:T(128)}, u32[]{:S(2)}) copy-start(f32[5]{0:T(128)} %constant.78) | copy-start | bytes 64
  664.3 9.5 %collective-permute-start.7 = (f32[5,32,1,1024]{3,1,0,2:T(8,128)S(1)}, f32[5,32,1,1024]{3,1,0,2:T(8,128)S(1)}, u32[]{:S(2)}, u32[]{:S(2)}) collective-permute-start(f32[5,32,1,1024]{3,1,0,2:T(8,128)S(1)} %get-tuple-element.28), channel_id=1, source_target_pairs={{0,1},{1,2},{2,3},{4,5},{5,6},{6,7},{8,9},{9,10},{10,11},{12,13},{... | collective-permute-start | bytes 1966088 | tf_op jit(solution)/shard_map/ppermute | solution.py:24
  666.6 9.0 %collective-permute-start.6 = (f32[5,32,1,1024]{3,1,0,2:T(8,128)S(1)}, f32[5,32,1,1024]{3,1,0,2:T(8,128)S(1)}, u32[]{:S(2)}, u32[]{:S(2)}) collective-permute-start(f32[5,32,1,1024]{3,1,0,2:T(8,128)S(1)} %get-tuple-element.29), channel_id=1, source_target_pairs={{1,0},{2,1},{3,2},{5,4},{6,5},{7,6},{9,8},{10,9},{11,10},{13,12},{... | collective-permute-start | bytes 1966088 | tf_op jit(solution)/shard_map/ppermute | solution.py:25
  668.0 6.2 collective-permute-start.4
  669.3 6.4 collective-permute-start.5
  676.9 12.8 %collective-permute-start.11 = (f32[5,32,1,1024]{3,1,0,2:T(8,128)S(1)}, f32[5,32,1,1024]{3,1,0,2:T(8,128)S(1)}, u32[]{:S(2)}, u32[]{:S(2)}) collective-permute-start(f32[5,32,1,1024]{3,1,0,2:T(8,128)S(1)} %get-tuple-element.24), channel_id=1, source_target_pairs={{0,1},{1,2},{2,3},{4,5},{5,6},{6,7},{8,9},{9,10},{10,11},{12,13},{... | collective-permute-start | bytes 1966088 | tf_op jit(solution)/shard_map/ppermute | solution.py:24
  682.2 9.0 %collective-permute-start.10 = (f32[5,32,1,1024]{3,1,0,2:T(8,128)S(1)}, f32[5,32,1,1024]{3,1,0,2:T(8,128)S(1)}, u32[]{:S(2)}, u32[]{:S(2)}) collective-permute-start(f32[5,32,1,1024]{3,1,0,2:T(8,128)S(1)} %get-tuple-element.25), channel_id=1, source_target_pairs={{1,0},{2,1},{3,2},{5,4},{6,5},{7,6},{9,8},{10,9},{11,10},{13,12},{... | collective-permute-start | bytes 1966088 | tf_op jit(solution)/shard_map/ppermute | solution.py:25
  683.6 6.2 collective-permute-start.8
  684.9 6.4 collective-permute-start.9
  692.4 12.0 %collective-permute-start.15 = (f32[5,32,1,1024]{3,1,0,2:T(8,128)S(1)}, f32[5,32,1,1024]{3,1,0,2:T(8,128)S(1)}, u32[]{:S(2)}, u32[]{:S(2)}) collective-permute-start(f32[5,32,1,1024]{3,1,0,2:T(8,128)S(1)} %get-tuple-element.20), channel_id=1, source_target_pairs={{0,1},{1,2},{2,3},{4,5},{5,6},{6,7},{8,9},{9,10},{10,11},{12,13},{... | collective-permute-start | bytes 1966088 | tf_op jit(solution)/shard_map/ppermute | solution.py:24
  697.2 9.0 %collective-permute-start.14 = (f32[5,32,1,1024]{3,1,0,2:T(8,128)S(1)}, f32[5,32,1,1024]{3,1,0,2:T(8,128)S(1)}, u32[]{:S(2)}, u32[]{:S(2)}) collective-permute-start(f32[5,32,1,1024]{3,1,0,2:T(8,128)S(1)} %get-tuple-element.21), channel_id=1, source_target_pairs={{1,0},{2,1},{3,2},{5,4},{6,5},{7,6},{9,8},{10,9},{11,10},{13,12},{... | collective-permute-start | bytes 1966088 | tf_op jit(solution)/shard_map/ppermute | solution.py:25
  698.6 6.2 collective-permute-start.12
  699.9 6.4 collective-permute-start.13
where the time goes:
time: 722 us; the launch traced here: 714 us
  waiting for transfers between devices  247 us (34%)
  local copies, waits for them, and re-layouts  225 us (31%)
  matrix products  143 us (20%)
  starting transfers between devices  55 us (8%)
  other arithmetic  34.3 us (5%)
  blocking collectives  7.69 us (1%)
    all_to_all x1, waiting for transfers between devices, on_device(): lax.all_to_all(stacked, 'az', split_axis=1, concat_axis=2, tiled=True)  138 us
    unnamed x20, local copies, waits for them, and re-layouts  112 us
    all_to_all x1, waiting for transfers between devices, on_device(): lax.all_to_all(moved, 'az', split_axis=2, concat_axis=1, tiled=True)  105 us
    ppermute x8, starting transfers between devices, padded(): before = lax.ppermute(last, axis, up)  33 us
    all_to_all x3, local copies, waits for them, and re-layouts, on_device(): lax.all_to_all(moved, 'az', split_axis=2, concat_axis=1, tiled=True)  32.1 us
    another operation x2, local copies, waits for them, and re-layouts, on_device(): spectral_shift(piece.reshape(-1, piece.shape[2]), shift_value)  28.5 us
    another operation x2, local copies, waits for them, and re-layouts, spectral_shift(): grid = rows.reshape(count, outer, inner)  21.5 us
    dot_general x1, matrix products, spectral_shift(): jnp.einsum('bkq,qm->bkm', twist_im, cos_inner, precision=hp)  19.1 us
  transfers between devices with their start and end apart: 18, of which 7 were waited for; matrix products, arithmetic and copies ran while one was open for 16% of the time, Pallas kernels for 0%

commit v1 on v0

v1 whole, which is shorter than its diff:
```python
import math

import jax
import jax.numpy as jnp
import numpy as np
from jax import lax
from jax.experimental import pallas as pl
from jax.experimental.pallas import tpu as pltpu
from jax.sharding import PartitionSpec as P

KR = 8


LAYER_WEIGHTS = (0.4, 0.3, 0.2, 0.1)
AXIAL_SPEEDS = (0.35, 0.2, 0.3, 0.25, 0.4)
DIFFUSION = 0.15
SWIRL_SPEED = 0.1
MIB = 1024 * 1024


def class_counts(length):
    top = (length - 1) // 3
    kept = np.arange(-top, top + 1)
    first = kept[kept % 4 == 1]
    assert length % 4 == 0 and (first - 1).sum() == 0
    even, odd, half = [int((kept % 4 == r).sum()) for r in (0, 1, 2)]
    assert even == odd
    return even, half


def shift_tables(shift_value, length):
    quarter = length // 4
    even, half = class_counts(length)
    target = jnp.arange(quarter, dtype=jnp.int32) - shift_value
    rows = []
    for count in (even, half):
        angle = jnp.remainder(count * target, 2 * quarter).astype(jnp.float32) * (math.pi / quarter)
        rows += [jnp.sin(angle), jnp.cos(angle)]
    angle = jnp.remainder(target, length).astype(jnp.float32) * (2.0 * math.pi / length)
    rows += [jnp.cos(angle), jnp.sin(angle)]
    source = np.arange(quarter) * (2.0 * np.pi / length)
    rows += [jnp.asarray(np.cos(source), jnp.float32), jnp.asarray(np.sin(source), jnp.float32)]
    return jnp.stack(rows)


def source_tables(length):
    quarter = length // 4
    source = np.arange(quarter)
    cols = []
    for count in class_counts(length):
        angle = (count * source % (2 * quarter)) * (np.pi / quarter)
        cols += [np.sin(angle), np.cos(angle)]
    return jnp.asarray(np.stack(cols, axis=1), jnp.float32)


def kernel_matrix_body(length, block, shift_ref, rows_ref, cols_ref, eh_ref, el_ref, hh_ref, hl_ref):
    quarter = length // 4
    even, half = class_counts(length)
    shape = (block, quarter)
    source = lax.broadcasted_iota(jnp.int32, shape, 0) + pl.program_id(0) * block
    target = lax.broadcasted_iota(jnp.int32, shape, 1)
    apart = (target - source - shift_ref[0]) & (2 * quarter - 1)
    apart = jnp.where(apart >= quarter, apart - 2 * quarter, apart)
    near = jnp.where(apart > quarter // 2, quarter - apart, apart)
    near = jnp.where(apart < -(quarter // 2), -quarter - apart, near)
    u = near.astype(jnp.float32) * (math.pi / quarter)
    w = u * u
    poly = jnp.full(shape, 1.0 / 6227020800.0, jnp.float32)
    for c in (-1.0 / 39916800.0, 1.0 / 362880.0, -1.0 / 5040.0, 1.0 / 120.0, -1.0 / 6.0):
        poly = poly * w + c
    sine = u + u * (w * poly)
    zero = near == 0
    inverse = 0.25 / (quarter * jnp.where(zero, 1.0, sine))
    top_even = rows_ref[0:1, :] * cols_ref[:, 1:2] - rows_ref[1:2, :] * cols_ref[:, 0:1]
    top_half = rows_ref[2:3, :] * cols_ref[:, 3:4] - rows_ref[3:4, :] * cols_ref[:, 2:3]
    sign = jnp.where(apart == 0, 1.0, -1.0)
    m_even = jnp.where(zero, 0.25 * even / quarter, top_even * inverse)
    m_half = jnp.where(zero, sign * (0.25 * half / quarter), top_half * inverse)
    for value, high_ref, low_ref in ((m_even, eh_ref, el_ref), (m_half, hh_ref, hl_ref)):
        high = value.astype(jnp.bfloat16)
        high_ref[...] = high
        low_ref[...] = (value - high.astype(jnp.float32)).astype(jnp.bfloat16)


def filter_matrices(shift, tables, length):
    quarter = length // 4
    block = 128
    out = jax.ShapeDtypeStruct((quarter, quarter), jnp.bfloat16)
    return pl.pallas_call(
        lambda *refs: kernel_matrix_body(length, block, *refs),
        grid=(quarter // block,),
        out_shape=[out] * 4,
        in_specs=[
            pl.BlockSpec(memory_space=pltpu.SMEM),
            pl.BlockSpec((8, quarter), lambda i: (0, 0)),
            pl.BlockSpec((block, 4), lambda i: (i, 0)),
        ],
        out_specs=[pl.BlockSpec((block, quarter), lambda i: (i, 0))] * 4,
        compiler_params=pltpu.CompilerParams(vmem_limit_bytes=32 * MIB),
        cost_estimate=pl.CostEstimate(flops=60 * quarter * quarter, bytes_accessed=8 * quarter * quarter, transcendentals=0),
        name="filter_matrices",
    )(shift, tables, source_tables(length))


def split(value):
    high = value.astype(jnp.bfloat16)
    return high, (value - high.astype(jnp.float32)).astype(jnp.bfloat16)


def product(value, high_ref, low_ref):
    high, low = split(value)
    f32 = jnp.float32
    return (
        jnp.dot(high, low_ref[...], preferred_element_type=f32)
        + jnp.dot(low, high_ref[...], preferred_element_type=f32)
        + jnp.dot(high, high_ref[...], preferred_element_type=f32)
    )


def filter_body(x_ref, tab_ref, eh_ref, el_ref, hh_ref, hl_ref, out_ref):
    count = x_ref.shape[1]
    x0, x1, x2, x3 = [x_ref[i] for i in range(4)]
    cos_t, sin_t = 2.0 * tab_ref[4:5, :], 2.0 * tab_ref[5:6, :]
    cos_s, sin_s = tab_ref[6:7, :], tab_ref[7:8, :]
    even, odd = x0 + x2, x1 + x3
    re, im = x0 - x2, x3 - x1
    stacked = jnp.concatenate([even + odd, re * cos_s + im * sin_s, im * cos_s - re * sin_s], axis=0)
    turned = product(stacked, eh_ref, el_ref)
    z2 = product(even - odd, hh_ref, hl_ref)
    z0, ure, uim = turned[:count], turned[count : 2 * count], turned[2 * count :]
    zre = cos_t * ure - sin_t * uim
    zim = cos_t * uim + sin_t * ure
    plus, minus = z0 + z2, z0 - z2
    out_ref[0] = plus + zre
    out_ref[1] = minus - zim
    out_ref[2] = plus - zre
    out_ref[3] = minus + zim


def filtered(quarters, tables, matrices):
    _, count, quarter = quarters.shape
    block = next((b for b in (80, 64, 40, 32, 16, 8) if count % b == 0), count)
    whole = pl.BlockSpec((quarter, quarter), lambda i: (0, 0))
    part = pl.BlockSpec((4, block, quarter), lambda i: (0, i, 0))
    return pl.pallas_call(
        filter_body,
        grid=(count // block,),
        out_shape=jax.ShapeDtypeStruct(quarters.shape, jnp.float32),
        in_specs=[part, pl.BlockSpec((8, quarter), lambda i: (0, 0))] + [whole] * 4,
        out_specs=part,
        compiler_params=pltpu.CompilerParams(vmem_limit_bytes=48 * MIB),
        cost_estimate=pl.CostEstimate(
            flops=24 * count * quarter * quarter,
            bytes_accessed=32 * count * quarter + 8 * quarter * quarter,
            transcendentals=0,
        ),
        name="spectral_filter",
    )(quarters, tables, *matrices)


def to_quarters(pieces):
    sectors, count, sector = pieces.shape
    per = sectors // 4
    if per == 1:
        return pieces
    return pieces.reshape(4, per, count, sector).transpose(0, 2, 1, 3).reshape(4, count, per * sector)


def to_sectors(quarters, sectors):
    _, count, quarter = quarters.shape
    per = sectors // 4
    if per == 1:
        return quarters
    sector = quarter // per
    return quarters.reshape(4, count, per, sector).transpose(0, 2, 1, 3).reshape(sectors, count, sector)


def shifted(array, axis, dim, width):
    devices, length = (lax.axis_size(axis), array.shape[dim])
    up = [(i, (i + 1) % devices) for i in range(devices - 1)]
    down = [(j, i) for i, j in up]
    last = lax.slice_in_dim(array, length - width, length, axis=dim)
    leading = lax.slice_in_dim(array, 0, width, axis=dim)
    return lax.ppermute(last, axis, up), lax.ppermute(leading, axis, down)


def on_device(cycle, field, shift, owner):
    layers, variables, radial, sector = cycle.shape
    sectors = lax.axis_size("az")
    length = sectors * sector
    shift_value = shift[0]
    rows = layers * variables * radial
    piece = lax.all_to_all(cycle.reshape(sectors, rows // sectors, sector), "az", split_axis=0, concat_axis=0, tiled=True)
    tables = shift_tables(shift_value, length)
    matrices = filter_matrices(shift, tables, length)

    weights = jnp.array(LAYER_WEIGHTS, jnp.float32)
    cells = radial // KR
    grouped = cycle.reshape(layers, variables, cells, KR, sector)
    mean = jnp.sum(jnp.sum(grouped * weights[:, None, None, None, None], axis=0), axis=2) / KR
    around = lax.all_gather(mean.reshape(variables * cells, sector), "az", axis=0, tiled=False)
    ghost_all = to_sectors(filtered(to_quarters(around), tables, matrices), sectors)
    ghost = lax.dynamic_index_in_dim(ghost_all, lax.axis_index("az"), 0, keepdims=False)
    ghost = lax.all_gather(ghost.reshape(variables, cells, sector), "ax", axis=1, tiled=True)

    moved = to_sectors(filtered(to_quarters(piece), tables, matrices), sectors)
    shifted_cycle = lax.all_to_all(moved, "az", split_axis=0, concat_axis=0, tiled=True)
    shifted_cycle = shifted_cycle.reshape(layers, variables, radial, sector)

    mask = owner.astype(jnp.float32)[None, :, :, None]
    speeds = jnp.array(AXIAL_SPEEDS, jnp.float32)[:, None, None, None]
    at_inlet = lax.axis_index("ax") == 0

    def rates(state):
        inner, outer = shifted(state, "rad", 1, 1)
        under, over = shifted(state, "ax", 2, 1)
        lower = jnp.where(at_inlet, ghost[:, :, None], under)
        outward = jnp.concatenate([state[:, 1:], outer], axis=1)
        inward = jnp.concatenate([inner, state[:, :-1]], axis=1)
        above = jnp.concatenate([state[:, :, 1:], over], axis=2)
        below = jnp.concatenate([lower, state[:, :, :-1]], axis=2)
        return mask * (
            DIFFUSION * (outward + inward + above + below - 4.0 * state)
            - 0.5 * speeds * (above - below)
            - 0.5 * SWIRL_SPEED * (outward - inward)
        )

    first = rates(field)
    second = rates(field + 0.5 * first)
    third = rates(field + 0.5 * second)
    fourth = rates(field + third)
    field_next = field + (first + 2.0 * second + 2.0 * third + fourth) / 6.0
    return (field_next, shifted_cycle)


def solution(mesh):
    in_specs = (P(None, None, ("rad", "ax"), "az"), P(None, "rad", "ax", "az"), P(), P("rad", "ax"))
    out_specs = (P(None, "rad", "ax", "az"), P(None, None, ("rad", "ax"), "az"))
    return jax.shard_map(
        on_device, mesh=mesh, in_specs=in_specs, out_specs=out_specs, check_vma=False
    )
```

time: 722 us -> 348 us (0.48)
  local copies, waits for them, and re-layouts: 225 us -> 25.9 us
  matrix products: 143 us -> 0 us
  waiting for transfers between devices: 247 us -> 107 us
  blocking collectives: 7.69 us -> 118 us
  Pallas kernels: 0 us -> 27.7 us
  other arithmetic: 34.3 us -> 8.47 us
    dot_general x13 -> x0, matrix products: 143 us -> none  [the longest x1 19.1 us: spectral_shift(): jnp.einsum('bkq,qm->bkm', twist_im, cos_inner, precision=hp)]
    all_to_all x2, waiting for transfers between devices: 242 us -> 103 us  [the longest x1 103 us: on_device(): lax.all_to_all(cycle.reshape(sectors, rows // sectors, sector), 'az', spl...]
    all_gather x1 -> x2, blocking collectives: 7.69 us -> 118 us  [the longest x1 110 us: on_device(): lax.all_gather(mean.reshape(variables * cells, sector), 'az', axis=0, til...]
    unnamed x20 -> x36, local copies, waits for them, and re-layouts: 112 us -> 19.8 us
    another operation x4 -> x1, local copies, waits for them, and re-layouts: 49.9 us -> 0.06 us  [shift_tables(): return jnp.stack(rows)]
    all_to_all x4 -> x0, local copies, waits for them, and re-layouts: 40.7 us -> none  [the longest x3 32.1 us: on_device(): lax.all_to_all(moved, 'az', split_axis=2, concat_axis=1, tiled=True)]
    pallas_call x0 -> x3, Pallas kernels: none -> 27.7 us  [the longest x2 19.7 us: filtered(): pl.pallas_call(filter_body, grid=(count // block,), out_shape=jax.ShapeDt...]
    all_to_all x1 -> x0, other arithmetic: 18.3 us -> none  [on_device(): lax.all_to_all(moved, 'az', split_axis=2, concat_axis=1, tiled=True)]
  transfers between devices with their start and end apart: 18 -> 18, of which waited for: 7 -> 4; matrix products, arithmetic and copies ran while one was open for 16% -> 7% of each run, Pallas kernels for 0% -> 4%
where the time goes in v1:
time: 348 us; the launch traced here: 345 us
  blocking collectives  118 us (34%)
  waiting for transfers between devices  107 us (31%)
  starting transfers between devices  55.5 us (16%)
  Pallas kernels  27.7 us (8%)
  local copies, waits for them, and re-layouts  25.9 us (7%)
  other arithmetic  8.47 us (2%)
    all_gather x1, blocking collectives, on_device(): lax.all_gather(mean.reshape(variables * cells, sector), 'az', axis=0, til...  110 us
    all_to_all x1, waiting for transfers between devices, on_device(): lax.all_to_all(cycle.reshape(sectors, rows // sectors, sector), 'az', spl...  103 us
    ppermute x16, starting transfers between devices, shifted(): return (lax.ppermute(last, axis, up), lax.ppermute(leading, axis, down))  43.8 us
    unnamed x36, local copies, waits for them, and re-layouts  19.8 us
    pallas_call x2, Pallas kernels, filtered(): pl.pallas_call(filter_body, grid=(count // block,), out_shape=jax.ShapeDt...  19.7 us
    all_gather x1, blocking collectives, on_device(): lax.all_gather(ghost.reshape(variables, cells, sector), 'ax', axis=1, til...  8.27 us
    pallas_call x1, Pallas kernels, filter_matrices(): pl.pallas_call(lambda *refs: kernel_matrix_body(length, block, *refs), gr...  7.98 us
  transfers between devices with their start and end apart: 18, of which 4 were waited for; matrix products, arithmetic and copies ran while one was open for 7% of the time, Pallas kernels for 4%

profile of v1, /device:TPU:0, one launch (start us, length us, event | category | flops | bytes accessed | tf_op | source)
XLA Modules:
  0.0 344.6 jit_solution(4664975475983025744)
XLA Ops:
  0.7 6.5 %all-to-all-start = ((f32[4,320,1024]{2,1,0:T(8,128)}), f32[4,320,1024]{2,1,0:T(8,128)}, u32[]{:S(2)}, u32[]{:S(2)}) async-start(f32[4,320,1024]{2,1,0:T(8,128)} %bitcast.17), calls=%async_computation | async-start | bytes 10485760 | tf_op jit(solution)/shard_map/all_to_all | solution.py:193
  7.8 0.1 fusion.9
  7.9 0.1 fusion.11
  8.1 0.1 fusion.13
  8.3 0.1 stack.8.refs_1_.tab_ref
  8.3 8.0 %filter_matrices.1 = (bf16[1024,1024]{1,0:T(8,128)(2,1)S(1)}, bf16[1024,1024]{1,0:T(8,128)(2,1)S(1)}, bf16[1024,1024]{1,0:T(8,128)(2,1)S(1)}, bf16[1024,1024]{1,0:T(8,128)(2,1)S(1)}) custom-call(s32[1]{0:T(128)} %copy.61.refs_0_, f32[8,1024]{1,0:T(8,128)S(1)} %stack.8.refs_1_.tab_ref, f32[1024,4]{1,0:T(8,128)S(1)} %copy-done.5), custom_call_target="tpu_custom_call" | custom-call | flops 62914560 | bytes 8388608 | tf_op jit(solution)/shard_map/filter_matrices/pallas_call | solution.py:89
  16.3 1.3 copy-done
  17.6 1.4 copy-done.3
  19.0 1.3 copy-done.4
  20.3 102.9 %all-to-all-done.x_ref = f32[4,320,1024]{2,1,0:T(8,128)} async-done(((f32[4,320,1024]{2,1,0:T(8,128)}), f32[4,320,1024]{2,1,0:T(8,128)}, u32[]{:S(2)}, u32[]{:S(2)}) %all-to-all-start) | async-done | bytes 5242912 | tf_op jit(solution)/shard_map/all_to_all | solution.py:193
  123.2 1.6 copy-done.1
  124.8 15.4 %spectral_filter.3 = f32[4,320,1024]{2,1,0:T(8,128)} custom-call(f32[4,320,1024]{2,1,0:T(8,128)} %all-to-all-done.x_ref, f32[8,1024]{1,0:T(8,128)S(1)} %stack.8.refs_1_.tab_ref, bf16[1024,1024]{1,0:T(8,128)(2,1)S(1)} %get-tuple-element.6.eh_ref, bf16[1024,1024]{1,0:T(8,128)(2,1)S(1)} %copy-done.1, bf16[1024,1024]{1,0:T(8,128)(2,1)} %copy-done.3, ...), custom_call_target="tpu_custom_call" | custom-call | flops 8053063680 | bytes 18874368 | tf_op jit(solution)/shard_map/spectral_filter/pallas_call | solution.py:145
  140.2 5.2 %all-to-all-start.1 = ((f32[4,320,1024]{2,1,0:T(8,128)}), f32[4,320,1024]{2,1,0:T(8,128)}, u32[]{:S(2)}, u32[]{:S(2)}) async-start(f32[4,320,1024]{2,1,0:T(8,128)} %spectral_filter.3), calls=%async_computation.1 | async-start | bytes 10485760 | tf_op jit(solution)/shard_map/all_to_all | solution.py:207
  145.4 1.0 fusion.26
  146.5 1.0 copy.56
  147.4 2.1 collective-permute-start.3
  149.6 1.0 copy.55
  150.5 1.3 collective-permute-start.2
  151.8 0.6 copy.37
  152.5 1.3 collective-permute-start
  153.8 0.6 copy.38
  154.4 4.5 %collective-permute-start.1 = (f32[5,1,2,1024]{3,1,0,2:T(1,128)}, f32[5,1,2,1024]{3,1,0,2:T(1,128)S(1)}, u32[]{:S(2)}, u32[]{:S(2)}) collective-permute-start(f32[5,1,2,1024]{3,1,0,2:T(1,128)} %copy.38), channel_id=1, source_target_pairs={{0,4},{1,5},{2,6},{3,7},{8,12},{9,13},{10,14},{11,15},{16,20},{17,... | collective-permute-start | bytes 122888 | tf_op jit(solution)/shard_map/ppermute | solution.py:184
  159.0 0.8 multiply_reduce_fusion
  159.7 0.3 bitcast_reduce_fusion
  160.1 2.3 fusion.24
  162.4 109.7 %all_gather.6.x_ref = f32[4,40,1024]{2,1,0:T(8,128)S(1)} all-gather(f32[1,40,1024]{2,1,0:T(8,128)S(1)} %multiply_bitcast_fusion), channel_id=1, replica_groups=mesh['az'=4,'rad'=2,'ax'=4] {'az'}, dimensions={0}, use_global_device_ids=true | all-gather | bytes 819200 | tf_op jit(solution)/shard_map/all_gather | solution.py:201
  272.1 4.3 %spectral_filter.2 = f32[4,40,1024]{2,1,0:T(8,128)S(1)} custom-call(f32[4,40,1024]{2,1,0:T(8,128)S(1)} %all_gather.6.x_ref, f32[8,1024]{1,0:T(8,128)S(1)} %stack.8.refs_1_.tab_ref, bf16[1024,1024]{1,0:T(8,128)(2,1)S(1)} %get-tuple-element.6.eh_ref, bf16[1024,1024]{1,0:T(8,128)(2,1)S(1)} %copy-done.2, bf16[1024,1024]{1,0:T(8,128)(2,1)} %copy-done.3, ...), custom_call_target="tpu_custom_call" | custom-call | flops 1006632960 | bytes 9699328 | tf_op jit(solution)/shard_map/spectral_filter/pallas_call | solution.py:145
  276.5 1.7 copy.57
  278.2 2.8 copy.58
  281.1 8.3 %all_gather.7 = f32[5,32,1024]{2,1,0:T(8,128)S(1)} all-gather(f32[5,8,1024]{2,1,0:T(8,128)S(1)} %dynamic-slice_bitcast_fusion), channel_id=1, replica_groups=mesh['az'=4,'rad'=2,'ax'=4] {'ax'}, dimensions={1}, use_global_device_ids=true | all-gather | bytes 819200 | tf_op jit(solution)/shard_map/all_gather | solution.py:204
  289.3 0.1 bitcast_select_fusion.3
  289.5 2.6 multiply_add_fusion.2
  292.1 0.1 fusion.23
  292.3 3.4 collective-permute-start.7
  295.7 1.3 collective-permute-start.6
  297.0 0.1 fusion.22
  297.0 1.3 collective-permute-start.4
  298.3 4.5 %collective-permute-start.5 = (f32[5,1,2,1024]{3,1,0,2:T(1,128)S(1)}, f32[5,1,2,1024]{3,1,0,2:T(1,128)S(1)}, u32[]{:S(2)}, u32[]{:S(2)}) collective-permute-start(f32[5,1,2,1024]{3,1,0,2:T(1,128)S(1)} %get-tuple-element.37), channel_id=1, source_target_pairs={{0,4},{1,5},{2,6},{3,7},{8,12},{9,13},{10,14},{11,15},{16,20},{17,... | collective-permute-start | bytes 122888 | tf_op jit(solution)/shard_map/ppermute | solution.py:184
  302.9 0.2 fusion.21
  303.2 0.1 bitcast_select_fusion.2
  303.3 1.4 collective-permute-done.5
  304.7 1.3 multiply_add_fusion.1
  306.0 0.1 fusion.20
  306.1 5.0 %collective-permute-start.11 = (f32[5,32,1,1024]{3,1,0,2:T(8,128)S(1)}, f32[5,32,1,1024]{3,1,0,2:T(8,128)S(1)}, u32[]{:S(2)}, u32[]{:S(2)}) collective-permute-start(f32[5,32,1,1024]{3,1,0,2:T(8,128)S(1)} %get-tuple-element.32), channel_id=1, source_target_pairs={{0,1},{1,2},{2,3},{4,5},{5,6},{6,7},{8,9},{9,10},{10,11},{12,13},{... | collective-permute-start | bytes 1966088 | tf_op jit(solution)/shard_map/ppermute | solution.py:184
  311.2 1.3 collective-permute-start.10
  312.5 0.1 fusion.19
  312.5 1.3 collective-permute-start.8
  313.8 4.5 %collective-permute-start.9 = (f32[5,1,2,1024]{3,1,0,2:T(1,128)S(1)}, f32[5,1,2,1024]{3,1,0,2:T(1,128)S(1)}, u32[]{:S(2)}, u32[]{:S(2)}) collective-permute-start(f32[5,1,2,1024]{3,1,0,2:T(1,128)S(1)} %get-tuple-element.31), channel_id=1, source_target_pairs={{0,4},{1,5},{2,6},{3,7},{8,12},{9,13},{10,14},{11,15},{16,20},{17,... | collective-permute-start | bytes 122888 | tf_op jit(solution)/shard_map/ppermute | solution.py:184
  318.4 0.3 fusion.18
  318.7 0.1 bitcast_select_fusion.1
  318.8 1.4 collective-permute-done.9
  320.2 1.2 copy_add_fusion
  321.4 0.1 fusion.17
  321.5 4.8 %collective-permute-start.15 = (f32[5,32,1,1024]{3,1,0,2:T(8,128)S(1)}, f32[5,32,1,1024]{3,1,0,2:T(8,128)S(1)}, u32[]{:S(2)}, u32[]{:S(2)}) collective-permute-start(f32[5,32,1,1024]{3,1,0,2:T(8,128)S(1)} %get-tuple-element.26), channel_id=1, source_target_pairs={{0,1},{1,2},{2,3},{4,5},{5,6},{6,7},{8,9},{9,10},{10,11},{12,13},{... | collective-permute-start | bytes 1966088 | tf_op jit(solution)/shard_map/ppermute | solution.py:184
  326.3 1.3 collective-permute-start.14
  327.6 0.1 fusion.16
  327.7 1.3 collective-permute-start.12
  329.0 4.5 %collective-permute-start.13 = (f32[5,1,2,1024]{3,1,0,2:T(1,128)S(1)}, f32[5,1,2,1024]{3,1,0,2:T(1,128)S(1)}, u32[]{:S(2)}, u32[]{:S(2)}) collective-permute-start(f32[5,1,2,1024]{3,1,0,2:T(1,128)S(1)} %get-tuple-element.25), channel_id=1, source_target_pairs={{0,4},{1,5},{2,6},{3,7},{8,12},{9,13},{10,14},{11,15},{16,20},{17,... | collective-permute-start | bytes 122888 | tf_op jit(solution)/shard_map/ppermute | solution.py:184
  333.5 0.2 fusion.15
  333.8 0.1 bitcast_select_fusion
  333.9 1.5 collective-permute-done.13
  335.3 1.5 multiply_add_fusion
  336.9 2.1 copy.47
  338.9 5.7 %copy.62 = f32[4,5,64,1024]{3,2,1,0:T(8,128)} copy(f32[4,5,64,1024]{3,2,1,0:T(8,128)} %bitcast.6) | data formatting | bytes 10485760
  (44 shorter events, 0.1 us)
Async XLA Ops:
  0.6 7.6 %copy-start.11 = (f32[1,1024]{1,0:T(1,128)S(1)}, f32[1,1024]{1,0:T(1,128)}, u32[]{:S(2)}) copy-start(f32[1,1024]{1,0:T(1,128)} %constant.88) | copy-start | bytes 12292
  0.6 7.6 %copy-start.12 = (f32[1,1024]{1,0:T(1,128)S(1)}, f32[1,1024]{1,0:T(1,128)}, u32[]{:S(2)}) copy-start(f32[1,1024]{1,0:T(1,128)} %constant.89) | copy-start | bytes 12292
  0.7 7.7 %copy-start.5 = (f32[1024,4]{1,0:T(8,128)S(1)}, f32[1024,4]{1,0:T(8,128)}, u32[]{:S(2)}) copy-start(f32[1024,4]{1,0:T(8,128)} %constant.83.clone.refs_2_) | copy-start | bytes 49156
  0.7 122.6 %all-to-all-start = ((f32[4,320,1024]{2,1,0:T(8,128)}), f32[4,320,1024]{2,1,0:T(8,128)}, u32[]{:S(2)}, u32[]{:S(2)}) async-start(f32[4,320,1024]{2,1,0:T(8,128)} %bitcast.17), calls=%async_computation | async-start | bytes 10485760 | tf_op jit(solution)/shard_map/all_to_all | solution.py:193
  16.3 1.3 copy-start
  17.6 1.4 copy-start.3
  19.0 1.3 copy-start.4
  123.2 1.6 copy-start.1
  140.2 5.2 %copy-start.6 = (f32[5,32,2,1024]{3,2,1,0:T(2,128)S(1)}, f32[5,32,2,1024]{3,2,1,0:T(2,128)}, u32[]{:S(2)}) copy-start(f32[5,32,2,1024]{3,2,1,0:T(2,128)} %param.10) | copy-start | bytes 3932164
  140.2 198.8 %all-to-all-start.1 = ((f32[4,320,1024]{2,1,0:T(8,128)}), f32[4,320,1024]{2,1,0:T(8,128)}, u32[]{:S(2)}, u32[]{:S(2)}) async-start(f32[4,320,1024]{2,1,0:T(8,128)} %spectral_filter.3), calls=%async_computation.1 | async-start | bytes 10485760 | tf_op jit(solution)/shard_map/all_to_all | solution.py:207
  145.4 13.5 %copy-start.8 = (f32[4,5,64,1024]{3,2,1,0:T(8,128)S(1)}, f32[4,5,64,1024]{3,2,1,0:T(8,128)}, u32[]{:S(2)}) copy-start(f32[4,5,64,1024]{3,2,1,0:T(8,128)} %param.9) | copy-start | bytes 15728644
  146.5 12.5 %copy-start.14 = (f32[4]{0:T(128)S(1)}, f32[4]{0:T(128)}, u32[]{:S(2)}) copy-start(f32[4]{0:T(128)} %constant.84.clone) | copy-start | bytes 52
  147.4 141.9 %collective-permute-start.3 = (f32[5,32,1,1024]{3,1,0,2:T(8,128)}, f32[5,32,1,1024]{3,1,0,2:T(8,128)}, u32[]{:S(2)}, u32[]{:S(2)}) collective-permute-start(f32[5,32,1,1024]{3,1,0,2:T(8,128)} %copy.56), channel_id=1, source_target_pairs={{0,1},{1,2},{2,3},{4,5},{5,6},{6,7},{8,9},{9,10},{10,11},{12,13},{... | collective-permute-start | bytes 1966088 | tf_op jit(solution)/shard_map/ppermute | solution.py:184
  150.5 138.9 %collective-permute-start.2 = (f32[5,32,1,1024]{3,1,0,2:T(8,128)}, f32[5,32,1,1024]{3,1,0,2:T(8,128)}, u32[]{:S(2)}, u32[]{:S(2)}) collective-permute-start(f32[5,32,1,1024]{3,1,0,2:T(8,128)} %copy.55), channel_id=1, source_target_pairs={{1,0},{2,1},{3,2},{5,4},{6,5},{7,6},{9,8},{10,9},{11,10},{13,12},{... | collective-permute-start | bytes 1966088 | tf_op jit(solution)/shard_map/ppermute | solution.py:184
  152.5 137.0 %collective-permute-start = (f32[5,1,2,1024]{3,1,0,2:T(1,128)}, f32[5,1,2,1024]{3,1,0,2:T(1,128)S(1)}, u32[]{:S(2)}, u32[]{:S(2)}) collective-permute-start(f32[5,1,2,1024]{3,1,0,2:T(1,128)} %copy.37), channel_id=1, source_target_pairs={{4,0},{5,1},{6,2},{7,3},{12,8},{13,9},{14,10},{15,11},{20,16},{21,... | collective-permute-start | bytes 122888 | tf_op jit(solution)/shard_map/ppermute | solution.py:184
  154.4 135.0 %collective-permute-start.1 = (f32[5,1,2,1024]{3,1,0,2:T(1,128)}, f32[5,1,2,1024]{3,1,0,2:T(1,128)S(1)}, u32[]{:S(2)}, u32[]{:S(2)}) collective-permute-start(f32[5,1,2,1024]{3,1,0,2:T(1,128)} %copy.38), channel_id=1, source_target_pairs={{0,4},{1,5},{2,6},{3,7},{8,12},{9,13},{10,14},{11,15},{16,20},{17,... | collective-permute-start | bytes 122888 | tf_op jit(solution)/shard_map/ppermute | solution.py:184
  160.1 112.1 %copy-start.2 = (bf16[1024,1024]{1,0:T(8,128)(2,1)S(1)}, bf16[1024,1024]{1,0:T(8,128)(2,1)}, u32[]{:S(2)}) copy-start(bf16[1024,1024]{1,0:T(8,128)(2,1)} %copy-done) | copy-start | bytes 6291460
  272.1 4.3 %copy-start.13 = (s32[32,2]{0,1:T(2,128)S(1)}, s32[32,2]{0,1:T(2,128)}, u32[]{:S(2)}) copy-start(s32[32,2]{0,1:T(2,128)} %param.12) | copy-start | bytes 772
  281.0 8.4 %copy-start.7 = (f32[5,32,2,1024]{3,2,1,0:T(2,128)S(1)}, f32[5,32,2,1024]{3,2,1,0:T(2,128)}, u32[]{:S(2)}) copy-start(f32[5,32,2,1024]{3,2,1,0:T(2,128)} %param.10) | copy-start | bytes 3932164
  281.0 8.4 %copy-start.9 = (f32[5,31,2,1024]{3,1,0,2:T(8,128)S(1)}, f32[5,31,2,1024]{3,1,0,2:T(8,128)}, u32[]{:S(2)}) copy-start(f32[5,31,2,1024]{3,1,0,2:T(8,128)} %copy.58) | copy-start | bytes 3809284
  281.1 8.4 %copy-start.10 = (f32[5]{0:T(128)S(1)}, f32[5]{0:T(128)}, u32[]{:S(2)}) copy-start(f32[5]{0:T(128)} %constant.90) | copy-start | bytes 64
  292.3 10.9 %collective-permute-start.7 = (f32[5,32,1,1024]{3,1,0,2:T(8,128)S(1)}, f32[5,32,1,1024]{3,1,0,2:T(8,128)S(1)}, u32[]{:S(2)}, u32[]{:S(2)}) collective-permute-start(f32[5,32,1,1024]{3,1,0,2:T(8,128)S(1)} %get-tuple-element.38), channel_id=1, source_target_pairs={{0,1},{1,2},{2,3},{4,5},{5,6},{6,7},{8,9},{9,10},{10,11},{12,13},{... | collective-permute-start | bytes 1966088 | tf_op jit(solution)/shard_map/ppermute | solution.py:184
  295.7 9.0 %collective-permute-start.6 = (f32[5,32,1,1024]{3,1,0,2:T(8,128)S(1)}, f32[5,32,1,1024]{3,1,0,2:T(8,128)S(1)}, u32[]{:S(2)}, u32[]{:S(2)}) collective-permute-start(f32[5,32,1,1024]{3,1,0,2:T(8,128)S(1)} %get-tuple-element.39), channel_id=1, source_target_pairs={{1,0},{2,1},{3,2},{5,4},{6,5},{7,6},{9,8},{10,9},{11,10},{13,12},{... | collective-permute-start | bytes 1966088 | tf_op jit(solution)/shard_map/ppermute | solution.py:184
  297.0 6.2 %collective-permute-start.4 = (f32[5,1,2,1024]{3,1,0,2:T(1,128)S(1)}, f32[5,1,2,1024]{3,1,0,2:T(1,128)S(1)}, u32[]{:S(2)}, u32[]{:S(2)}) collective-permute-start(f32[5,1,2,1024]{3,1,0,2:T(1,128)S(1)} %get-tuple-element.36), channel_id=1, source_target_pairs={{4,0},{5,1},{6,2},{7,3},{12,8},{13,9},{14,10},{15,11},{20,16},{21,... | collective-permute-start | bytes 122888 | tf_op jit(solution)/shard_map/ppermute | solution.py:184
  298.3 6.4 %collective-permute-start.5 = (f32[5,1,2,1024]{3,1,0,2:T(1,128)S(1)}, f32[5,1,2,1024]{3,1,0,2:T(1,128)S(1)}, u32[]{:S(2)}, u32[]{:S(2)}) collective-permute-start(f32[5,1,2,1024]{3,1,0,2:T(1,128)S(1)} %get-tuple-element.37), channel_id=1, source_target_pairs={{0,4},{1,5},{2,6},{3,7},{8,12},{9,13},{10,14},{11,15},{16,20},{17,... | collective-permute-start | bytes 122888 | tf_op jit(solution)/shard_map/ppermute | solution.py:184
  306.1 12.6 %collective-permute-start.11 = (f32[5,32,1,1024]{3,1,0,2:T(8,128)S(1)}, f32[5,32,1,1024]{3,1,0,2:T(8,128)S(1)}, u32[]{:S(2)}, u32[]{:S(2)}) collective-permute-start(f32[5,32,1,1024]{3,1,0,2:T(8,128)S(1)} %get-tuple-element.32), channel_id=1, source_target_pairs={{0,1},{1,2},{2,3},{4,5},{5,6},{6,7},{8,9},{9,10},{10,11},{12,13},{... | collective-permute-start | bytes 1966088 | tf_op jit(solution)/shard_map/ppermute | solution.py:184
  311.2 9.0 %collective-permute-start.10 = (f32[5,32,1,1024]{3,1,0,2:T(8,128)S(1)}, f32[5,32,1,1024]{3,1,0,2:T(8,128)S(1)}, u32[]{:S(2)}, u32[]{:S(2)}) collective-permute-start(f32[5,32,1,1024]{3,1,0,2:T(8,128)S(1)} %get-tuple-element.33), channel_id=1, source_target_pairs={{1,0},{2,1},{3,2},{5,4},{6,5},{7,6},{9,8},{10,9},{11,10},{13,12},{... | collective-permute-start | bytes 1966088 | tf_op jit(solution)/shard_map/ppermute | solution.py:184
  312.5 6.3 %collective-permute-start.8 = (f32[5,1,2,1024]{3,1,0,2:T(1,128)S(1)}, f32[5,1,2,1024]{3,1,0,2:T(1,128)S(1)}, u32[]{:S(2)}, u32[]{:S(2)}) collective-permute-start(f32[5,1,2,1024]{3,1,0,2:T(1,128)S(1)} %get-tuple-element.30), channel_id=1, source_target_pairs={{4,0},{5,1},{6,2},{7,3},{12,8},{13,9},{14,10},{15,11},{20,16},{21,... | collective-permute-start | bytes 122888 | tf_op jit(solution)/shard_map/ppermute | solution.py:184
  313.8 6.4 %collective-permute-start.9 = (f32[5,1,2,1024]{3,1,0,2:T(1,128)S(1)}, f32[5,1,2,1024]{3,1,0,2:T(1,128)S(1)}, u32[]{:S(2)}, u32[]{:S(2)}) collective-permute-start(f32[5,1,2,1024]{3,1,0,2:T(1,128)S(1)} %get-tuple-element.31), channel_id=1, source_target_pairs={{0,4},{1,5},{2,6},{3,7},{8,12},{9,13},{10,14},{11,15},{16,20},{17,... | collective-permute-start | bytes 122888 | tf_op jit(solution)/shard_map/ppermute | solution.py:184
  321.5 12.3 %collective-permute-start.15 = (f32[5,32,1,1024]{3,1,0,2:T(8,128)S(1)}, f32[5,32,1,1024]{3,1,0,2:T(8,128)S(1)}, u32[]{:S(2)}, u32[]{:S(2)}) collective-permute-start(f32[5,32,1,1024]{3,1,0,2:T(8,128)S(1)} %get-tuple-element.26), channel_id=1, source_target_pairs={{0,1},{1,2},{2,3},{4,5},{5,6},{6,7},{8,9},{9,10},{10,11},{12,13},{... | collective-permute-start | bytes 1966088 | tf_op jit(solution)/shard_map/ppermute | solution.py:184
  326.3 9.0 %collective-permute-start.14 = (f32[5,32,1,1024]{3,1,0,2:T(8,128)S(1)}, f32[5,32,1,1024]{3,1,0,2:T(8,128)S(1)}, u32[]{:S(2)}, u32[]{:S(2)}) collective-permute-start(f32[5,32,1,1024]{3,1,0,2:T(8,128)S(1)} %get-tuple-element.27), channel_id=1, source_target_pairs={{1,0},{2,1},{3,2},{5,4},{6,5},{7,6},{9,8},{10,9},{11,10},{13,12},{... | collective-permute-start | bytes 1966088 | tf_op jit(solution)/shard_map/ppermute | solution.py:184
  327.7 6.2 %collective-permute-start.12 = (f32[5,1,2,1024]{3,1,0,2:T(1,128)S(1)}, f32[5,1,2,1024]{3,1,0,2:T(1,128)S(1)}, u32[]{:S(2)}, u32[]{:S(2)}) collective-permute-start(f32[5,1,2,1024]{3,1,0,2:T(1,128)S(1)} %get-tuple-element.24), channel_id=1, source_target_pairs={{4,0},{5,1},{6,2},{7,3},{12,8},{13,9},{14,10},{15,11},{20,16},{21,... | collective-permute-start | bytes 122888 | tf_op jit(solution)/shard_map/ppermute | solution.py:184
  329.0 6.4 %collective-permute-start.13 = (f32[5,1,2,1024]{3,1,0,2:T(1,128)S(1)}, f32[5,1,2,1024]{3,1,0,2:T(1,128)S(1)}, u32[]{:S(2)}, u32[]{:S(2)}) collective-permute-start(f32[5,1,2,1024]{3,1,0,2:T(1,128)S(1)} %get-tuple-element.25), channel_id=1, source_target_pairs={{0,4},{1,5},{2,6},{3,7},{8,12},{9,13},{10,14},{11,15},{16,20},{17,... | collective-permute-start | bytes 122888 | tf_op jit(solution)/shard_map/ppermute | solution.py:184

commit v2 on v1

--- a/solution.py
+++ b/solution.py
@@ -189,23 +189,34 @@
     sectors = lax.axis_size("az")
     length = sectors * sector
     shift_value = shift[0]
-    rows = layers * variables * radial
-    piece = lax.all_to_all(cycle.reshape(sectors, rows // sectors, sector), "az", split_axis=0, concat_axis=0, tiled=True)
     tables = shift_tables(shift_value, length)
     matrices = filter_matrices(shift, tables, length)
+
+    def across(part):
+        return lax.all_to_all(part, "az", split_axis=0, concat_axis=0, tiled=True)
+
+    def passed(pieces):
+        return to_sectors(filtered(to_quarters(pieces), tables, matrices), sectors)
+
+    lead = cycle[:1].reshape(sectors, -1, sector)
+    rest = cycle[1:].reshape(sectors, -1, sector)
+    lead = across(lead)
 
     weights = jnp.array(LAYER_WEIGHTS, jnp.float32)
     cells = radial // KR
     grouped = cycle.reshape(layers, variables, cells, KR, sector)
     mean = jnp.sum(jnp.sum(grouped * weights[:, None, None, None, None], axis=0), axis=2) / KR
     around = lax.all_gather(mean.reshape(variables * cells, sector), "az", axis=0, tiled=False)
-    ghost_all = to_sectors(filtered(to_quarters(around), tables, matrices), sectors)
-    ghost = lax.dynamic_index_in_dim(ghost_all, lax.axis_index("az"), 0, keepdims=False)
+    lead, around, rest = lax.optimization_barrier((lead, around, rest))
+    rest = across(rest)
+
+    ghost = lax.dynamic_index_in_dim(passed(around), lax.axis_index("az"), 0, keepdims=False)
     ghost = lax.all_gather(ghost.reshape(variables, cells, sector), "ax", axis=1, tiled=True)
 
-    moved = to_sectors(filtered(to_quarters(piece), tables, matrices), sectors)
-    shifted_cycle = lax.all_to_all(moved, "az", split_axis=0, concat_axis=0, tiled=True)
-    shifted_cycle = shifted_cycle.reshape(layers, variables, radial, sector)
+    lead, rest = lax.optimization_barrier((passed(lead), rest))
+    lead = across(lead).reshape(1, variables, radial, sector)
+    rest = across(passed(rest)).reshape(layers - 1, variables, radial, sector)
+    shifted_cycle = jnp.concatenate([lead, rest], axis=0)
 
     mask = owner.astype(jnp.float32)[None, :, :, None]
     speeds = jnp.array(AXIAL_SPEEDS, jnp.float32)[:, None, None, None]

time: 348 us -> 284 us (0.82)
  blocking collectives: 118 us -> 48.5 us
  waiting for transfers between devices: 107 us -> 95.1 us
  starting transfers between devices: 55.5 us -> 65.9 us
  other arithmetic: 8.47 us -> 14.2 us
  Pallas kernels: 27.7 us -> 31.6 us
    all_gather x1, blocking collectives: 110 us -> 38.4 us  [on_device(): lax.all_gather(mean.reshape(variables * cells, sector), 'az', axis=0, til...]
    all_to_all x2 -> x4, waiting for transfers between devices: 103 us -> 91 us  [across(): return lax.all_to_all(part, 'az', split_axis=0, concat_axis=0, tiled=True)]
    all_to_all x2 -> x4, starting transfers between devices: 11.7 us -> 20.9 us  [across(): return lax.all_to_all(part, 'az', split_axis=0, concat_axis=0, tiled=True)]
    slice x0 -> x2, local copies, waits for them, and re-layouts: none -> 7.25 us  [the longest x1 4.73 us: on_device(): rest = cycle[1:].reshape(sectors, -1, sector)]
    unnamed x36 -> x39, local copies, waits for them, and re-layouts: 19.8 us -> 13.8 us
    concatenate x0 -> x1, other arithmetic: none -> 5.71 us  [on_device(): shifted_cycle = jnp.concatenate([lead, rest], axis=0)]
    pallas_call x2 -> x3, Pallas kernels: 19.7 us -> 23.6 us  [filtered(): pl.pallas_call(filter_body, grid=(count // block,), out_shape=jax.ShapeDt...]
  transfers between devices with their start and end apart: 18 -> 20, of which waited for: 4 -> 5; matrix products, arithmetic and copies ran while one was open for 7% -> 9% of each run, Pallas kernels for 4% -> 11%
where the time goes in v2:
time: 284 us; the launch traced here: 283 us
  waiting for transfers between devices  95.1 us (33%)
  starting transfers between devices  65.9 us (23%)
  blocking collectives  48.5 us (17%)
  Pallas kernels  31.6 us (11%)
  local copies, waits for them, and re-layouts  25.5 us (9%)
  other arithmetic  14.2 us (5%)
    all_to_all x4, waiting for transfers between devices, across(): return lax.all_to_all(part, 'az', split_axis=0, concat_axis=0, tiled=True)  91 us
    ppermute x16, starting transfers between devices, shifted(): return (lax.ppermute(last, axis, up), lax.ppermute(leading, axis, down))  45 us
    all_gather x1, blocking collectives, on_device(): lax.all_gather(mean.reshape(variables * cells, sector), 'az', axis=0, til...  38.4 us
    pallas_call x3, Pallas kernels, filtered(): pl.pallas_call(filter_body, grid=(count // block,), out_shape=jax.ShapeDt...  23.6 us
    all_to_all x4, starting transfers between devices, across(): return lax.all_to_all(part, 'az', split_axis=0, concat_axis=0, tiled=True)  20.9 us
    unnamed x39, local copies, waits for them, and re-layouts  13.8 us
    all_gather x1, blocking collectives, on_device(): lax.all_gather(ghost.reshape(variables, cells, sector), 'ax', axis=1, til...  10.2 us
    pallas_call x1, Pallas kernels, filter_matrices(): pl.pallas_call(lambda *refs: kernel_matrix_body(length, block, *refs), gr...  7.95 us
  transfers between devices with their start and end apart: 20, of which 5 were waited for; matrix products, arithmetic and copies ran while one was open for 9% of the time, Pallas kernels for 11%

profile of v2, /device:TPU:0, one launch (start us, length us, event | category | flops | bytes accessed | tf_op | source)
XLA Modules:
  0.0 282.7 jit_solution(6211971278771144785)
XLA Ops:
  0.6 2.5 slice.92
  3.2 6.4 %all-to-all-start = ((f32[4,80,1024]{2,1,0:T(8,128)}), f32[4,80,1024]{2,1,0:T(8,128)S(1)}, u32[]{:S(2)}, u32[]{:S(2)}) async-start(f32[4,80,1024]{2,1,0:T(8,128)} %bitcast.22), calls=%async_computation | async-start | bytes 2621440 | tf_op jit(solution)/shard_map/all_to_all | solution.py:196
  9.6 4.7 %slice.93 = f32[3,5,64,1024]{3,2,1,0:T(8,128)} slice(f32[4,5,64,1024]{3,2,1,0:T(8,128)} %param.9), slice={[1:4], [0:5], [0:64], [0:1024]} | slice | bytes 7864320 | tf_op jit(solution)/shard_map/slice | solution.py:202
  14.4 0.7 multiply_reduce_fusion
  15.1 0.3 bitcast_reduce_fusion
  15.4 38.4 %all_gather.6.x_ref = f32[4,40,1024]{2,1,0:T(8,128)} all-gather(f32[1,40,1024]{2,1,0:T(8,128)S(1)} %multiply_bitcast_fusion), channel_id=1, replica_groups=mesh['az'=4,'rad'=2,'ax'=4] {'az'}, dimensions={0}, use_global_device_ids=true | all-gather | bytes 819200 | tf_op jit(solution)/shard_map/all_gather | solution.py:209
  53.8 5.0 %all-to-all-start.1 = ((f32[4,240,1024]{2,1,0:T(8,128)}), f32[4,240,1024]{2,1,0:T(8,128)}, u32[]{:S(2)}, u32[]{:S(2)}) async-start(f32[4,240,1024]{2,1,0:T(8,128)} %bitcast.21), calls=%async_computation.1 | async-start | bytes 7864320 | tf_op jit(solution)/shard_map/all_to_all | solution.py:196
  59.5 0.1 fusion.9
  59.6 0.1 fusion.11
  59.8 0.1 fusion.13
  60.0 1.0 copy-done.5
  61.1 8.0 %filter_matrices.1 = (bf16[1024,1024]{1,0:T(8,128)(2,1)S(1)}, bf16[1024,1024]{1,0:T(8,128)(2,1)S(1)}, bf16[1024,1024]{1,0:T(8,128)(2,1)S(1)}, bf16[1024,1024]{1,0:T(8,128)(2,1)S(1)}) custom-call(s32[1]{0:T(128)} %copy.60.refs_0_, f32[8,1024]{1,0:T(8,128)S(1)} %stack.8.refs_1_.tab_ref, f32[1024,4]{1,0:T(8,128)S(1)} %copy-done.5), custom_call_target="tpu_custom_call" | custom-call | flops 62914560 | bytes 8388608 | tf_op jit(solution)/shard_map/filter_matrices/pallas_call | solution.py:89
  69.0 1.4 copy-done
  70.4 1.4 copy-done.2
  71.8 1.4 copy-done.3
  73.2 6.9 %spectral_filter.4 = f32[4,80,1024]{2,1,0:T(8,128)} custom-call(f32[4,80,1024]{2,1,0:T(8,128)S(1)} %all-to-all-done.x_ref, f32[8,1024]{1,0:T(8,128)S(1)} %stack.8.refs_1_.tab_ref, bf16[1024,1024]{1,0:T(8,128)(2,1)S(1)} %get-tuple-element.12.eh_ref, bf16[1024,1024]{1,0:T(8,128)(2,1)} %copy-done, bf16[1024,1024]{1,0:T(8,128)(2,1)} %copy-done.2, ...), custom_call_target="tpu_custom_call" | custom-call | flops 2013265920 | bytes 11010048 | tf_op jit(solution)/shard_map/spectral_filter/pallas_call | solution.py:145
  80.1 63.0 %all-to-all-done.1.x_ref = f32[4,240,1024]{2,1,0:T(8,128)} async-done(((f32[4,240,1024]{2,1,0:T(8,128)}), f32[4,240,1024]{2,1,0:T(8,128)}, u32[]{:S(2)}, u32[]{:S(2)}) %all-to-all-start.1) | async-done | bytes 3932192 | tf_op jit(solution)/shard_map/all_to_all | solution.py:196
  143.1 4.3 %all-to-all-start.2 = ((f32[4,80,1024]{2,1,0:T(8,128)}), f32[4,80,1024]{2,1,0:T(8,128)}, u32[]{:S(2)}, u32[]{:S(2)}) async-start(f32[4,80,1024]{2,1,0:T(8,128)} %spectral_filter.4), calls=%async_computation.2 | async-start | bytes 2621440 | tf_op jit(solution)/shard_map/all_to_all | solution.py:196
  147.4 1.0 fusion.26
  148.4 1.0 copy.56
  149.4 2.1 collective-permute-start.3
  151.5 0.9 copy.55
  152.5 1.3 collective-permute-start.2
  153.8 0.7 copy.37
  154.5 1.3 collective-permute-start
  155.7 0.7 copy.38
  156.4 4.7 %collective-permute-start.1 = (f32[5,1,2,1024]{3,1,0,2:T(1,128)}, f32[5,1,2,1024]{3,1,0,2:T(1,128)S(1)}, u32[]{:S(2)}, u32[]{:S(2)}) collective-permute-start(f32[5,1,2,1024]{3,1,0,2:T(1,128)} %copy.38), channel_id=1, source_target_pairs={{0,4},{1,5},{2,6},{3,7},{8,12},{9,13},{10,14},{11,15},{16,20},{17,... | collective-permute-start | bytes 122888 | tf_op jit(solution)/shard_map/ppermute | solution.py:184
  161.1 0.7 fusion.24
  161.8 1.5 copy.57
  163.3 1.5 copy.58
  164.8 1.6 copy-done.1
  166.4 4.3 %spectral_filter.3 = f32[4,40,1024]{2,1,0:T(8,128)S(1)} custom-call(f32[4,40,1024]{2,1,0:T(8,128)S(1)} %copy-done.4, f32[8,1024]{1,0:T(8,128)S(1)} %stack.8.refs_1_.tab_ref, bf16[1024,1024]{1,0:T(8,128)(2,1)S(1)} %get-tuple-element.12.eh_ref, bf16[1024,1024]{1,0:T(8,128)(2,1)S(1)} %copy-done.1, bf16[1024,1024]{1,0:T(8,128)(2,1)} %copy-done.2, ...), custom_call_target="tpu_custom_call" | custom-call | flops 1006632960 | bytes 9699328 | tf_op jit(solution)/shard_map/spectral_filter/pallas_call | solution.py:145
  170.7 12.5 %spectral_filter.5 = f32[4,240,1024]{2,1,0:T(8,128)} custom-call(f32[4,240,1024]{2,1,0:T(8,128)} %all-to-all-done.1.x_ref, f32[8,1024]{1,0:T(8,128)S(1)} %stack.8.refs_1_.tab_ref, bf16[1024,1024]{1,0:T(8,128)(2,1)S(1)} %get-tuple-element.12.eh_ref, bf16[1024,1024]{1,0:T(8,128)(2,1)S(1)} %copy-done.1, bf16[1024,1024]{1,0:T(8,128)(2,1)} %copy-done.2, ...), custom_call_target="tpu_custom_call" | custom-call | flops 6039797760 | bytes 16252928 | tf_op jit(solution)/shard_map/spectral_filter/pallas_call | solution.py:145
  183.2 5.2 %all-to-all-start.3 = ((f32[4,240,1024]{2,1,0:T(8,128)}), f32[4,240,1024]{2,1,0:T(8,128)}, u32[]{:S(2)}, u32[]{:S(2)}) async-start(f32[4,240,1024]{2,1,0:T(8,128)} %spectral_filter.5), calls=%async_computation.3 | async-start | bytes 7864320 | tf_op jit(solution)/shard_map/all_to_all | solution.py:196
  188.4 10.2 %all_gather.7 = f32[5,32,1024]{2,1,0:T(8,128)S(1)} all-gather(f32[5,8,1024]{2,1,0:T(8,128)S(1)} %dynamic-slice_bitcast_fusion), channel_id=1, replica_groups=mesh['az'=4,'rad'=2,'ax'=4] {'ax'}, dimensions={1}, use_global_device_ids=true | all-gather | bytes 819200 | tf_op jit(solution)/shard_map/all_gather | solution.py:214
  198.5 0.1 bitcast_select_fusion.3
  198.7 2.6 multiply_add_fusion.2
  201.4 0.1 fusion.23
  201.5 3.4 %collective-permute-start.7 = (f32[5,32,1,1024]{3,1,0,2:T(8,128)S(1)}, f32[5,32,1,1024]{3,1,0,2:T(8,128)S(1)}, u32[]{:S(2)}, u32[]{:S(2)}) collective-permute-start(f32[5,32,1,1024]{3,1,0,2:T(8,128)S(1)} %get-tuple-element.48), channel_id=1, source_target_pairs={{0,1},{1,2},{2,3},{4,5},{5,6},{6,7},{8,9},{9,10},{10,11},{12,13},{... | collective-permute-start | bytes 1966088 | tf_op jit(solution)/shard_map/ppermute | solution.py:184
  204.9 1.3 collective-permute-start.6
  206.3 1.3 collective-permute-start.4
  207.6 4.5 %collective-permute-start.5 = (f32[5,1,2,1024]{3,1,0,2:T(1,128)S(1)}, f32[5,1,2,1024]{3,1,0,2:T(1,128)S(1)}, u32[]{:S(2)}, u32[]{:S(2)}) collective-permute-start(f32[5,1,2,1024]{3,1,0,2:T(1,128)S(1)} %get-tuple-element.47), channel_id=1, source_target_pairs={{0,4},{1,5},{2,6},{3,7},{8,12},{9,13},{10,14},{11,15},{16,20},{17,... | collective-permute-start | bytes 122888 | tf_op jit(solution)/shard_map/ppermute | solution.py:184
  212.1 0.2 fusion.21
  212.5 1.4 collective-permute-done.5
  213.9 1.3 multiply_add_fusion.1
  215.2 0.1 fusion.20
  215.4 5.4 %collective-permute-start.11 = (f32[5,32,1,1024]{3,1,0,2:T(8,128)S(1)}, f32[5,32,1,1024]{3,1,0,2:T(8,128)S(1)}, u32[]{:S(2)}, u32[]{:S(2)}) collective-permute-start(f32[5,32,1,1024]{3,1,0,2:T(8,128)S(1)} %get-tuple-element.42), channel_id=1, source_target_pairs={{0,1},{1,2},{2,3},{4,5},{5,6},{6,7},{8,9},{9,10},{10,11},{12,13},{... | collective-permute-start | bytes 1966088 | tf_op jit(solution)/shard_map/ppermute | solution.py:184
  220.8 1.3 collective-permute-start.10
  222.1 1.3 collective-permute-start.8
  223.4 4.5 %collective-permute-start.9 = (f32[5,1,2,1024]{3,1,0,2:T(1,128)S(1)}, f32[5,1,2,1024]{3,1,0,2:T(1,128)S(1)}, u32[]{:S(2)}, u32[]{:S(2)}) collective-permute-start(f32[5,1,2,1024]{3,1,0,2:T(1,128)S(1)} %get-tuple-element.41), channel_id=1, source_target_pairs={{0,4},{1,5},{2,6},{3,7},{8,12},{9,13},{10,14},{11,15},{16,20},{17,... | collective-permute-start | bytes 122888 | tf_op jit(solution)/shard_map/ppermute | solution.py:184
  228.0 0.3 fusion.18
  228.4 1.4 collective-permute-done.9
  229.8 1.2 copy_add_fusion
  231.0 0.1 fusion.17
  231.1 5.2 %collective-permute-start.15 = (f32[5,32,1,1024]{3,1,0,2:T(8,128)S(1)}, f32[5,32,1,1024]{3,1,0,2:T(8,128)S(1)}, u32[]{:S(2)}, u32[]{:S(2)}) collective-permute-start(f32[5,32,1,1024]{3,1,0,2:T(8,128)S(1)} %get-tuple-element.36), channel_id=1, source_target_pairs={{0,1},{1,2},{2,3},{4,5},{5,6},{6,7},{8,9},{9,10},{10,11},{12,13},{... | collective-permute-start | bytes 1966088 | tf_op jit(solution)/shard_map/ppermute | solution.py:184
  236.3 1.3 collective-permute-start.14
  237.7 1.3 collective-permute-start.12
  239.0 4.8 %collective-permute-start.13 = (f32[5,1,2,1024]{3,1,0,2:T(1,128)S(1)}, f32[5,1,2,1024]{3,1,0,2:T(1,128)S(1)}, u32[]{:S(2)}, u32[]{:S(2)}) collective-permute-start(f32[5,1,2,1024]{3,1,0,2:T(1,128)S(1)} %get-tuple-element.35), channel_id=1, source_target_pairs={{0,4},{1,5},{2,6},{3,7},{8,12},{9,13},{10,14},{11,15},{16,20},{17,... | collective-permute-start | bytes 122888 | tf_op jit(solution)/shard_map/ppermute | solution.py:184
  243.8 0.2 fusion.15
  244.1 1.2 collective-permute-done.13
  245.4 1.5 multiply_add_fusion
  246.9 2.1 copy.47
  249.0 28.0 %all-to-all-done.3 = f32[4,240,1024]{2,1,0:T(8,128)} async-done(((f32[4,240,1024]{2,1,0:T(8,128)}), f32[4,240,1024]{2,1,0:T(8,128)}, u32[]{:S(2)}, u32[]{:S(2)}) %all-to-all-start.3) | async-done | bytes 3932192 | tf_op jit(solution)/shard_map/all_to_all | solution.py:196
  277.0 5.7 %pad_maximum_fusion = f32[4,5,64,1024]{3,2,1,0:T(8,128)} fusion(f32[3,5,64,1024]{3,2,1,0:T(8,128)} %bitcast.8, f32[1,5,64,1024]{3,2,1,0:T(8,128)} %bitcast.7), kind=kLoop, calls=%fused_computation | loop fusion | flops 1310720 | bytes 10485760 | tf_op jit(solution)/shard_map/concatenate | solution.py:219
  (56 shorter events, 0.6 us)
Async XLA Ops:
  3.2 11.2 %slice-start = ((s8[5242880]{0:T(1024)(128)(4,1)}), s8[1048576]{0:T(1024)(128)(4,1)S(1)}, s32[]{:S(2)}) async-start(s8[5242880]{0:T(1024)(128)(4,1)} %bitcast.19), calls=%async_computation.4 | async-start | bytes 2097152
  3.2 50.7 %all-to-all-start = ((f32[4,80,1024]{2,1,0:T(8,128)}), f32[4,80,1024]{2,1,0:T(8,128)S(1)}, u32[]{:S(2)}, u32[]{:S(2)}) async-start(f32[4,80,1024]{2,1,0:T(8,128)} %bitcast.22), calls=%async_computation | async-start | bytes 2621440 | tf_op jit(solution)/shard_map/all_to_all | solution.py:196
  9.6 4.7 %slice-start.1 = ((s8[5242880]{0:T(1024)(128)(4,1)}), s8[4194304]{0:T(1024)(128)(4,1)S(1)}, s32[]{:S(2)}) async-start(s8[5242880]{0:T(1024)(128)(4,1)} %bitcast.19), calls=%async_computation.5 | async-start | bytes 8388608
  9.6 4.7 %copy-start.14 = (f32[4]{0:T(128)S(1)}, f32[4]{0:T(128)}, u32[]{:S(2)}) copy-start(f32[4]{0:T(128)} %constant.84.clone) | copy-start | bytes 52
  53.8 6.1 %copy-start.11 = (f32[1,1024]{1,0:T(1,128)S(1)}, f32[1,1024]{1,0:T(1,128)}, u32[]{:S(2)}) copy-start(f32[1,1024]{1,0:T(1,128)} %constant.88) | copy-start | bytes 12292
  53.8 6.1 %copy-start.12 = (f32[1,1024]{1,0:T(1,128)S(1)}, f32[1,1024]{1,0:T(1,128)}, u32[]{:S(2)}) copy-start(f32[1,1024]{1,0:T(1,128)} %constant.89) | copy-start | bytes 12292
  53.8 89.2 %all-to-all-start.1 = ((f32[4,240,1024]{2,1,0:T(8,128)}), f32[4,240,1024]{2,1,0:T(8,128)}, u32[]{:S(2)}, u32[]{:S(2)}) async-start(f32[4,240,1024]{2,1,0:T(8,128)} %bitcast.21), calls=%async_computation.1 | async-start | bytes 7864320 | tf_op jit(solution)/shard_map/all_to_all | solution.py:196
  60.0 1.0 copy-start.5
  69.0 1.4 copy-start
  70.4 1.4 copy-start.2
  71.8 1.4 copy-start.3
  80.0 67.3 %copy-start.6 = (f32[5,32,2,1024]{3,2,1,0:T(2,128)S(1)}, f32[5,32,2,1024]{3,2,1,0:T(2,128)}, u32[]{:S(2)}) copy-start(f32[5,32,2,1024]{3,2,1,0:T(2,128)} %param.10) | copy-start | bytes 3932164
  143.1 40.1 %all-to-all-start.2 = ((f32[4,80,1024]{2,1,0:T(8,128)}), f32[4,80,1024]{2,1,0:T(8,128)}, u32[]{:S(2)}, u32[]{:S(2)}) async-start(f32[4,80,1024]{2,1,0:T(8,128)} %spectral_filter.4), calls=%async_computation.2 | async-start | bytes 2621440 | tf_op jit(solution)/shard_map/all_to_all | solution.py:196
  148.4 12.7 %copy-start.13 = (s32[32,2]{0,1:T(2,128)S(1)}, s32[32,2]{0,1:T(2,128)}, u32[]{:S(2)}) copy-start(s32[32,2]{0,1:T(2,128)} %param.12) | copy-start | bytes 772
  149.4 49.1 %collective-permute-start.3 = (f32[5,32,1,1024]{3,1,0,2:T(8,128)}, f32[5,32,1,1024]{3,1,0,2:T(8,128)}, u32[]{:S(2)}, u32[]{:S(2)}) collective-permute-start(f32[5,32,1,1024]{3,1,0,2:T(8,128)} %copy.56), channel_id=1, source_target_pairs={{0,1},{1,2},{2,3},{4,5},{5,6},{6,7},{8,9},{9,10},{10,11},{12,13},{... | collective-permute-start | bytes 1966088 | tf_op jit(solution)/shard_map/ppermute | solution.py:184
  152.5 46.2 %collective-permute-start.2 = (f32[5,32,1,1024]{3,1,0,2:T(8,128)}, f32[5,32,1,1024]{3,1,0,2:T(8,128)}, u32[]{:S(2)}, u32[]{:S(2)}) collective-permute-start(f32[5,32,1,1024]{3,1,0,2:T(8,128)} %copy.55), channel_id=1, source_target_pairs={{1,0},{2,1},{3,2},{5,4},{6,5},{7,6},{9,8},{10,9},{11,10},{13,12},{... | collective-permute-start | bytes 1966088 | tf_op jit(solution)/shard_map/ppermute | solution.py:184
  154.5 44.2 %collective-permute-start = (f32[5,1,2,1024]{3,1,0,2:T(1,128)}, f32[5,1,2,1024]{3,1,0,2:T(1,128)S(1)}, u32[]{:S(2)}, u32[]{:S(2)}) collective-permute-start(f32[5,1,2,1024]{3,1,0,2:T(1,128)} %copy.37), channel_id=1, source_target_pairs={{4,0},{5,1},{6,2},{7,3},{12,8},{13,9},{14,10},{15,11},{20,16},{21,... | collective-permute-start | bytes 122888 | tf_op jit(solution)/shard_map/ppermute | solution.py:184
  156.4 42.3 %collective-permute-start.1 = (f32[5,1,2,1024]{3,1,0,2:T(1,128)}, f32[5,1,2,1024]{3,1,0,2:T(1,128)S(1)}, u32[]{:S(2)}, u32[]{:S(2)}) collective-permute-start(f32[5,1,2,1024]{3,1,0,2:T(1,128)} %copy.38), channel_id=1, source_target_pairs={{0,4},{1,5},{2,6},{3,7},{8,12},{9,13},{10,14},{11,15},{16,20},{17,... | collective-permute-start | bytes 122888 | tf_op jit(solution)/shard_map/ppermute | solution.py:184
  163.3 1.5 copy-start.4
  164.8 1.6 copy-start.1
  183.2 15.5 %copy-start.9 = (f32[5,31,2,1024]{3,1,0,2:T(8,128)S(1)}, f32[5,31,2,1024]{3,1,0,2:T(8,128)}, u32[]{:S(2)}) copy-start(f32[5,31,2,1024]{3,1,0,2:T(8,128)} %copy.58) | copy-start | bytes 3809284
  183.2 93.8 %all-to-all-start.3 = ((f32[4,240,1024]{2,1,0:T(8,128)}), f32[4,240,1024]{2,1,0:T(8,128)}, u32[]{:S(2)}, u32[]{:S(2)}) async-start(f32[4,240,1024]{2,1,0:T(8,128)} %spectral_filter.5), calls=%async_computation.3 | async-start | bytes 7864320 | tf_op jit(solution)/shard_map/all_to_all | solution.py:196
  188.3 10.3 %copy-start.7 = (f32[5,32,2,1024]{3,2,1,0:T(2,128)S(1)}, f32[5,32,2,1024]{3,2,1,0:T(2,128)}, u32[]{:S(2)}) copy-start(f32[5,32,2,1024]{3,2,1,0:T(2,128)} %param.10) | copy-start | bytes 3932164
  188.4 10.3 %copy-start.8 = (f32[5,31,2,1024]{3,1,0,2:T(8,128)S(1)}, f32[5,31,2,1024]{3,1,0,2:T(8,128)}, u32[]{:S(2)}) copy-start(f32[5,31,2,1024]{3,1,0,2:T(8,128)} %copy.57) | copy-start | bytes 3809284
  188.4 10.3 %copy-start.10 = (f32[5]{0:T(128)S(1)}, f32[5]{0:T(128)}, u32[]{:S(2)}) copy-start(f32[5]{0:T(128)} %constant.90) | copy-start | bytes 64
  201.5 10.9 %collective-permute-start.7 = (f32[5,32,1,1024]{3,1,0,2:T(8,128)S(1)}, f32[5,32,1,1024]{3,1,0,2:T(8,128)S(1)}, u32[]{:S(2)}, u32[]{:S(2)}) collective-permute-start(f32[5,32,1,1024]{3,1,0,2:T(8,128)S(1)} %get-tuple-element.48), channel_id=1, source_target_pairs={{0,1},{1,2},{2,3},{4,5},{5,6},{6,7},{8,9},{9,10},{10,11},{12,13},{... | collective-permute-start | bytes 1966088 | tf_op jit(solution)/shard_map/ppermute | solution.py:184
  204.9 9.0 %collective-permute-start.6 = (f32[5,32,1,1024]{3,1,0,2:T(8,128)S(1)}, f32[5,32,1,1024]{3,1,0,2:T(8,128)S(1)}, u32[]{:S(2)}, u32[]{:S(2)}) collective-permute-start(f32[5,32,1,1024]{3,1,0,2:T(8,128)S(1)} %get-tuple-element.49), channel_id=1, source_target_pairs={{1,0},{2,1},{3,2},{5,4},{6,5},{7,6},{9,8},{10,9},{11,10},{13,12},{... | collective-permute-start | bytes 1966088 | tf_op jit(solution)/shard_map/ppermute | solution.py:184
  206.3 6.2 %collective-permute-start.4 = (f32[5,1,2,1024]{3,1,0,2:T(1,128)S(1)}, f32[5,1,2,1024]{3,1,0,2:T(1,128)S(1)}, u32[]{:S(2)}, u32[]{:S(2)}) collective-permute-start(f32[5,1,2,1024]{3,1,0,2:T(1,128)S(1)} %get-tuple-element.46), channel_id=1, source_target_pairs={{4,0},{5,1},{6,2},{7,3},{12,8},{13,9},{14,10},{15,11},{20,16},{21,... | collective-permute-start | bytes 122888 | tf_op jit(solution)/shard_map/ppermute | solution.py:184
  207.6 6.4 %collective-permute-start.5 = (f32[5,1,2,1024]{3,1,0,2:T(1,128)S(1)}, f32[5,1,2,1024]{3,1,0,2:T(1,128)S(1)}, u32[]{:S(2)}, u32[]{:S(2)}) collective-permute-start(f32[5,1,2,1024]{3,1,0,2:T(1,128)S(1)} %get-tuple-element.47), channel_id=1, source_target_pairs={{0,4},{1,5},{2,6},{3,7},{8,12},{9,13},{10,14},{11,15},{16,20},{17,... | collective-permute-start | bytes 122888 | tf_op jit(solution)/shard_map/ppermute | solution.py:184
  215.4 13.0 %collective-permute-start.11 = (f32[5,32,1,1024]{3,1,0,2:T(8,128)S(1)}, f32[5,32,1,1024]{3,1,0,2:T(8,128)S(1)}, u32[]{:S(2)}, u32[]{:S(2)}) collective-permute-start(f32[5,32,1,1024]{3,1,0,2:T(8,128)S(1)} %get-tuple-element.42), channel_id=1, source_target_pairs={{0,1},{1,2},{2,3},{4,5},{5,6},{6,7},{8,9},{9,10},{10,11},{12,13},{... | collective-permute-start | bytes 1966088 | tf_op jit(solution)/shard_map/ppermute | solution.py:184
  220.8 9.0 %collective-permute-start.10 = (f32[5,32,1,1024]{3,1,0,2:T(8,128)S(1)}, f32[5,32,1,1024]{3,1,0,2:T(8,128)S(1)}, u32[]{:S(2)}, u32[]{:S(2)}) collective-permute-start(f32[5,32,1,1024]{3,1,0,2:T(8,128)S(1)} %get-tuple-element.43), channel_id=1, source_target_pairs={{1,0},{2,1},{3,2},{5,4},{6,5},{7,6},{9,8},{10,9},{11,10},{13,12},{... | collective-permute-start | bytes 1966088 | tf_op jit(solution)/shard_map/ppermute | solution.py:184
  222.1 6.3 %collective-permute-start.8 = (f32[5,1,2,1024]{3,1,0,2:T(1,128)S(1)}, f32[5,1,2,1024]{3,1,0,2:T(1,128)S(1)}, u32[]{:S(2)}, u32[]{:S(2)}) collective-permute-start(f32[5,1,2,1024]{3,1,0,2:T(1,128)S(1)} %get-tuple-element.40), channel_id=1, source_target_pairs={{4,0},{5,1},{6,2},{7,3},{12,8},{13,9},{14,10},{15,11},{20,16},{21,... | collective-permute-start | bytes 122888 | tf_op jit(solution)/shard_map/ppermute | solution.py:184
  223.4 6.4 %collective-permute-start.9 = (f32[5,1,2,1024]{3,1,0,2:T(1,128)S(1)}, f32[5,1,2,1024]{3,1,0,2:T(1,128)S(1)}, u32[]{:S(2)}, u32[]{:S(2)}) collective-permute-start(f32[5,1,2,1024]{3,1,0,2:T(1,128)S(1)} %get-tuple-element.41), channel_id=1, source_target_pairs={{0,4},{1,5},{2,6},{3,7},{8,12},{9,13},{10,14},{11,15},{16,20},{17,... | collective-permute-start | bytes 122888 | tf_op jit(solution)/shard_map/ppermute | solution.py:184
  231.1 12.9 %collective-permute-start.15 = (f32[5,32,1,1024]{3,1,0,2:T(8,128)S(1)}, f32[5,32,1,1024]{3,1,0,2:T(8,128)S(1)}, u32[]{:S(2)}, u32[]{:S(2)}) collective-permute-start(f32[5,32,1,1024]{3,1,0,2:T(8,128)S(1)} %get-tuple-element.36), channel_id=1, source_target_pairs={{0,1},{1,2},{2,3},{4,5},{5,6},{6,7},{8,9},{9,10},{10,11},{12,13},{... | collective-permute-start | bytes 1966088 | tf_op jit(solution)/shard_map/ppermute | solution.py:184
  236.3 9.0 %collective-permute-start.14 = (f32[5,32,1,1024]{3,1,0,2:T(8,128)S(1)}, f32[5,32,1,1024]{3,1,0,2:T(8,128)S(1)}, u32[]{:S(2)}, u32[]{:S(2)}) collective-permute-start(f32[5,32,1,1024]{3,1,0,2:T(8,128)S(1)} %get-tuple-element.37), channel_id=1, source_target_pairs={{1,0},{2,1},{3,2},{5,4},{6,5},{7,6},{9,8},{10,9},{11,10},{13,12},{... | collective-permute-start | bytes 1966088 | tf_op jit(solution)/shard_map/ppermute | solution.py:184
  237.7 6.4 %collective-permute-start.12 = (f32[5,1,2,1024]{3,1,0,2:T(1,128)S(1)}, f32[5,1,2,1024]{3,1,0,2:T(1,128)S(1)}, u32[]{:S(2)}, u32[]{:S(2)}) collective-permute-start(f32[5,1,2,1024]{3,1,0,2:T(1,128)S(1)} %get-tuple-element.34), channel_id=1, source_target_pairs={{4,0},{5,1},{6,2},{7,3},{12,8},{13,9},{14,10},{15,11},{20,16},{21,... | collective-permute-start | bytes 122888 | tf_op jit(solution)/shard_map/ppermute | solution.py:184
  239.0 6.4 %collective-permute-start.13 = (f32[5,1,2,1024]{3,1,0,2:T(1,128)S(1)}, f32[5,1,2,1024]{3,1,0,2:T(1,128)S(1)}, u32[]{:S(2)}, u32[]{:S(2)}) collective-permute-start(f32[5,1,2,1024]{3,1,0,2:T(1,128)S(1)} %get-tuple-element.35), channel_id=1, source_target_pairs={{0,4},{1,5},{2,6},{3,7},{8,12},{9,13},{10,14},{11,15},{16,20},{17,... | collective-permute-start | bytes 122888 | tf_op jit(solution)/shard_map/ppermute | solution.py:184

commit v3 on v2

--- a/solution.py
+++ b/solution.py
@@ -53,13 +53,13 @@
     return jnp.asarray(np.stack(cols, axis=1), jnp.float32)
 
 
-def kernel_matrix_body(length, block, shift_ref, rows_ref, cols_ref, eh_ref, el_ref, hh_ref, hl_ref):
+def matrix_values(length, first, block, shift_value, rows, cols):
     quarter = length // 4
     even, half = class_counts(length)
     shape = (block, quarter)
-    source = lax.broadcasted_iota(jnp.int32, shape, 0) + pl.program_id(0) * block
+    source = lax.broadcasted_iota(jnp.int32, shape, 0) + first
     target = lax.broadcasted_iota(jnp.int32, shape, 1)
-    apart = (target - source - shift_ref[0]) & (2 * quarter - 1)
+    apart = (target - source - shift_value) & (2 * quarter - 1)
     apart = jnp.where(apart >= quarter, apart - 2 * quarter, apart)
     near = jnp.where(apart > quarter // 2, quarter - apart, apart)
     near = jnp.where(apart < -(quarter // 2), -quarter - apart, near)
@@ -71,15 +71,19 @@
     sine = u + u * (w * poly)
     zero = near == 0
     inverse = 0.25 / (quarter * jnp.where(zero, 1.0, sine))
-    top_even = rows_ref[0:1, :] * cols_ref[:, 1:2] - rows_ref[1:2, :] * cols_ref[:, 0:1]
-    top_half = rows_ref[2:3, :] * cols_ref[:, 3:4] - rows_ref[3:4, :] * cols_ref[:, 2:3]
+    top_even = rows[0:1, :] * cols[:, 1:2] - rows[1:2, :] * cols[:, 0:1]
+    top_half = rows[2:3, :] * cols[:, 3:4] - rows[3:4, :] * cols[:, 2:3]
     sign = jnp.where(apart == 0, 1.0, -1.0)
     m_even = jnp.where(zero, 0.25 * even / quarter, top_even * inverse)
     m_half = jnp.where(zero, sign * (0.25 * half / quarter), top_half * inverse)
-    for value, high_ref, low_ref in ((m_even, eh_ref, el_ref), (m_half, hh_ref, hl_ref)):
-        high = value.astype(jnp.bfloat16)
-        high_ref[...] = high
-        low_ref[...] = (value - high.astype(jnp.float32)).astype(jnp.bfloat16)
+    return split(m_even) + split(m_half)
+
+
+def kernel_matrix_body(length, block, shift_ref, rows_ref, cols_ref, *out_refs):
+    first = pl.program_id(0) * block
+    values = matrix_values(length, first, block, shift_ref[0], rows_ref[...], cols_ref[...])
+    for ref, value in zip(out_refs, values):
+        ref[...] = value
 
 
 def filter_matrices(shift, tables, length):
@@ -117,9 +121,10 @@
     )
 
 
-def filter_body(x_ref, tab_ref, eh_ref, el_ref, hh_ref, hl_ref, out_ref):
-    count = x_ref.shape[1]
-    x0, x1, x2, x3 = [x_ref[i] for i in range(4)]
+def filter_quarters(parts, tab_ref, matrix_refs):
+    x0, x1, x2, x3 = parts
+    count = x0.shape[0]
+    eh_ref, el_ref, hh_ref, hl_ref = matrix_refs
     cos_t, sin_t = 2.0 * tab_ref[4:5, :], 2.0 * tab_ref[5:6, :]
     cos_s, sin_s = tab_ref[6:7, :], tab_ref[7:8, :]
     even, odd = x0 + x2, x1 + x3
@@ -131,10 +136,13 @@
     zre = cos_t * ure - sin_t * uim
     zim = cos_t * uim + sin_t * ure
     plus, minus = z0 + z2, z0 - z2
-    out_ref[0] = plus + zre
-    out_ref[1] = minus - zim
-    out_ref[2] = plus - zre
-    out_ref[3] = minus + zim
+    return plus + zre, minus - zim, plus - zre, minus + zim
+
+
+def filter_body(x_ref, tab_ref, eh_ref, el_ref, hh_ref, hl_ref, out_ref):
+    values = filter_quarters([x_ref[i] for i in range(4)], tab_ref, (eh_ref, el_ref, hh_ref, hl_ref))
+    for i, value in enumerate(values):
+        out_ref[i] = value
 
 
 def filtered(quarters, tables, matrices):
@@ -175,6 +183,167 @@
     return quarters.reshape(4, count, per, sector).transpose(0, 2, 1, 3).reshape(sectors, count, sector)
 
 
+def still_tables(length):
+    quarter = length // 4
+    target = np.arange(quarter)
+    rows = []
+    for count in class_counts(length):
+        angle = (count * target % (2 * quarter)) * (np.pi / quarter)
+        rows += [np.sin(angle), np.cos(angle)]
+    angle = target * (2.0 * np.pi / length)
+    rows += [np.cos(angle), np.sin(angle)] * 2
+    return jnp.asarray(np.stack(rows), jnp.float32)
+
+
+def turn_values(shift_value, length):
+    quarter = length // 4
+    even, half = class_counts(length)
+    steps = jnp.array([2 * even, 2 * half, 1], jnp.int32) * shift_value
+    angle = jnp.remainder(steps, length).astype(jnp.float32) * (2.0 * math.pi / length)
+    return jnp.concatenate([jnp.sin(angle), jnp.cos(angle)])
+
+
+def forward_body(length, block, cells, turn_ref, shift_ref, rows_ref, cols_ref, cycle_ref, out_ref, ghost_ref,
+                 land, done, local, mean, ghosts, eh, el, hh, hl, tab, send_sem, recv_sem, mean_send, mean_recv, local_sem, store_sem):
+    count = land.shape[1]
+    chunks = count // block
+    quarter = length // 4
+    me = lax.axis_index("az")
+    matrices = (eh, el, hh, hl)
+
+    barrier = pltpu.get_barrier_semaphore()
+    for k in (1, 2, 3):
+        pl.semaphore_signal(barrier, inc=1, device_id={"az": lax.rem(me + k, 4)}, device_id_type=pl.DeviceIdType.MESH)
+    pl.semaphore_wait(barrier, 3)
+
+    def part(c):
+        return pl.ds(pl.multiple_of(c * block, block), block)
+
+    def send(c, k):
+        peer = lax.rem(me + k, 4)
+        return pltpu.make_async_remote_copy(
+            src_ref=cycle_ref.at[peer, part(c)],
+            dst_ref=land.at[me, part(c)],
+            send_sem=send_sem.at[c, k - 1],
+            recv_sem=recv_sem.at[c, k - 1],
+            device_id={"az": peer},
+            device_id_type=pl.DeviceIdType.MESH,
+        )
+
+    def send_mean(k):
+        return pltpu.make_async_remote_copy(
+            src_ref=mean.at[me],
+            dst_ref=mean.at[me],
+            send_sem=mean_send.at[k - 1],
+            recv_sem=mean_recv.at[k - 1],
+            device_id={"az": lax.rem(me + k, 4)},
+            device_id_type=pl.DeviceIdType.MESH,
+        )
+
+    def store(c):
+        return pltpu.make_async_copy(done.at[:, part(c)], out_ref.at[:, part(c)], store_sem.at[c])
+
+    whole = pltpu.make_async_copy(cycle_ref, local, local_sem.at[0])
+    own = pltpu.make_async_copy(cycle_ref.at[me], land.at[me], local_sem.at[1])
+    for c in (0, 1):
+        for k in (2, 1, 3):
+            send(c, k).start()
+    whole.start()
+    own.start()
+
+    whole.wait()
+
+    def average(c, carry):
+        rows = pl.ds(pl.multiple_of(c * 8 * KR, 8 * KR), 8 * KR)
+        total = LAYER_WEIGHTS[0] * local[0, rows]
+        for layer in (1, 2, 3):
+            total = total + LAYER_WEIGHTS[layer] * local[layer, rows]
+        mean[me, pl.ds(pl.multiple_of(c * 8, 8), 8)] = jnp.sum(total.reshape(8, KR, quarter), axis=1) / KR
+        return carry
+
+    lax.fori_loop(0, cells // 8, average, 0)
+    for k in (2, 1, 3):
+        send_mean(k).start()
+
+    tab[...] = rows_ref[...]
+    for at, turn in ((0, 0), (2, 1)):
+        sine, cosine = rows_ref[at : at + 1, :], rows_ref[at + 1 : at + 2, :]
+        tab[at : at + 1, :] = sine * turn_ref[3 + turn] - cosine * turn_ref[turn]
+        tab[at + 1 : at + 2, :] = cosine * turn_ref[3 + turn] + sine * turn_ref[turn]
+    cosine, sine = rows_ref[4:5, :], rows_ref[5:6, :]
+    tab[4:5, :] = cosine * turn_ref[5] + sine * turn_ref[2]
+    tab[5:6, :] = sine * turn_ref[5] - cosine * turn_ref[2]
+
+    def build(i, carry):
+        first = pl.multiple_of(i * 128, 128)
+        rows = pl.ds(first, 128)
+        values = matrix_values(length, first, 128, shift_ref[0], tab[...], cols_ref[rows, :])
+        for ref, value in zip(matrices, values):
+            ref[rows, :] = value
+        return carry
+
+    lax.fori_loop(0, quarter // 128, build, 0)
+    own.wait()
+
+    def step(c, carry):
+        for k in (2, 1, 3):
+            send(c, k).wait_recv()
+
+        @pl.when(c + 2 < chunks)
+        def _():
+            for k in (2, 1, 3):
+                send(c + 2, k).start()
+
+        values = filter_quarters([land[i, part(c)] for i in range(4)], tab, matrices)
+        for i, value in enumerate(values):
+            done[i, part(c)] = value
+        store(c).start()
+        return carry
+
+    lax.fori_loop(0, chunks, step, 0)
+
+    for k in (1, 2, 3):
+        send_mean(k).wait_recv()
+    for i, value in enumerate(filter_quarters([mean[i] for i in range(4)], tab, matrices)):
+        ghosts[i] = value
+    ghost_ref[...] = ghosts[me]
+
+    def finish(c, carry):
+        for k in (1, 2, 3):
+            send(c, k).wait_send()
+        store(c).wait()
+        return carry
+
+    lax.fori_loop(0, chunks, finish, 0)
+    for k in (1, 2, 3):
+        send_mean(k).wait_send()
+
+
+def forward(rows, shift, cells):
+    sectors, count, sector = rows.shape
+    length = sectors * sector
+    block = 80
+    chunks = count // block
+    f32, bf16 = jnp.float32, jnp.bfloat16
+    smem = pl.BlockSpec(memory_space=pltpu.SMEM)
+    vmem = pl.BlockSpec(memory_space=pltpu.VMEM)
+    hbm = pl.BlockSpec(memory_space=pl.ANY)
+    dma = pltpu.SemaphoreType.DMA
+    return pl.pallas_call(
+        lambda *refs: forward_body(length, block, cells, *refs),
+        out_shape=[jax.ShapeDtypeStruct(rows.shape, f32), jax.ShapeDtypeStruct((cells, sector), f32)],
+        in_specs=[smem, smem, vmem, vmem, hbm],
+        out_specs=[hbm, vmem],
+        scratch_shapes=[pltpu.VMEM(rows.shape, f32)] * 3
+        + [pltpu.VMEM((4, cells, sector), f32)] * 2
+        + [pltpu.VMEM((sector, sector), bf16)] * 4
+        + [pltpu.VMEM((8, sector), f32), dma((chunks, 3)), dma((chunks, 3)), dma((3,)), dma((3,)), dma((2,)), dma((chunks,))],
+        compiler_params=pltpu.CompilerParams(vmem_limit_bytes=52 * MIB, collective_id=0, has_side_effects=True),
+        cost_estimate=pl.CostEstimate(flops=24 * count * sector * sector, bytes_accessed=12 * count * length, transcendentals=0),
+        name="forward_filter",
+    )(turn_values(shift[0], length), shift, still_tables(length), source_tables(length), rows)
+
+
 def shifted(array, axis, dim, width):
     devices, length = (lax.axis_size(axis), array.shape[dim])
     up = [(i, (i + 1) % devices) for i in range(devices - 1)]
@@ -184,7 +353,7 @@
     return lax.ppermute(last, axis, up), lax.ppermute(leading, axis, down)
 
 
-def on_device(cycle, field, shift, owner):
+def chunked(cycle, shift):
     layers, variables, radial, sector = cycle.shape
     sectors = lax.axis_size("az")
     length = sectors * sector
@@ -211,12 +380,24 @@
     rest = across(rest)
 
     ghost = lax.dynamic_index_in_dim(passed(around), lax.axis_index("az"), 0, keepdims=False)
-    ghost = lax.all_gather(ghost.reshape(variables, cells, sector), "ax", axis=1, tiled=True)
 
     lead, rest = lax.optimization_barrier((passed(lead), rest))
     lead = across(lead).reshape(1, variables, radial, sector)
     rest = across(passed(rest)).reshape(layers - 1, variables, radial, sector)
     shifted_cycle = jnp.concatenate([lead, rest], axis=0)
+    return ghost, shifted_cycle
+
+
+def on_device(cycle, field, shift, owner):
+    layers, variables, radial, sector = cycle.shape
+    sectors = lax.axis_size("az")
+    cells = variables * (radial // KR)
+    if sectors == layers == 4 and (variables * radial) % 160 == 0 and cells % 8 == 0:
+        moved, ghost = forward(cycle.reshape(layers, variables * radial, sector), shift, cells)
+        shifted_cycle = lax.all_to_all(moved, "az", split_axis=0, concat_axis=0, tiled=True).reshape(cycle.shape)
+    else:
+        ghost, shifted_cycle = chunked(cycle, shift)
+    ghost = lax.all_gather(ghost.reshape(variables, radial // KR, sector), "ax", axis=1, tiled=True)
 
     mask = owner.astype(jnp.float32)[None, :, :, None]
     speeds = jnp.array(AXIAL_SPEEDS, jnp.float32)[:, None, None, None]

time: 284 us -> 268 us (0.944)
  Pallas kernels: 31.6 us -> 132 us
  waiting for transfers between devices: 95.1 us -> 41 us
  blocking collectives: 48.5 us -> 10.9 us
  starting transfers between devices: 65.9 us -> 53.4 us
  other arithmetic: 14.2 us -> 8.27 us
  local copies, waits for them, and re-layouts: 25.5 us -> 20.2 us
    pallas_call x4 -> x1, Pallas kernels: 31.6 us -> 132 us  [forward(): pl.pallas_call(lambda *refs: forward_body(length, block, cells, *refs), o...]
    all_to_all x4 -> x1, waiting for transfers between devices: 91 us -> 37 us  [on_device(): lax.all_to_all(moved, 'az', split_axis=0, concat_axis=0, tiled=True)]
    all_gather x2 -> x1, blocking collectives: 48.5 us -> 10.9 us  [on_device(): lax.all_gather(ghost.reshape(variables, radial // KR, sector), 'ax', axis...]
    all_to_all x4 -> x1, starting transfers between devices: 20.9 us -> 9.94 us  [on_device(): lax.all_to_all(moved, 'az', split_axis=0, concat_axis=0, tiled=True)]
    slice x2 -> x0, local copies, waits for them, and re-layouts: 7.25 us -> none  [the longest x1 4.73 us: on_device(): rest = cycle[1:].reshape(sectors, -1, sector)]
    concatenate x1, other arithmetic: 5.71 us -> 0.08 us  [turn_values(): return jnp.concatenate([jnp.sin(angle), jnp.cos(angle)])]
    unnamed x39 -> x20, local copies, waits for them, and re-layouts: 13.8 us -> 14 us
  transfers between devices with their start and end apart: 20 -> 17, of which waited for: 5 -> 4; matrix products, arithmetic and copies ran while one was open for 9% -> 8% of each run, Pallas kernels for 11% -> 0%
where the time goes in v3:
time: 268 us; the launch traced here: 267 us
  Pallas kernels  132 us (49%)
  starting transfers between devices  53.4 us (20%)
  waiting for transfers between devices  41 us (15%)
  local copies, waits for them, and re-layouts  20.2 us (8%)
  blocking collectives  10.9 us (4%)
  other arithmetic  8.27 us (3%)
    pallas_call x1, Pallas kernels, forward(): pl.pallas_call(lambda *refs: forward_body(length, block, cells, *refs), o...  132 us
    ppermute x16, starting transfers between devices, shifted(): return (lax.ppermute(last, axis, up), lax.ppermute(leading, axis, down))  43.5 us
    all_to_all x1, waiting for transfers between devices, on_device(): lax.all_to_all(moved, 'az', split_axis=0, concat_axis=0, tiled=True)  37 us
    unnamed x20, local copies, waits for them, and re-layouts  14 us
    all_gather x1, blocking collectives, on_device(): lax.all_gather(ghost.reshape(variables, radial // KR, sector), 'ax', axis...  10.9 us
    all_to_all x1, starting transfers between devices, on_device(): lax.all_to_all(moved, 'az', split_axis=0, concat_axis=0, tiled=True)  9.94 us
  transfers between devices with their start and end apart: 17, of which 4 were waited for; matrix products, arithmetic and copies ran while one was open for 8% of the time, Pallas kernels for 0%

profile of v3, /device:TPU:0, one launch (start us, length us, event | category | flops | bytes accessed | tf_op | source)
XLA Modules:
  0.0 267.1 jit_solution(2780515776006350669)
XLA Ops:
  1.3 0.7 fusion.3
  2.0 0.1 pad_maximum_fusion.16.refs_0_
  2.1 1.0 copy-done
  3.2 0.8 copy-done.1
  3.9 131.7 %forward_filter.1 = (f32[4,320,1024]{2,1,0:T(8,128)}, f32[40,1024]{1,0:T(8,128)S(1)}) custom-call(f32[6]{0:T(128)S(1)} %pad_maximum_fusion.16.refs_0_, s32[1]{0:T(128)} %copy.36.refs_1_, f32[8,1024]{1,0:T(8,128)S(1)} %copy-done.1, f32[1024,4]{1,0:T(8,128)S(1)} %copy-done, f32[4,320,1024]{2,1,0:T(8,128)} %bitcast.11), custom_call_target="tpu_custom_call" | custom-call | flops 8053063680 | bytes 15728640 | tf_op jit(solution)/shard_map/forward_filter/pallas_call | solution.py:332
  135.6 0.0 copy-start.2
  135.6 9.9 %all-to-all-start = ((f32[4,320,1024]{2,1,0:T(8,128)}), f32[4,320,1024]{2,1,0:T(8,128)}, u32[]{:S(2)}, u32[]{:S(2)}) async-start(f32[4,320,1024]{2,1,0:T(8,128)} %get-tuple-element.5), calls=%async_computation | async-start | bytes 10485760 | tf_op jit(solution)/shard_map/all_to_all | solution.py:397
  145.5 1.0 fusion.16
  146.5 0.1 copy.31
  146.7 2.1 collective-permute-start.3
  148.8 0.7 copy.13
  149.5 3.4 %collective-permute-start.1 = (f32[5,1,2,1024]{3,1,0,2:T(1,128)}, f32[5,1,2,1024]{3,1,0,2:T(1,128)S(1)}, u32[]{:S(2)}, u32[]{:S(2)}) collective-permute-start(f32[5,1,2,1024]{3,1,0,2:T(1,128)} %copy.13), channel_id=1, source_target_pairs={{0,4},{1,5},{2,6},{3,7},{8,12},{9,13},{10,14},{11,15},{16,20},{17,... | collective-permute-start | bytes 122888 | tf_op jit(solution)/shard_map/ppermute | solution.py:353
  152.9 0.7 copy.12
  153.5 1.3 collective-permute-start
  154.8 1.0 copy.30
  155.8 1.4 collective-permute-start.2
  157.2 2.3 fusion.14
  159.5 1.8 copy.33
  161.4 1.5 copy.32
  162.8 10.9 %all_gather.3 = f32[5,32,1024]{2,1,0:T(8,128)S(1)} all-gather(f32[5,8,1024]{2,1,0:T(8,128)S(1)} %bitcast.10), channel_id=1, replica_groups=mesh['az'=4,'rad'=2,'ax'=4] {'ax'}, dimensions={1}, use_global_device_ids=true | all-gather | bytes 819200 | tf_op jit(solution)/shard_map/all_gather | solution.py:400
  173.7 0.0 collective-permute-done.3
  173.7 0.1 bitcast_select_fusion.3
  173.8 0.0 collective-permute-done.1
  173.8 0.0 collective-permute-done
  173.8 0.0 collective-permute-done.2
  173.9 2.4 multiply_add_fusion.2
  176.3 0.1 fusion.13
  176.5 3.4 %collective-permute-start.7 = (f32[5,32,1,1024]{3,1,0,2:T(8,128)S(1)}, f32[5,32,1,1024]{3,1,0,2:T(8,128)S(1)}, u32[]{:S(2)}, u32[]{:S(2)}) collective-permute-start(f32[5,32,1,1024]{3,1,0,2:T(8,128)S(1)} %get-tuple-element.32), channel_id=1, source_target_pairs={{0,1},{1,2},{2,3},{4,5},{5,6},{6,7},{8,9},{9,10},{10,11},{12,13},{... | collective-permute-start | bytes 1966088 | tf_op jit(solution)/shard_map/ppermute | solution.py:353
  179.9 1.3 collective-permute-start.6
  181.2 0.1 fusion.12
  181.2 1.3 collective-permute-start.4
  182.5 4.7 %collective-permute-start.5 = (f32[5,1,2,1024]{3,1,0,2:T(1,128)S(1)}, f32[5,1,2,1024]{3,1,0,2:T(1,128)S(1)}, u32[]{:S(2)}, u32[]{:S(2)}) collective-permute-start(f32[5,1,2,1024]{3,1,0,2:T(1,128)S(1)} %get-tuple-element.31), channel_id=1, source_target_pairs={{0,4},{1,5},{2,6},{3,7},{8,12},{9,13},{10,14},{11,15},{16,20},{17,... | collective-permute-start | bytes 122888 | tf_op jit(solution)/shard_map/ppermute | solution.py:353
  187.3 0.3 fusion.11
  187.6 0.0 collective-permute-done.7
  187.6 0.1 bitcast_select_fusion.2
  187.7 0.0 collective-permute-done.4
  187.7 1.2 collective-permute-done.5
  188.9 1.5 multiply_add_fusion.1
  190.4 0.1 fusion.10
  190.5 5.2 %collective-permute-start.11 = (f32[5,32,1,1024]{3,1,0,2:T(8,128)S(1)}, f32[5,32,1,1024]{3,1,0,2:T(8,128)S(1)}, u32[]{:S(2)}, u32[]{:S(2)}) collective-permute-start(f32[5,32,1,1024]{3,1,0,2:T(8,128)S(1)} %get-tuple-element.26), channel_id=1, source_target_pairs={{0,1},{1,2},{2,3},{4,5},{5,6},{6,7},{8,9},{9,10},{10,11},{12,13},{... | collective-permute-start | bytes 1966088 | tf_op jit(solution)/shard_map/ppermute | solution.py:353
  195.7 1.3 collective-permute-start.10
  197.0 0.1 fusion.9
  197.1 1.3 collective-permute-start.8
  198.4 4.5 %collective-permute-start.9 = (f32[5,1,2,1024]{3,1,0,2:T(1,128)S(1)}, f32[5,1,2,1024]{3,1,0,2:T(1,128)S(1)}, u32[]{:S(2)}, u32[]{:S(2)}) collective-permute-start(f32[5,1,2,1024]{3,1,0,2:T(1,128)S(1)} %get-tuple-element.25), channel_id=1, source_target_pairs={{0,4},{1,5},{2,6},{3,7},{8,12},{9,13},{10,14},{11,15},{16,20},{17,... | collective-permute-start | bytes 122888 | tf_op jit(solution)/shard_map/ppermute | solution.py:353
  202.9 0.3 fusion.8
  203.2 0.0 collective-permute-done.11
  203.3 0.1 bitcast_select_fusion.1
  203.4 1.4 collective-permute-done.9
  204.8 1.4 copy_add_fusion
  206.2 0.1 fusion.7
  206.3 5.2 %collective-permute-start.15 = (f32[5,32,1,1024]{3,1,0,2:T(8,128)S(1)}, f32[5,32,1,1024]{3,1,0,2:T(8,128)S(1)}, u32[]{:S(2)}, u32[]{:S(2)}) collective-permute-start(f32[5,32,1,1024]{3,1,0,2:T(8,128)S(1)} %get-tuple-element.20), channel_id=1, source_target_pairs={{0,1},{1,2},{2,3},{4,5},{5,6},{6,7},{8,9},{9,10},{10,11},{12,13},{... | collective-permute-start | bytes 1966088 | tf_op jit(solution)/shard_map/ppermute | solution.py:353
  211.5 1.3 collective-permute-start.14
  212.8 0.1 fusion.6
  212.9 1.3 collective-permute-start.12
  214.2 4.5 %collective-permute-start.13 = (f32[5,1,2,1024]{3,1,0,2:T(1,128)S(1)}, f32[5,1,2,1024]{3,1,0,2:T(1,128)S(1)}, u32[]{:S(2)}, u32[]{:S(2)}) collective-permute-start(f32[5,1,2,1024]{3,1,0,2:T(1,128)S(1)} %get-tuple-element.19), channel_id=1, source_target_pairs={{0,4},{1,5},{2,6},{3,7},{8,12},{9,13},{10,14},{11,15},{16,20},{17,... | collective-permute-start | bytes 122888 | tf_op jit(solution)/shard_map/ppermute | solution.py:353
  218.7 0.3 fusion.5
  219.1 0.0 collective-permute-done.15
  219.1 0.1 bitcast_select_fusion
  219.2 1.4 collective-permute-done.13
  220.6 0.0 collective-permute-done.14
  220.6 1.8 multiply_add_fusion
  222.4 2.1 copy.22
  224.4 37.0 %all-to-all-done = f32[4,320,1024]{2,1,0:T(8,128)} async-done(((f32[4,320,1024]{2,1,0:T(8,128)}), f32[4,320,1024]{2,1,0:T(8,128)}, u32[]{:S(2)}, u32[]{:S(2)}) %all-to-all-start) | async-done | bytes 5242912 | tf_op jit(solution)/shard_map/all_to_all | solution.py:397
  261.4 5.7 %copy.37 = f32[4,5,64,1024]{3,2,1,0:T(8,128)} copy(f32[4,5,64,1024]{3,2,1,0:T(8,128)} %bitcast.4) | data formatting | bytes 10485760
  (18 shorter events, 0.1 us)
Async XLA Ops:
  2.1 1.0 copy-start
  3.2 0.8 copy-start.1
  135.6 10.0 %copy-start.2 = (f32[5,32,2,1024]{3,2,1,0:T(2,128)S(1)}, f32[5,32,2,1024]{3,2,1,0:T(2,128)}, u32[]{:S(2)}) copy-start(f32[5,32,2,1024]{3,2,1,0:T(2,128)} %param.9) | copy-start | bytes 3932164
  135.6 125.8 %all-to-all-start = ((f32[4,320,1024]{2,1,0:T(8,128)}), f32[4,320,1024]{2,1,0:T(8,128)}, u32[]{:S(2)}, u32[]{:S(2)}) async-start(f32[4,320,1024]{2,1,0:T(8,128)} %get-tuple-element.5), calls=%async_computation | async-start | bytes 10485760 | tf_op jit(solution)/shard_map/all_to_all | solution.py:397
  146.7 27.0 %collective-permute-start.3 = (f32[5,32,1,1024]{3,1,0,2:T(8,128)S(1)}, f32[5,32,1,1024]{3,1,0,2:T(8,128)}, u32[]{:S(2)}, u32[]{:S(2)}) collective-permute-start(f32[5,32,1,1024]{3,1,0,2:T(8,128)S(1)} %copy.31), channel_id=1, source_target_pairs={{0,1},{1,2},{2,3},{4,5},{5,6},{6,7},{8,9},{9,10},{10,11},{12,13},{... | collective-permute-start | bytes 1966088 | tf_op jit(solution)/shard_map/ppermute | solution.py:353
  149.5 24.3 %collective-permute-start.1 = (f32[5,1,2,1024]{3,1,0,2:T(1,128)}, f32[5,1,2,1024]{3,1,0,2:T(1,128)S(1)}, u32[]{:S(2)}, u32[]{:S(2)}) collective-permute-start(f32[5,1,2,1024]{3,1,0,2:T(1,128)} %copy.13), channel_id=1, source_target_pairs={{0,4},{1,5},{2,6},{3,7},{8,12},{9,13},{10,14},{11,15},{16,20},{17,... | collective-permute-start | bytes 122888 | tf_op jit(solution)/shard_map/ppermute | solution.py:353
  153.5 20.3 %collective-permute-start = (f32[5,1,2,1024]{3,1,0,2:T(1,128)}, f32[5,1,2,1024]{3,1,0,2:T(1,128)S(1)}, u32[]{:S(2)}, u32[]{:S(2)}) collective-permute-start(f32[5,1,2,1024]{3,1,0,2:T(1,128)} %copy.12), channel_id=1, source_target_pairs={{4,0},{5,1},{6,2},{7,3},{12,8},{13,9},{14,10},{15,11},{20,16},{21,... | collective-permute-start | bytes 122888 | tf_op jit(solution)/shard_map/ppermute | solution.py:353
  155.8 3.7 %copy-start.6 = (s32[32,2]{0,1:T(2,128)S(1)}, s32[32,2]{0,1:T(2,128)}, u32[]{:S(2)}) copy-start(s32[32,2]{0,1:T(2,128)} %param.11) | copy-start | bytes 772
  155.8 18.1 %collective-permute-start.2 = (f32[5,32,1,1024]{3,1,0,2:T(8,128)}, f32[5,32,1,1024]{3,1,0,2:T(8,128)}, u32[]{:S(2)}, u32[]{:S(2)}) collective-permute-start(f32[5,32,1,1024]{3,1,0,2:T(8,128)} %copy.30), channel_id=1, source_target_pairs={{1,0},{2,1},{3,2},{5,4},{6,5},{7,6},{9,8},{10,9},{11,10},{13,12},{... | collective-permute-start | bytes 1966088 | tf_op jit(solution)/shard_map/ppermute | solution.py:353
  159.5 1.8 copy-start.4
  162.8 11.0 %copy-start.3 = (f32[5,31,2,1024]{3,1,0,2:T(8,128)S(1)}, f32[5,31,2,1024]{3,1,0,2:T(8,128)}, u32[]{:S(2)}) copy-start(f32[5,31,2,1024]{3,1,0,2:T(8,128)} %copy.32) | copy-start | bytes 3809284
  162.8 11.0 %copy-start.5 = (f32[5]{0:T(128)S(1)}, f32[5]{0:T(128)}, u32[]{:S(2)}) copy-start(f32[5]{0:T(128)} %constant.50) | copy-start | bytes 64
  176.5 11.1 %collective-permute-start.7 = (f32[5,32,1,1024]{3,1,0,2:T(8,128)S(1)}, f32[5,32,1,1024]{3,1,0,2:T(8,128)S(1)}, u32[]{:S(2)}, u32[]{:S(2)}) collective-permute-start(f32[5,32,1,1024]{3,1,0,2:T(8,128)S(1)} %get-tuple-element.32), channel_id=1, source_target_pairs={{0,1},{1,2},{2,3},{4,5},{5,6},{6,7},{8,9},{9,10},{10,11},{12,13},{... | collective-permute-start | bytes 1966088 | tf_op jit(solution)/shard_map/ppermute | solution.py:353
  179.9 9.0 %collective-permute-start.6 = (f32[5,32,1,1024]{3,1,0,2:T(8,128)S(1)}, f32[5,32,1,1024]{3,1,0,2:T(8,128)S(1)}, u32[]{:S(2)}, u32[]{:S(2)}) collective-permute-start(f32[5,32,1,1024]{3,1,0,2:T(8,128)S(1)} %get-tuple-element.33), channel_id=1, source_target_pairs={{1,0},{2,1},{3,2},{5,4},{6,5},{7,6},{9,8},{10,9},{11,10},{13,12},{... | collective-permute-start | bytes 1966088 | tf_op jit(solution)/shard_map/ppermute | solution.py:353
  181.2 6.5 %collective-permute-start.4 = (f32[5,1,2,1024]{3,1,0,2:T(1,128)S(1)}, f32[5,1,2,1024]{3,1,0,2:T(1,128)S(1)}, u32[]{:S(2)}, u32[]{:S(2)}) collective-permute-start(f32[5,1,2,1024]{3,1,0,2:T(1,128)S(1)} %get-tuple-element.30), channel_id=1, source_target_pairs={{4,0},{5,1},{6,2},{7,3},{12,8},{13,9},{14,10},{15,11},{20,16},{21,... | collective-permute-start | bytes 122888 | tf_op jit(solution)/shard_map/ppermute | solution.py:353
  182.5 6.4 %collective-permute-start.5 = (f32[5,1,2,1024]{3,1,0,2:T(1,128)S(1)}, f32[5,1,2,1024]{3,1,0,2:T(1,128)S(1)}, u32[]{:S(2)}, u32[]{:S(2)}) collective-permute-start(f32[5,1,2,1024]{3,1,0,2:T(1,128)S(1)} %get-tuple-element.31), channel_id=1, source_target_pairs={{0,4},{1,5},{2,6},{3,7},{8,12},{9,13},{10,14},{11,15},{16,20},{17,... | collective-permute-start | bytes 122888 | tf_op jit(solution)/shard_map/ppermute | solution.py:353
  190.5 12.7 %collective-permute-start.11 = (f32[5,32,1,1024]{3,1,0,2:T(8,128)S(1)}, f32[5,32,1,1024]{3,1,0,2:T(8,128)S(1)}, u32[]{:S(2)}, u32[]{:S(2)}) collective-permute-start(f32[5,32,1,1024]{3,1,0,2:T(8,128)S(1)} %get-tuple-element.26), channel_id=1, source_target_pairs={{0,1},{1,2},{2,3},{4,5},{5,6},{6,7},{8,9},{9,10},{10,11},{12,13},{... | collective-permute-start | bytes 1966088 | tf_op jit(solution)/shard_map/ppermute | solution.py:353
  195.7 9.1 %collective-permute-start.10 = (f32[5,32,1,1024]{3,1,0,2:T(8,128)S(1)}, f32[5,32,1,1024]{3,1,0,2:T(8,128)S(1)}, u32[]{:S(2)}, u32[]{:S(2)}) collective-permute-start(f32[5,32,1,1024]{3,1,0,2:T(8,128)S(1)} %get-tuple-element.27), channel_id=1, source_target_pairs={{1,0},{2,1},{3,2},{5,4},{6,5},{7,6},{9,8},{10,9},{11,10},{13,12},{... | collective-permute-start | bytes 1966088 | tf_op jit(solution)/shard_map/ppermute | solution.py:353
  197.1 6.3 %collective-permute-start.8 = (f32[5,1,2,1024]{3,1,0,2:T(1,128)S(1)}, f32[5,1,2,1024]{3,1,0,2:T(1,128)S(1)}, u32[]{:S(2)}, u32[]{:S(2)}) collective-permute-start(f32[5,1,2,1024]{3,1,0,2:T(1,128)S(1)} %get-tuple-element.24), channel_id=1, source_target_pairs={{4,0},{5,1},{6,2},{7,3},{12,8},{13,9},{14,10},{15,11},{20,16},{21,... | collective-permute-start | bytes 122888 | tf_op jit(solution)/shard_map/ppermute | solution.py:353
  198.4 6.4 %collective-permute-start.9 = (f32[5,1,2,1024]{3,1,0,2:T(1,128)S(1)}, f32[5,1,2,1024]{3,1,0,2:T(1,128)S(1)}, u32[]{:S(2)}, u32[]{:S(2)}) collective-permute-start(f32[5,1,2,1024]{3,1,0,2:T(1,128)S(1)} %get-tuple-element.25), channel_id=1, source_target_pairs={{0,4},{1,5},{2,6},{3,7},{8,12},{9,13},{10,14},{11,15},{16,20},{17,... | collective-permute-start | bytes 122888 | tf_op jit(solution)/shard_map/ppermute | solution.py:353
  206.3 12.7 %collective-permute-start.15 = (f32[5,32,1,1024]{3,1,0,2:T(8,128)S(1)}, f32[5,32,1,1024]{3,1,0,2:T(8,128)S(1)}, u32[]{:S(2)}, u32[]{:S(2)}) collective-permute-start(f32[5,32,1,1024]{3,1,0,2:T(8,128)S(1)} %get-tuple-element.20), channel_id=1, source_target_pairs={{0,1},{1,2},{2,3},{4,5},{5,6},{6,7},{8,9},{9,10},{10,11},{12,13},{... | collective-permute-start | bytes 1966088 | tf_op jit(solution)/shard_map/ppermute | solution.py:353
  211.5 9.1 %collective-permute-start.14 = (f32[5,32,1,1024]{3,1,0,2:T(8,128)S(1)}, f32[5,32,1,1024]{3,1,0,2:T(8,128)S(1)}, u32[]{:S(2)}, u32[]{:S(2)}) collective-permute-start(f32[5,32,1,1024]{3,1,0,2:T(8,128)S(1)} %get-tuple-element.21), channel_id=1, source_target_pairs={{1,0},{2,1},{3,2},{5,4},{6,5},{7,6},{9,8},{10,9},{11,10},{13,12},{... | collective-permute-start | bytes 1966088 | tf_op jit(solution)/shard_map/ppermute | solution.py:353
  212.9 6.3 %collective-permute-start.12 = (f32[5,1,2,1024]{3,1,0,2:T(1,128)S(1)}, f32[5,1,2,1024]{3,1,0,2:T(1,128)S(1)}, u32[]{:S(2)}, u32[]{:S(2)}) collective-permute-start(f32[5,1,2,1024]{3,1,0,2:T(1,128)S(1)} %get-tuple-element.18), channel_id=1, source_target_pairs={{4,0},{5,1},{6,2},{7,3},{12,8},{13,9},{14,10},{15,11},{20,16},{21,... | collective-permute-start | bytes 122888 | tf_op jit(solution)/shard_map/ppermute | solution.py:353
  214.2 6.4 %collective-permute-start.13 = (f32[5,1,2,1024]{3,1,0,2:T(1,128)S(1)}, f32[5,1,2,1024]{3,1,0,2:T(1,128)S(1)}, u32[]{:S(2)}, u32[]{:S(2)}) collective-permute-start(f32[5,1,2,1024]{3,1,0,2:T(1,128)S(1)} %get-tuple-element.19), channel_id=1, source_target_pairs={{0,4},{1,5},{2,6},{3,7},{8,12},{9,13},{10,14},{11,15},{16,20},{17,... | collective-permute-start | bytes 122888 | tf_op jit(solution)/shard_map/ppermute | solution.py:353

commit v4 on v3

--- a/solution.py
+++ b/solution.py
@@ -245,9 +245,8 @@
 
     whole = pltpu.make_async_copy(cycle_ref, local, local_sem.at[0])
     own = pltpu.make_async_copy(cycle_ref.at[me], land.at[me], local_sem.at[1])
-    for c in (0, 1):
-        for k in (2, 1, 3):
-            send(c, k).start()
+    for k in (2, 1, 3):
+        send(0, k).start()
     whole.start()
     own.start()
 
@@ -264,6 +263,8 @@
     lax.fori_loop(0, cells // 8, average, 0)
     for k in (2, 1, 3):
         send_mean(k).start()
+    for k in (2, 1, 3):
+        send(1, k).start()
 
     tab[...] = rows_ref[...]
     for at, turn in ((0, 0), (2, 1)):
@@ -286,6 +287,14 @@
     own.wait()
 
     def step(c, carry):
+        @pl.when(c == chunks - 1)
+        def _():
+            for k in (1, 2, 3):
+                send_mean(k).wait_recv()
+            for i, value in enumerate(filter_quarters([mean[i] for i in range(4)], tab, matrices)):
+                ghosts[i] = value
+            ghost_ref[...] = ghosts[me]
+
         for k in (2, 1, 3):
             send(c, k).wait_recv()
 
@@ -302,12 +311,6 @@
 
     lax.fori_loop(0, chunks, step, 0)
 
-    for k in (1, 2, 3):
-        send_mean(k).wait_recv()
-    for i, value in enumerate(filter_quarters([mean[i] for i in range(4)], tab, matrices)):
-        ghosts[i] = value
-    ghost_ref[...] = ghosts[me]
-
     def finish(c, carry):
         for k in (1, 2, 3):
             send(c, k).wait_send()
@@ -322,7 +325,7 @@
 def forward(rows, shift, cells):
     sectors, count, sector = rows.shape
     length = sectors * sector
-    block = 80
+    block = 64
     chunks = count // block
     f32, bf16 = jnp.float32, jnp.bfloat16
     smem = pl.BlockSpec(memory_space=pltpu.SMEM)
@@ -392,9 +395,9 @@
     layers, variables, radial, sector = cycle.shape
     sectors = lax.axis_size("az")
     cells = variables * (radial // KR)
-    if sectors == layers == 4 and (variables * radial) % 160 == 0 and cells % 8 == 0:
+    if sectors == layers == 4 and variables * radial % 64 == 0 and variables * radial >= 128 and cells % 8 == 0:
         moved, ghost = forward(cycle.reshape(layers, variables * radial, sector), shift, cells)
-        shifted_cycle = lax.all_to_all(moved, "az", split_axis=0, concat_axis=0, tiled=True).reshape(cycle.shape)
+        shifted_cycle = lax.all_to_all(moved.reshape(cycle.shape), "az", split_axis=0, concat_axis=0, tiled=True)
     else:
         ghost, shifted_cycle = chunked(cycle, shift)
     ghost = lax.all_gather(ghost.reshape(variables, radial // KR, sector), "ax", axis=1, tiled=True)

time: 268 us -> 267 us (level)
  no operation moved by 1% of the time
where the time goes in v4:
time: 267 us; the launch traced here: 266 us
  Pallas kernels  132 us (49%)
  starting transfers between devices  52.1 us (20%)
  waiting for transfers between devices  41 us (15%)
  local copies, waits for them, and re-layouts  20.2 us (8%)
  blocking collectives  10.9 us (4%)
  other arithmetic  8.27 us (3%)
    pallas_call x1, Pallas kernels, forward(): pl.pallas_call(lambda *refs: forward_body(length, block, cells, *refs), o...  132 us
    ppermute x16, starting transfers between devices, shifted(): return (lax.ppermute(last, axis, up), lax.ppermute(leading, axis, down))  43.5 us
    all_to_all x1, waiting for transfers between devices, on_device(): lax.all_to_all(moved.reshape(cycle.shape), 'az', split_axis=0, concat_axi...  37 us
    unnamed x20, local copies, waits for them, and re-layouts  14 us
    all_gather x1, blocking collectives, on_device(): lax.all_gather(ghost.reshape(variables, radial // KR, sector), 'ax', axis...  10.9 us
    all_to_all x1, starting transfers between devices, on_device(): lax.all_to_all(moved.reshape(cycle.shape), 'az', split_axis=0, concat_axi...  8.58 us
  transfers between devices with their start and end apart: 17, of which 4 were waited for; matrix products, arithmetic and copies ran while one was open for 8% of the time, Pallas kernels for 0%

profile of v4, /device:TPU:0, one launch (start us, length us, event | category | flops | bytes accessed | tf_op | source)
XLA Modules:
  0.0 265.7 jit_solution(10678003096729539767)
XLA Ops:
  1.3 0.7 fusion.3
  2.0 0.1 pad_maximum_fusion.16.refs_0_
  2.1 1.0 copy-done
  3.2 0.8 copy-done.1
  3.9 131.6 %forward_filter.1 = (f32[4,320,1024]{2,1,0:T(8,128)}, f32[40,1024]{1,0:T(8,128)S(1)}) custom-call(f32[6]{0:T(128)S(1)} %pad_maximum_fusion.16.refs_0_, s32[1]{0:T(128)} %copy.36.refs_1_, f32[8,1024]{1,0:T(8,128)S(1)} %copy-done.1, f32[1024,4]{1,0:T(8,128)S(1)} %copy-done, f32[4,320,1024]{2,1,0:T(8,128)} %bitcast.12), custom_call_target="tpu_custom_call" | custom-call | flops 8053063680 | bytes 15728640 | tf_op jit(solution)/shard_map/forward_filter/pallas_call | solution.py:335
  135.5 0.0 copy-start.2
  135.5 8.6 %all-to-all-start = ((f32[4,5,64,1024]{3,2,1,0:T(8,128)}), f32[4,5,64,1024]{3,2,1,0:T(8,128)}, u32[]{:S(2)}, u32[]{:S(2)}) async-start(f32[4,5,64,1024]{3,2,1,0:T(8,128)} %bitcast.11), calls=%async_computation | async-start | bytes 10485760 | tf_op jit(solution)/shard_map/all_to_all | solution.py:400
  144.1 1.0 fusion.16
  145.1 0.1 copy.31
  145.2 2.1 collective-permute-start.3
  147.4 0.7 copy.13
  148.1 3.4 %collective-permute-start.1 = (f32[5,1,2,1024]{3,1,0,2:T(1,128)}, f32[5,1,2,1024]{3,1,0,2:T(1,128)S(1)}, u32[]{:S(2)}, u32[]{:S(2)}) collective-permute-start(f32[5,1,2,1024]{3,1,0,2:T(1,128)} %copy.13), channel_id=1, source_target_pairs={{0,4},{1,5},{2,6},{3,7},{8,12},{9,13},{10,14},{11,15},{16,20},{17,... | collective-permute-start | bytes 122888 | tf_op jit(solution)/shard_map/ppermute | solution.py:356
  151.4 0.7 copy.12
  152.1 1.3 collective-permute-start
  153.4 1.0 copy.30
  154.4 1.4 collective-permute-start.2
  155.8 2.3 fusion.14
  158.1 1.8 copy.33
  159.9 1.5 copy.32
  161.4 10.9 %all_gather.3 = f32[5,32,1024]{2,1,0:T(8,128)S(1)} all-gather(f32[5,8,1024]{2,1,0:T(8,128)S(1)} %bitcast.10), channel_id=1, replica_groups=mesh['az'=4,'rad'=2,'ax'=4] {'ax'}, dimensions={1}, use_global_device_ids=true | all-gather | bytes 819200 | tf_op jit(solution)/shard_map/all_gather | solution.py:403
  172.3 0.0 collective-permute-done.3
  172.3 0.1 bitcast_select_fusion.3
  172.4 0.0 collective-permute-done.1
  172.4 0.0 collective-permute-done
  172.4 0.0 collective-permute-done.2
  172.5 2.4 multiply_add_fusion.2
  174.9 0.1 fusion.13
  175.1 3.4 %collective-permute-start.7 = (f32[5,32,1,1024]{3,1,0,2:T(8,128)S(1)}, f32[5,32,1,1024]{3,1,0,2:T(8,128)S(1)}, u32[]{:S(2)}, u32[]{:S(2)}) collective-permute-start(f32[5,32,1,1024]{3,1,0,2:T(8,128)S(1)} %get-tuple-element.32), channel_id=1, source_target_pairs={{0,1},{1,2},{2,3},{4,5},{5,6},{6,7},{8,9},{9,10},{10,11},{12,13},{... | collective-permute-start | bytes 1966088 | tf_op jit(solution)/shard_map/ppermute | solution.py:356
  178.4 1.3 collective-permute-start.6
  179.7 0.1 fusion.12
  179.8 1.3 collective-permute-start.4
  181.1 4.7 %collective-permute-start.5 = (f32[5,1,2,1024]{3,1,0,2:T(1,128)S(1)}, f32[5,1,2,1024]{3,1,0,2:T(1,128)S(1)}, u32[]{:S(2)}, u32[]{:S(2)}) collective-permute-start(f32[5,1,2,1024]{3,1,0,2:T(1,128)S(1)} %get-tuple-element.31), channel_id=1, source_target_pairs={{0,4},{1,5},{2,6},{3,7},{8,12},{9,13},{10,14},{11,15},{16,20},{17,... | collective-permute-start | bytes 122888 | tf_op jit(solution)/shard_map/ppermute | solution.py:356
  185.8 0.3 fusion.11
  186.2 0.1 bitcast_select_fusion.2
  186.3 0.0 collective-permute-done.4
  186.3 1.2 collective-permute-done.5
  187.5 0.0 collective-permute-done.6
  187.5 1.5 multiply_add_fusion.1
  188.9 0.1 fusion.10
  189.1 5.2 %collective-permute-start.11 = (f32[5,32,1,1024]{3,1,0,2:T(8,128)S(1)}, f32[5,32,1,1024]{3,1,0,2:T(8,128)S(1)}, u32[]{:S(2)}, u32[]{:S(2)}) collective-permute-start(f32[5,32,1,1024]{3,1,0,2:T(8,128)S(1)} %get-tuple-element.26), channel_id=1, source_target_pairs={{0,1},{1,2},{2,3},{4,5},{5,6},{6,7},{8,9},{9,10},{10,11},{12,13},{... | collective-permute-start | bytes 1966088 | tf_op jit(solution)/shard_map/ppermute | solution.py:356
  194.3 1.3 collective-permute-start.10
  195.6 0.1 fusion.9
  195.6 1.3 collective-permute-start.8
  196.9 4.5 %collective-permute-start.9 = (f32[5,1,2,1024]{3,1,0,2:T(1,128)S(1)}, f32[5,1,2,1024]{3,1,0,2:T(1,128)S(1)}, u32[]{:S(2)}, u32[]{:S(2)}) collective-permute-start(f32[5,1,2,1024]{3,1,0,2:T(1,128)S(1)} %get-tuple-element.25), channel_id=1, source_target_pairs={{0,4},{1,5},{2,6},{3,7},{8,12},{9,13},{10,14},{11,15},{16,20},{17,... | collective-permute-start | bytes 122888 | tf_op jit(solution)/shard_map/ppermute | solution.py:356
  201.5 0.3 fusion.8
  201.8 0.1 bitcast_select_fusion.1
  201.9 0.0 collective-permute-done.8
  201.9 1.4 collective-permute-done.9
  203.3 0.0 collective-permute-done.10
  203.3 1.4 copy_add_fusion
  204.8 0.1 fusion.7
  204.9 5.2 %collective-permute-start.15 = (f32[5,32,1,1024]{3,1,0,2:T(8,128)S(1)}, f32[5,32,1,1024]{3,1,0,2:T(8,128)S(1)}, u32[]{:S(2)}, u32[]{:S(2)}) collective-permute-start(f32[5,32,1,1024]{3,1,0,2:T(8,128)S(1)} %get-tuple-element.20), channel_id=1, source_target_pairs={{0,1},{1,2},{2,3},{4,5},{5,6},{6,7},{8,9},{9,10},{10,11},{12,13},{... | collective-permute-start | bytes 1966088 | tf_op jit(solution)/shard_map/ppermute | solution.py:356
  210.1 1.3 collective-permute-start.14
  211.4 0.1 fusion.6
  211.5 1.3 collective-permute-start.12
  212.8 4.5 %collective-permute-start.13 = (f32[5,1,2,1024]{3,1,0,2:T(1,128)S(1)}, f32[5,1,2,1024]{3,1,0,2:T(1,128)S(1)}, u32[]{:S(2)}, u32[]{:S(2)}) collective-permute-start(f32[5,1,2,1024]{3,1,0,2:T(1,128)S(1)} %get-tuple-element.19), channel_id=1, source_target_pairs={{0,4},{1,5},{2,6},{3,7},{8,12},{9,13},{10,14},{11,15},{16,20},{17,... | collective-permute-start | bytes 122888 | tf_op jit(solution)/shard_map/ppermute | solution.py:356
  217.3 0.3 fusion.5
  217.6 0.1 bitcast_select_fusion
  217.7 0.0 collective-permute-done.12
  217.8 1.4 collective-permute-done.13
  219.2 1.8 multiply_add_fusion
  221.0 2.1 copy.22
  223.0 37.0 %all-to-all-done = f32[4,5,64,1024]{3,2,1,0:T(8,128)} async-done(((f32[4,5,64,1024]{3,2,1,0:T(8,128)}), f32[4,5,64,1024]{3,2,1,0:T(8,128)}, u32[]{:S(2)}, u32[]{:S(2)}) %all-to-all-start) | async-done | bytes 5242912 | tf_op jit(solution)/shard_map/all_to_all | solution.py:400
  260.0 5.7 %copy.37 = f32[4,5,64,1024]{3,2,1,0:T(8,128)} copy(f32[4,5,64,1024]{3,2,1,0:T(8,128)} %all-to-all-done) | data formatting | bytes 10485760
  (18 shorter events, 0.1 us)
Async XLA Ops:
  2.1 1.0 copy-start
  3.2 0.8 copy-start.1
  135.5 8.6 %copy-start.2 = (f32[5,32,2,1024]{3,2,1,0:T(2,128)S(1)}, f32[5,32,2,1024]{3,2,1,0:T(2,128)}, u32[]{:S(2)}) copy-start(f32[5,32,2,1024]{3,2,1,0:T(2,128)} %param.9) | copy-start | bytes 3932164
  135.5 124.5 %all-to-all-start = ((f32[4,5,64,1024]{3,2,1,0:T(8,128)}), f32[4,5,64,1024]{3,2,1,0:T(8,128)}, u32[]{:S(2)}, u32[]{:S(2)}) async-start(f32[4,5,64,1024]{3,2,1,0:T(8,128)} %bitcast.11), calls=%async_computation | async-start | bytes 10485760 | tf_op jit(solution)/shard_map/all_to_all | solution.py:400
  145.2 27.1 %collective-permute-start.3 = (f32[5,32,1,1024]{3,1,0,2:T(8,128)S(1)}, f32[5,32,1,1024]{3,1,0,2:T(8,128)}, u32[]{:S(2)}, u32[]{:S(2)}) collective-permute-start(f32[5,32,1,1024]{3,1,0,2:T(8,128)S(1)} %copy.31), channel_id=1, source_target_pairs={{0,1},{1,2},{2,3},{4,5},{5,6},{6,7},{8,9},{9,10},{10,11},{12,13},{... | collective-permute-start | bytes 1966088 | tf_op jit(solution)/shard_map/ppermute | solution.py:356
  148.1 24.4 %collective-permute-start.1 = (f32[5,1,2,1024]{3,1,0,2:T(1,128)}, f32[5,1,2,1024]{3,1,0,2:T(1,128)S(1)}, u32[]{:S(2)}, u32[]{:S(2)}) collective-permute-start(f32[5,1,2,1024]{3,1,0,2:T(1,128)} %copy.13), channel_id=1, source_target_pairs={{0,4},{1,5},{2,6},{3,7},{8,12},{9,13},{10,14},{11,15},{16,20},{17,... | collective-permute-start | bytes 122888 | tf_op jit(solution)/shard_map/ppermute | solution.py:356
  152.1 20.3 %collective-permute-start = (f32[5,1,2,1024]{3,1,0,2:T(1,128)}, f32[5,1,2,1024]{3,1,0,2:T(1,128)S(1)}, u32[]{:S(2)}, u32[]{:S(2)}) collective-permute-start(f32[5,1,2,1024]{3,1,0,2:T(1,128)} %copy.12), channel_id=1, source_target_pairs={{4,0},{5,1},{6,2},{7,3},{12,8},{13,9},{14,10},{15,11},{20,16},{21,... | collective-permute-start | bytes 122888 | tf_op jit(solution)/shard_map/ppermute | solution.py:356
  154.4 3.7 %copy-start.6 = (s32[32,2]{0,1:T(2,128)S(1)}, s32[32,2]{0,1:T(2,128)}, u32[]{:S(2)}) copy-start(s32[32,2]{0,1:T(2,128)} %param.11) | copy-start | bytes 772
  154.4 18.1 %collective-permute-start.2 = (f32[5,32,1,1024]{3,1,0,2:T(8,128)}, f32[5,32,1,1024]{3,1,0,2:T(8,128)}, u32[]{:S(2)}, u32[]{:S(2)}) collective-permute-start(f32[5,32,1,1024]{3,1,0,2:T(8,128)} %copy.30), channel_id=1, source_target_pairs={{1,0},{2,1},{3,2},{5,4},{6,5},{7,6},{9,8},{10,9},{11,10},{13,12},{... | collective-permute-start | bytes 1966088 | tf_op jit(solution)/shard_map/ppermute | solution.py:356
  158.1 1.8 copy-start.4
  161.4 11.0 %copy-start.3 = (f32[5,31,2,1024]{3,1,0,2:T(8,128)S(1)}, f32[5,31,2,1024]{3,1,0,2:T(8,128)}, u32[]{:S(2)}) copy-start(f32[5,31,2,1024]{3,1,0,2:T(8,128)} %copy.32) | copy-start | bytes 3809284
  161.4 11.0 %copy-start.5 = (f32[5]{0:T(128)S(1)}, f32[5]{0:T(128)}, u32[]{:S(2)}) copy-start(f32[5]{0:T(128)} %constant.50) | copy-start | bytes 64
  175.1 11.1 %collective-permute-start.7 = (f32[5,32,1,1024]{3,1,0,2:T(8,128)S(1)}, f32[5,32,1,1024]{3,1,0,2:T(8,128)S(1)}, u32[]{:S(2)}, u32[]{:S(2)}) collective-permute-start(f32[5,32,1,1024]{3,1,0,2:T(8,128)S(1)} %get-tuple-element.32), channel_id=1, source_target_pairs={{0,1},{1,2},{2,3},{4,5},{5,6},{6,7},{8,9},{9,10},{10,11},{12,13},{... | collective-permute-start | bytes 1966088 | tf_op jit(solution)/shard_map/ppermute | solution.py:356
  178.4 9.0 %collective-permute-start.6 = (f32[5,32,1,1024]{3,1,0,2:T(8,128)S(1)}, f32[5,32,1,1024]{3,1,0,2:T(8,128)S(1)}, u32[]{:S(2)}, u32[]{:S(2)}) collective-permute-start(f32[5,32,1,1024]{3,1,0,2:T(8,128)S(1)} %get-tuple-element.33), channel_id=1, source_target_pairs={{1,0},{2,1},{3,2},{5,4},{6,5},{7,6},{9,8},{10,9},{11,10},{13,12},{... | collective-permute-start | bytes 1966088 | tf_op jit(solution)/shard_map/ppermute | solution.py:356
  179.8 6.5 %collective-permute-start.4 = (f32[5,1,2,1024]{3,1,0,2:T(1,128)S(1)}, f32[5,1,2,1024]{3,1,0,2:T(1,128)S(1)}, u32[]{:S(2)}, u32[]{:S(2)}) collective-permute-start(f32[5,1,2,1024]{3,1,0,2:T(1,128)S(1)} %get-tuple-element.30), channel_id=1, source_target_pairs={{4,0},{5,1},{6,2},{7,3},{12,8},{13,9},{14,10},{15,11},{20,16},{21,... | collective-permute-start | bytes 122888 | tf_op jit(solution)/shard_map/ppermute | solution.py:356
  181.1 6.4 %collective-permute-start.5 = (f32[5,1,2,1024]{3,1,0,2:T(1,128)S(1)}, f32[5,1,2,1024]{3,1,0,2:T(1,128)S(1)}, u32[]{:S(2)}, u32[]{:S(2)}) collective-permute-start(f32[5,1,2,1024]{3,1,0,2:T(1,128)S(1)} %get-tuple-element.31), channel_id=1, source_target_pairs={{0,4},{1,5},{2,6},{3,7},{8,12},{9,13},{10,14},{11,15},{16,20},{17,... | collective-permute-start | bytes 122888 | tf_op jit(solution)/shard_map/ppermute | solution.py:356
  189.1 12.7 %collective-permute-start.11 = (f32[5,32,1,1024]{3,1,0,2:T(8,128)S(1)}, f32[5,32,1,1024]{3,1,0,2:T(8,128)S(1)}, u32[]{:S(2)}, u32[]{:S(2)}) collective-permute-start(f32[5,32,1,1024]{3,1,0,2:T(8,128)S(1)} %get-tuple-element.26), channel_id=1, source_target_pairs={{0,1},{1,2},{2,3},{4,5},{5,6},{6,7},{8,9},{9,10},{10,11},{12,13},{... | collective-permute-start | bytes 1966088 | tf_op jit(solution)/shard_map/ppermute | solution.py:356
  194.3 9.1 %collective-permute-start.10 = (f32[5,32,1,1024]{3,1,0,2:T(8,128)S(1)}, f32[5,32,1,1024]{3,1,0,2:T(8,128)S(1)}, u32[]{:S(2)}, u32[]{:S(2)}) collective-permute-start(f32[5,32,1,1024]{3,1,0,2:T(8,128)S(1)} %get-tuple-element.27), channel_id=1, source_target_pairs={{1,0},{2,1},{3,2},{5,4},{6,5},{7,6},{9,8},{10,9},{11,10},{13,12},{... | collective-permute-start | bytes 1966088 | tf_op jit(solution)/shard_map/ppermute | solution.py:356
  195.6 6.3 %collective-permute-start.8 = (f32[5,1,2,1024]{3,1,0,2:T(1,128)S(1)}, f32[5,1,2,1024]{3,1,0,2:T(1,128)S(1)}, u32[]{:S(2)}, u32[]{:S(2)}) collective-permute-start(f32[5,1,2,1024]{3,1,0,2:T(1,128)S(1)} %get-tuple-element.24), channel_id=1, source_target_pairs={{4,0},{5,1},{6,2},{7,3},{12,8},{13,9},{14,10},{15,11},{20,16},{21,... | collective-permute-start | bytes 122888 | tf_op jit(solution)/shard_map/ppermute | solution.py:356
  196.9 6.4 %collective-permute-start.9 = (f32[5,1,2,1024]{3,1,0,2:T(1,128)S(1)}, f32[5,1,2,1024]{3,1,0,2:T(1,128)S(1)}, u32[]{:S(2)}, u32[]{:S(2)}) collective-permute-start(f32[5,1,2,1024]{3,1,0,2:T(1,128)S(1)} %get-tuple-element.25), channel_id=1, source_target_pairs={{0,4},{1,5},{2,6},{3,7},{8,12},{9,13},{10,14},{11,15},{16,20},{17,... | collective-permute-start | bytes 122888 | tf_op jit(solution)/shard_map/ppermute | solution.py:356
  204.9 12.7 %collective-permute-start.15 = (f32[5,32,1,1024]{3,1,0,2:T(8,128)S(1)}, f32[5,32,1,1024]{3,1,0,2:T(8,128)S(1)}, u32[]{:S(2)}, u32[]{:S(2)}) collective-permute-start(f32[5,32,1,1024]{3,1,0,2:T(8,128)S(1)} %get-tuple-element.20), channel_id=1, source_target_pairs={{0,1},{1,2},{2,3},{4,5},{5,6},{6,7},{8,9},{9,10},{10,11},{12,13},{... | collective-permute-start | bytes 1966088 | tf_op jit(solution)/shard_map/ppermute | solution.py:356
  210.1 9.1 %collective-permute-start.14 = (f32[5,32,1,1024]{3,1,0,2:T(8,128)S(1)}, f32[5,32,1,1024]{3,1,0,2:T(8,128)S(1)}, u32[]{:S(2)}, u32[]{:S(2)}) collective-permute-start(f32[5,32,1,1024]{3,1,0,2:T(8,128)S(1)} %get-tuple-element.21), channel_id=1, source_target_pairs={{1,0},{2,1},{3,2},{5,4},{6,5},{7,6},{9,8},{10,9},{11,10},{13,12},{... | collective-permute-start | bytes 1966088 | tf_op jit(solution)/shard_map/ppermute | solution.py:356
  211.5 6.3 %collective-permute-start.12 = (f32[5,1,2,1024]{3,1,0,2:T(1,128)S(1)}, f32[5,1,2,1024]{3,1,0,2:T(1,128)S(1)}, u32[]{:S(2)}, u32[]{:S(2)}) collective-permute-start(f32[5,1,2,1024]{3,1,0,2:T(1,128)S(1)} %get-tuple-element.18), channel_id=1, source_target_pairs={{4,0},{5,1},{6,2},{7,3},{12,8},{13,9},{14,10},{15,11},{20,16},{21,... | collective-permute-start | bytes 122888 | tf_op jit(solution)/shard_map/ppermute | solution.py:356
  212.8 6.4 %collective-permute-start.13 = (f32[5,1,2,1024]{3,1,0,2:T(1,128)S(1)}, f32[5,1,2,1024]{3,1,0,2:T(1,128)S(1)}, u32[]{:S(2)}, u32[]{:S(2)}) collective-permute-start(f32[5,1,2,1024]{3,1,0,2:T(1,128)S(1)} %get-tuple-element.19), channel_id=1, source_target_pairs={{0,4},{1,5},{2,6},{3,7},{8,12},{9,13},{10,14},{11,15},{16,20},{17,... | collective-permute-start | bytes 122888 | tf_op jit(solution)/shard_map/ppermute | solution.py:356

commit v5 on v4

--- a/solution.py
+++ b/solution.py
@@ -285,6 +285,8 @@
 
     lax.fori_loop(0, quarter // 128, build, 0)
     own.wait()
+    for k in (2, 1, 3):
+        send(2, k).start()
 
     def step(c, carry):
         @pl.when(c == chunks - 1)
@@ -298,10 +300,10 @@
         for k in (2, 1, 3):
             send(c, k).wait_recv()
 
-        @pl.when(c + 2 < chunks)
+        @pl.when(c + 3 < chunks)
         def _():
             for k in (2, 1, 3):
-                send(c + 2, k).start()
+                send(c + 3, k).start()
 
         values = filter_quarters([land[i, part(c)] for i in range(4)], tab, matrices)
         for i, value in enumerate(values):
@@ -395,7 +397,7 @@
     layers, variables, radial, sector = cycle.shape
     sectors = lax.axis_size("az")
     cells = variables * (radial // KR)
-    if sectors == layers == 4 and variables * radial % 64 == 0 and variables * radial >= 128 and cells % 8 == 0:
+    if sectors == layers == 4 and variables * radial % 64 == 0 and variables * radial >= 192 and cells % 8 == 0:
         moved, ghost = forward(cycle.reshape(layers, variables * radial, sector), shift, cells)
         shifted_cycle = lax.all_to_all(moved.reshape(cycle.shape), "az", split_axis=0, concat_axis=0, tiled=True)
     else:

time: 267 us -> 266 us (level)
  no operation moved by 1% of the time
where the time goes in v5:
time: 266 us
  Pallas kernels  132 us (50%)
  starting transfers between devices  52.1 us (20%)
  waiting for transfers between devices  41 us (15%)
  local copies, waits for them, and re-layouts  20.2 us (8%)
  blocking collectives  10.9 us (4%)
  other arithmetic  8.27 us (3%)
    pallas_call x1, Pallas kernels, forward(): pl.pallas_call(lambda *refs: forward_body(length, block, cells, *refs), o...  132 us
    ppermute x16, starting transfers between devices, shifted(): return (lax.ppermute(last, axis, up), lax.ppermute(leading, axis, down))  43.5 us
    all_to_all x1, waiting for transfers between devices, on_device(): lax.all_to_all(moved.reshape(cycle.shape), 'az', split_axis=0, concat_axi...  37 us
    unnamed x20, local copies, waits for them, and re-layouts  14 us
    all_gather x1, blocking collectives, on_device(): lax.all_gather(ghost.reshape(variables, radial // KR, sector), 'ax', axis...  10.9 us
    all_to_all x1, starting transfers between devices, on_device(): lax.all_to_all(moved.reshape(cycle.shape), 'az', split_axis=0, concat_axi...  8.54 us
  transfers between devices with their start and end apart: 17, of which 4 were waited for; matrix products, arithmetic and copies ran while one was open for 8% of the time, Pallas kernels for 0%

profile of v5, /device:TPU:0, one launch (start us, length us, event | category | flops | bytes accessed | tf_op | source)
XLA Modules:
  0.0 265.6 jit_solution(12587254521849757913)
XLA Ops:
  1.3 0.7 fusion.3
  2.0 0.1 pad_maximum_fusion.16.refs_0_
  2.1 1.0 copy-done
  3.2 0.8 copy-done.1
  3.9 131.6 %forward_filter.1 = (f32[4,320,1024]{2,1,0:T(8,128)}, f32[40,1024]{1,0:T(8,128)S(1)}) custom-call(f32[6]{0:T(128)S(1)} %pad_maximum_fusion.16.refs_0_, s32[1]{0:T(128)} %copy.36.refs_1_, f32[8,1024]{1,0:T(8,128)S(1)} %copy-done.1, f32[1024,4]{1,0:T(8,128)S(1)} %copy-done, f32[4,320,1024]{2,1,0:T(8,128)} %bitcast.12), custom_call_target="tpu_custom_call" | custom-call | flops 8053063680 | bytes 15728640 | tf_op jit(solution)/shard_map/forward_filter/pallas_call | solution.py:337
  135.5 0.0 copy-start.2
  135.5 8.5 %all-to-all-start = ((f32[4,5,64,1024]{3,2,1,0:T(8,128)}), f32[4,5,64,1024]{3,2,1,0:T(8,128)}, u32[]{:S(2)}, u32[]{:S(2)}) async-start(f32[4,5,64,1024]{3,2,1,0:T(8,128)} %bitcast.11), calls=%async_computation | async-start | bytes 10485760 | tf_op jit(solution)/shard_map/all_to_all | solution.py:402
  144.1 1.0 fusion.16
  145.1 0.1 copy.31
  145.2 2.1 collective-permute-start.3
  147.3 0.7 copy.13
  148.0 3.4 %collective-permute-start.1 = (f32[5,1,2,1024]{3,1,0,2:T(1,128)}, f32[5,1,2,1024]{3,1,0,2:T(1,128)S(1)}, u32[]{:S(2)}, u32[]{:S(2)}) collective-permute-start(f32[5,1,2,1024]{3,1,0,2:T(1,128)} %copy.13), channel_id=1, source_target_pairs={{0,4},{1,5},{2,6},{3,7},{8,12},{9,13},{10,14},{11,15},{16,20},{17,... | collective-permute-start | bytes 122888 | tf_op jit(solution)/shard_map/ppermute | solution.py:358
  151.4 0.7 copy.12
  152.1 1.3 collective-permute-start
  153.3 1.0 copy.30
  154.3 1.4 collective-permute-start.2
  155.7 2.3 fusion.14
  158.1 1.8 copy.33
  159.9 1.5 copy.32
  161.4 10.9 %all_gather.3 = f32[5,32,1024]{2,1,0:T(8,128)S(1)} all-gather(f32[5,8,1024]{2,1,0:T(8,128)S(1)} %bitcast.10), channel_id=1, replica_groups=mesh['az'=4,'rad'=2,'ax'=4] {'ax'}, dimensions={1}, use_global_device_ids=true | all-gather | bytes 819200 | tf_op jit(solution)/shard_map/all_gather | solution.py:405
  172.3 0.1 bitcast_select_fusion.3
  172.4 0.0 collective-permute-done
  172.4 0.0 collective-permute-done.2
  172.4 2.4 multiply_add_fusion.2
  174.9 0.1 fusion.13
  175.0 3.4 %collective-permute-start.7 = (f32[5,32,1,1024]{3,1,0,2:T(8,128)S(1)}, f32[5,32,1,1024]{3,1,0,2:T(8,128)S(1)}, u32[]{:S(2)}, u32[]{:S(2)}) collective-permute-start(f32[5,32,1,1024]{3,1,0,2:T(8,128)S(1)} %get-tuple-element.32), channel_id=1, source_target_pairs={{0,1},{1,2},{2,3},{4,5},{5,6},{6,7},{8,9},{9,10},{10,11},{12,13},{... | collective-permute-start | bytes 1966088 | tf_op jit(solution)/shard_map/ppermute | solution.py:358
  178.4 1.3 collective-permute-start.6
  179.7 0.1 fusion.12
  179.8 1.3 collective-permute-start.4
  181.1 4.7 %collective-permute-start.5 = (f32[5,1,2,1024]{3,1,0,2:T(1,128)S(1)}, f32[5,1,2,1024]{3,1,0,2:T(1,128)S(1)}, u32[]{:S(2)}, u32[]{:S(2)}) collective-permute-start(f32[5,1,2,1024]{3,1,0,2:T(1,128)S(1)} %get-tuple-element.31), channel_id=1, source_target_pairs={{0,4},{1,5},{2,6},{3,7},{8,12},{9,13},{10,14},{11,15},{16,20},{17,... | collective-permute-start | bytes 122888 | tf_op jit(solution)/shard_map/ppermute | solution.py:358
  185.8 0.3 fusion.11
  186.1 0.0 collective-permute-done.7
  186.1 0.1 bitcast_select_fusion.2
  186.2 0.0 collective-permute-done.4
  186.2 1.2 collective-permute-done.5
  187.4 0.0 collective-permute-done.6
  187.4 1.5 multiply_add_fusion.1
  188.9 0.1 fusion.10
  189.0 5.2 %collective-permute-start.11 = (f32[5,32,1,1024]{3,1,0,2:T(8,128)S(1)}, f32[5,32,1,1024]{3,1,0,2:T(8,128)S(1)}, u32[]{:S(2)}, u32[]{:S(2)}) collective-permute-start(f32[5,32,1,1024]{3,1,0,2:T(8,128)S(1)} %get-tuple-element.26), channel_id=1, source_target_pairs={{0,1},{1,2},{2,3},{4,5},{5,6},{6,7},{8,9},{9,10},{10,11},{12,13},{... | collective-permute-start | bytes 1966088 | tf_op jit(solution)/shard_map/ppermute | solution.py:358
  194.2 1.3 collective-permute-start.10
  195.5 0.1 fusion.9
  195.6 1.3 collective-permute-start.8
  196.9 4.5 %collective-permute-start.9 = (f32[5,1,2,1024]{3,1,0,2:T(1,128)S(1)}, f32[5,1,2,1024]{3,1,0,2:T(1,128)S(1)}, u32[]{:S(2)}, u32[]{:S(2)}) collective-permute-start(f32[5,1,2,1024]{3,1,0,2:T(1,128)S(1)} %get-tuple-element.25), channel_id=1, source_target_pairs={{0,4},{1,5},{2,6},{3,7},{8,12},{9,13},{10,14},{11,15},{16,20},{17,... | collective-permute-start | bytes 122888 | tf_op jit(solution)/shard_map/ppermute | solution.py:358
  201.5 0.3 fusion.8
  201.8 0.0 collective-permute-done.11
  201.8 0.1 bitcast_select_fusion.1
  201.9 0.0 collective-permute-done.8
  201.9 1.4 collective-permute-done.9
  203.3 0.0 collective-permute-done.10
  203.3 1.4 copy_add_fusion
  204.7 0.1 fusion.7
  204.9 5.2 %collective-permute-start.15 = (f32[5,32,1,1024]{3,1,0,2:T(8,128)S(1)}, f32[5,32,1,1024]{3,1,0,2:T(8,128)S(1)}, u32[]{:S(2)}, u32[]{:S(2)}) collective-permute-start(f32[5,32,1,1024]{3,1,0,2:T(8,128)S(1)} %get-tuple-element.20), channel_id=1, source_target_pairs={{0,1},{1,2},{2,3},{4,5},{5,6},{6,7},{8,9},{9,10},{10,11},{12,13},{... | collective-permute-start | bytes 1966088 | tf_op jit(solution)/shard_map/ppermute | solution.py:358
  210.0 1.3 collective-permute-start.14
  211.3 0.1 fusion.6
  211.4 1.3 collective-permute-start.12
  212.7 4.5 %collective-permute-start.13 = (f32[5,1,2,1024]{3,1,0,2:T(1,128)S(1)}, f32[5,1,2,1024]{3,1,0,2:T(1,128)S(1)}, u32[]{:S(2)}, u32[]{:S(2)}) collective-permute-start(f32[5,1,2,1024]{3,1,0,2:T(1,128)S(1)} %get-tuple-element.19), channel_id=1, source_target_pairs={{0,4},{1,5},{2,6},{3,7},{8,12},{9,13},{10,14},{11,15},{16,20},{17,... | collective-permute-start | bytes 122888 | tf_op jit(solution)/shard_map/ppermute | solution.py:358
  217.3 0.3 fusion.5
  217.6 0.1 bitcast_select_fusion
  217.7 0.0 collective-permute-done.12
  217.7 1.4 collective-permute-done.13
  219.1 1.8 multiply_add_fusion
  220.9 2.1 copy.22
  223.0 37.0 %all-to-all-done = f32[4,5,64,1024]{3,2,1,0:T(8,128)} async-done(((f32[4,5,64,1024]{3,2,1,0:T(8,128)}), f32[4,5,64,1024]{3,2,1,0:T(8,128)}, u32[]{:S(2)}, u32[]{:S(2)}) %all-to-all-start) | async-done | bytes 5242912 | tf_op jit(solution)/shard_map/all_to_all | solution.py:402
  259.9 5.7 %copy.37 = f32[4,5,64,1024]{3,2,1,0:T(8,128)} copy(f32[4,5,64,1024]{3,2,1,0:T(8,128)} %all-to-all-done) | data formatting | bytes 10485760
  (18 shorter events, 0.1 us)
Async XLA Ops:
  2.1 1.0 copy-start
  3.2 0.8 copy-start.1
  135.5 8.6 %copy-start.2 = (f32[5,32,2,1024]{3,2,1,0:T(2,128)S(1)}, f32[5,32,2,1024]{3,2,1,0:T(2,128)}, u32[]{:S(2)}) copy-start(f32[5,32,2,1024]{3,2,1,0:T(2,128)} %param.9) | copy-start | bytes 3932164
  135.5 124.4 %all-to-all-start = ((f32[4,5,64,1024]{3,2,1,0:T(8,128)}), f32[4,5,64,1024]{3,2,1,0:T(8,128)}, u32[]{:S(2)}, u32[]{:S(2)}) async-start(f32[4,5,64,1024]{3,2,1,0:T(8,128)} %bitcast.11), calls=%async_computation | async-start | bytes 10485760 | tf_op jit(solution)/shard_map/all_to_all | solution.py:402
  145.2 27.0 %collective-permute-start.3 = (f32[5,32,1,1024]{3,1,0,2:T(8,128)S(1)}, f32[5,32,1,1024]{3,1,0,2:T(8,128)}, u32[]{:S(2)}, u32[]{:S(2)}) collective-permute-start(f32[5,32,1,1024]{3,1,0,2:T(8,128)S(1)} %copy.31), channel_id=1, source_target_pairs={{0,1},{1,2},{2,3},{4,5},{5,6},{6,7},{8,9},{9,10},{10,11},{12,13},{... | collective-permute-start | bytes 1966088 | tf_op jit(solution)/shard_map/ppermute | solution.py:358
  148.0 24.3 %collective-permute-start.1 = (f32[5,1,2,1024]{3,1,0,2:T(1,128)}, f32[5,1,2,1024]{3,1,0,2:T(1,128)S(1)}, u32[]{:S(2)}, u32[]{:S(2)}) collective-permute-start(f32[5,1,2,1024]{3,1,0,2:T(1,128)} %copy.13), channel_id=1, source_target_pairs={{0,4},{1,5},{2,6},{3,7},{8,12},{9,13},{10,14},{11,15},{16,20},{17,... | collective-permute-start | bytes 122888 | tf_op jit(solution)/shard_map/ppermute | solution.py:358
  152.1 20.3 %collective-permute-start = (f32[5,1,2,1024]{3,1,0,2:T(1,128)}, f32[5,1,2,1024]{3,1,0,2:T(1,128)S(1)}, u32[]{:S(2)}, u32[]{:S(2)}) collective-permute-start(f32[5,1,2,1024]{3,1,0,2:T(1,128)} %copy.12), channel_id=1, source_target_pairs={{4,0},{5,1},{6,2},{7,3},{12,8},{13,9},{14,10},{15,11},{20,16},{21,... | collective-permute-start | bytes 122888 | tf_op jit(solution)/shard_map/ppermute | solution.py:358
  154.3 3.7 %copy-start.6 = (s32[32,2]{0,1:T(2,128)S(1)}, s32[32,2]{0,1:T(2,128)}, u32[]{:S(2)}) copy-start(s32[32,2]{0,1:T(2,128)} %param.11) | copy-start | bytes 772
  154.3 18.1 %collective-permute-start.2 = (f32[5,32,1,1024]{3,1,0,2:T(8,128)}, f32[5,32,1,1024]{3,1,0,2:T(8,128)}, u32[]{:S(2)}, u32[]{:S(2)}) collective-permute-start(f32[5,32,1,1024]{3,1,0,2:T(8,128)} %copy.30), channel_id=1, source_target_pairs={{1,0},{2,1},{3,2},{5,4},{6,5},{7,6},{9,8},{10,9},{11,10},{13,12},{... | collective-permute-start | bytes 1966088 | tf_op jit(solution)/shard_map/ppermute | solution.py:358
  158.0 1.8 copy-start.4
  161.4 11.0 %copy-start.3 = (f32[5,31,2,1024]{3,1,0,2:T(8,128)S(1)}, f32[5,31,2,1024]{3,1,0,2:T(8,128)}, u32[]{:S(2)}) copy-start(f32[5,31,2,1024]{3,1,0,2:T(8,128)} %copy.32) | copy-start | bytes 3809284
  161.4 11.0 %copy-start.5 = (f32[5]{0:T(128)S(1)}, f32[5]{0:T(128)}, u32[]{:S(2)}) copy-start(f32[5]{0:T(128)} %constant.50) | copy-start | bytes 64
  175.0 11.1 %collective-permute-start.7 = (f32[5,32,1,1024]{3,1,0,2:T(8,128)S(1)}, f32[5,32,1,1024]{3,1,0,2:T(8,128)S(1)}, u32[]{:S(2)}, u32[]{:S(2)}) collective-permute-start(f32[5,32,1,1024]{3,1,0,2:T(8,128)S(1)} %get-tuple-element.32), channel_id=1, source_target_pairs={{0,1},{1,2},{2,3},{4,5},{5,6},{6,7},{8,9},{9,10},{10,11},{12,13},{... | collective-permute-start | bytes 1966088 | tf_op jit(solution)/shard_map/ppermute | solution.py:358
  178.4 9.0 %collective-permute-start.6 = (f32[5,32,1,1024]{3,1,0,2:T(8,128)S(1)}, f32[5,32,1,1024]{3,1,0,2:T(8,128)S(1)}, u32[]{:S(2)}, u32[]{:S(2)}) collective-permute-start(f32[5,32,1,1024]{3,1,0,2:T(8,128)S(1)} %get-tuple-element.33), channel_id=1, source_target_pairs={{1,0},{2,1},{3,2},{5,4},{6,5},{7,6},{9,8},{10,9},{11,10},{13,12},{... | collective-permute-start | bytes 1966088 | tf_op jit(solution)/shard_map/ppermute | solution.py:358
  179.8 6.5 %collective-permute-start.4 = (f32[5,1,2,1024]{3,1,0,2:T(1,128)S(1)}, f32[5,1,2,1024]{3,1,0,2:T(1,128)S(1)}, u32[]{:S(2)}, u32[]{:S(2)}) collective-permute-start(f32[5,1,2,1024]{3,1,0,2:T(1,128)S(1)} %get-tuple-element.30), channel_id=1, source_target_pairs={{4,0},{5,1},{6,2},{7,3},{12,8},{13,9},{14,10},{15,11},{20,16},{21,... | collective-permute-start | bytes 122888 | tf_op jit(solution)/shard_map/ppermute | solution.py:358
  181.1 6.4 %collective-permute-start.5 = (f32[5,1,2,1024]{3,1,0,2:T(1,128)S(1)}, f32[5,1,2,1024]{3,1,0,2:T(1,128)S(1)}, u32[]{:S(2)}, u32[]{:S(2)}) collective-permute-start(f32[5,1,2,1024]{3,1,0,2:T(1,128)S(1)} %get-tuple-element.31), channel_id=1, source_target_pairs={{0,4},{1,5},{2,6},{3,7},{8,12},{9,13},{10,14},{11,15},{16,20},{17,... | collective-permute-start | bytes 122888 | tf_op jit(solution)/shard_map/ppermute | solution.py:358
  189.0 12.7 %collective-permute-start.11 = (f32[5,32,1,1024]{3,1,0,2:T(8,128)S(1)}, f32[5,32,1,1024]{3,1,0,2:T(8,128)S(1)}, u32[]{:S(2)}, u32[]{:S(2)}) collective-permute-start(f32[5,32,1,1024]{3,1,0,2:T(8,128)S(1)} %get-tuple-element.26), channel_id=1, source_target_pairs={{0,1},{1,2},{2,3},{4,5},{5,6},{6,7},{8,9},{9,10},{10,11},{12,13},{... | collective-permute-start | bytes 1966088 | tf_op jit(solution)/shard_map/ppermute | solution.py:358
  194.2 9.1 %collective-permute-start.10 = (f32[5,32,1,1024]{3,1,0,2:T(8,128)S(1)}, f32[5,32,1,1024]{3,1,0,2:T(8,128)S(1)}, u32[]{:S(2)}, u32[]{:S(2)}) collective-permute-start(f32[5,32,1,1024]{3,1,0,2:T(8,128)S(1)} %get-tuple-element.27), channel_id=1, source_target_pairs={{1,0},{2,1},{3,2},{5,4},{6,5},{7,6},{9,8},{10,9},{11,10},{13,12},{... | collective-permute-start | bytes 1966088 | tf_op jit(solution)/shard_map/ppermute | solution.py:358
  195.6 6.3 %collective-permute-start.8 = (f32[5,1,2,1024]{3,1,0,2:T(1,128)S(1)}, f32[5,1,2,1024]{3,1,0,2:T(1,128)S(1)}, u32[]{:S(2)}, u32[]{:S(2)}) collective-permute-start(f32[5,1,2,1024]{3,1,0,2:T(1,128)S(1)} %get-tuple-element.24), channel_id=1, source_target_pairs={{4,0},{5,1},{6,2},{7,3},{12,8},{13,9},{14,10},{15,11},{20,16},{21,... | collective-permute-start | bytes 122888 | tf_op jit(solution)/shard_map/ppermute | solution.py:358
  196.9 6.4 %collective-permute-start.9 = (f32[5,1,2,1024]{3,1,0,2:T(1,128)S(1)}, f32[5,1,2,1024]{3,1,0,2:T(1,128)S(1)}, u32[]{:S(2)}, u32[]{:S(2)}) collective-permute-start(f32[5,1,2,1024]{3,1,0,2:T(1,128)S(1)} %get-tuple-element.25), channel_id=1, source_target_pairs={{0,4},{1,5},{2,6},{3,7},{8,12},{9,13},{10,14},{11,15},{16,20},{17,... | collective-permute-start | bytes 122888 | tf_op jit(solution)/shard_map/ppermute | solution.py:358
  204.9 12.7 %collective-permute-start.15 = (f32[5,32,1,1024]{3,1,0,2:T(8,128)S(1)}, f32[5,32,1,1024]{3,1,0,2:T(8,128)S(1)}, u32[]{:S(2)}, u32[]{:S(2)}) collective-permute-start(f32[5,32,1,1024]{3,1,0,2:T(8,128)S(1)} %get-tuple-element.20), channel_id=1, source_target_pairs={{0,1},{1,2},{2,3},{4,5},{5,6},{6,7},{8,9},{9,10},{10,11},{12,13},{... | collective-permute-start | bytes 1966088 | tf_op jit(solution)/shard_map/ppermute | solution.py:358
  210.0 9.1 %collective-permute-start.14 = (f32[5,32,1,1024]{3,1,0,2:T(8,128)S(1)}, f32[5,32,1,1024]{3,1,0,2:T(8,128)S(1)}, u32[]{:S(2)}, u32[]{:S(2)}) collective-permute-start(f32[5,32,1,1024]{3,1,0,2:T(8,128)S(1)} %get-tuple-element.21), channel_id=1, source_target_pairs={{1,0},{2,1},{3,2},{5,4},{6,5},{7,6},{9,8},{10,9},{11,10},{13,12},{... | collective-permute-start | bytes 1966088 | tf_op jit(solution)/shard_map/ppermute | solution.py:358
  211.4 6.3 %collective-permute-start.12 = (f32[5,1,2,1024]{3,1,0,2:T(1,128)S(1)}, f32[5,1,2,1024]{3,1,0,2:T(1,128)S(1)}, u32[]{:S(2)}, u32[]{:S(2)}) collective-permute-start(f32[5,1,2,1024]{3,1,0,2:T(1,128)S(1)} %get-tuple-element.18), channel_id=1, source_target_pairs={{4,0},{5,1},{6,2},{7,3},{12,8},{13,9},{14,10},{15,11},{20,16},{21,... | collective-permute-start | bytes 122888 | tf_op jit(solution)/shard_map/ppermute | solution.py:358
  212.7 6.4 %collective-permute-start.13 = (f32[5,1,2,1024]{3,1,0,2:T(1,128)S(1)}, f32[5,1,2,1024]{3,1,0,2:T(1,128)S(1)}, u32[]{:S(2)}, u32[]{:S(2)}) collective-permute-start(f32[5,1,2,1024]{3,1,0,2:T(1,128)S(1)} %get-tuple-element.19), channel_id=1, source_target_pairs={{0,4},{1,5},{2,6},{3,7},{8,12},{9,13},{10,14},{11,15},{16,20},{17,... | collective-permute-start | bytes 122888 | tf_op jit(solution)/shard_map/ppermute | solution.py:358

commit v6 on v4

--- a/solution.py
+++ b/solution.py
@@ -216,11 +216,14 @@
         pl.semaphore_signal(barrier, inc=1, device_id={"az": lax.rem(me + k, 4)}, device_id_type=pl.DeviceIdType.MESH)
     pl.semaphore_wait(barrier, 3)
 
+    def partner(k):
+        return (None, me + 1 - 2 * lax.rem(me, 2), lax.rem(me + 2, 4), 3 - me)[k]
+
     def part(c):
         return pl.ds(pl.multiple_of(c * block, block), block)
 
     def send(c, k):
-        peer = lax.rem(me + k, 4)
+        peer = partner(k)
         return pltpu.make_async_remote_copy(
             src_ref=cycle_ref.at[peer, part(c)],
             dst_ref=land.at[me, part(c)],
@@ -236,7 +239,7 @@
             dst_ref=mean.at[me],
             send_sem=mean_send.at[k - 1],
             recv_sem=mean_recv.at[k - 1],
-            device_id={"az": lax.rem(me + k, 4)},
+            device_id={"az": partner(k)},
             device_id_type=pl.DeviceIdType.MESH,
         )
 
@@ -245,7 +248,7 @@
 
     whole = pltpu.make_async_copy(cycle_ref, local, local_sem.at[0])
     own = pltpu.make_async_copy(cycle_ref.at[me], land.at[me], local_sem.at[1])
-    for k in (2, 1, 3):
+    for k in (2, 3, 1):
         send(0, k).start()
     whole.start()
     own.start()
@@ -261,9 +264,9 @@
         return carry
 
     lax.fori_loop(0, cells // 8, average, 0)
-    for k in (2, 1, 3):
+    for k in (2, 3, 1):
         send_mean(k).start()
-    for k in (2, 1, 3):
+    for k in (2, 3, 1):
         send(1, k).start()
 
     tab[...] = rows_ref[...]
@@ -295,12 +298,12 @@
                 ghosts[i] = value
             ghost_ref[...] = ghosts[me]
 
-        for k in (2, 1, 3):
+        for k in (2, 3, 1):
             send(c, k).wait_recv()
 
         @pl.when(c + 2 < chunks)
         def _():
-            for k in (2, 1, 3):
+            for k in (2, 3, 1):
                 send(c + 2, k).start()
 
         values = filter_quarters([land[i, part(c)] for i in range(4)], tab, matrices)

time: 267 us -> 266 us (level)
  no operation moved by 1% of the time
where the time goes in v6:
time: 266 us
  Pallas kernels  132 us (50%)
  starting transfers between devices  52 us (20%)
  waiting for transfers between devices  41 us (15%)
  local copies, waits for them, and re-layouts  20.2 us (8%)
  blocking collectives  10.9 us (4%)
  other arithmetic  8.27 us (3%)
    pallas_call x1, Pallas kernels, forward(): pl.pallas_call(lambda *refs: forward_body(length, block, cells, *refs), o...  132 us
    ppermute x16, starting transfers between devices, shifted(): return (lax.ppermute(last, axis, up), lax.ppermute(leading, axis, down))  43.5 us
    all_to_all x1, waiting for transfers between devices, on_device(): lax.all_to_all(moved.reshape(cycle.shape), 'az', split_axis=0, concat_axi...  37 us
    unnamed x20, local copies, waits for them, and re-layouts  14 us
    all_gather x1, blocking collectives, on_device(): lax.all_gather(ghost.reshape(variables, radial // KR, sector), 'ax', axis...  10.9 us
    all_to_all x1, starting transfers between devices, on_device(): lax.all_to_all(moved.reshape(cycle.shape), 'az', split_axis=0, concat_axi...  8.54 us
  transfers between devices with their start and end apart: 17, of which 4 were waited for; matrix products, arithmetic and copies ran while one was open for 8% of the time, Pallas kernels for 0%

profile of v6, /device:TPU:0, one launch (start us, length us, event | category | flops | bytes accessed | tf_op | source)
XLA Modules:
  0.0 265.6 jit_solution(7005540670441398618)
XLA Ops:
  1.3 0.7 fusion.3
  2.0 0.1 pad_maximum_fusion.16.refs_0_
  2.1 1.0 copy-done
  3.2 0.8 copy-done.1
  3.9 131.6 %forward_filter.1 = (f32[4,320,1024]{2,1,0:T(8,128)}, f32[40,1024]{1,0:T(8,128)S(1)}) custom-call(f32[6]{0:T(128)S(1)} %pad_maximum_fusion.16.refs_0_, s32[1]{0:T(128)} %copy.36.refs_1_, f32[8,1024]{1,0:T(8,128)S(1)} %copy-done.1, f32[1024,4]{1,0:T(8,128)S(1)} %copy-done, f32[4,320,1024]{2,1,0:T(8,128)} %bitcast.12), custom_call_target="tpu_custom_call" | custom-call | flops 8053063680 | bytes 15728640 | tf_op jit(solution)/shard_map/forward_filter/pallas_call | solution.py:338
  135.5 0.0 copy-start.2
  135.5 8.5 %all-to-all-start = ((f32[4,5,64,1024]{3,2,1,0:T(8,128)}), f32[4,5,64,1024]{3,2,1,0:T(8,128)}, u32[]{:S(2)}, u32[]{:S(2)}) async-start(f32[4,5,64,1024]{3,2,1,0:T(8,128)} %bitcast.11), calls=%async_computation | async-start | bytes 10485760 | tf_op jit(solution)/shard_map/all_to_all | solution.py:403
  144.1 1.0 fusion.16
  145.1 0.1 copy.31
  145.2 2.1 collective-permute-start.3
  147.4 0.7 copy.13
  148.0 3.4 %collective-permute-start.1 = (f32[5,1,2,1024]{3,1,0,2:T(1,128)}, f32[5,1,2,1024]{3,1,0,2:T(1,128)S(1)}, u32[]{:S(2)}, u32[]{:S(2)}) collective-permute-start(f32[5,1,2,1024]{3,1,0,2:T(1,128)} %copy.13), channel_id=1, source_target_pairs={{0,4},{1,5},{2,6},{3,7},{8,12},{9,13},{10,14},{11,15},{16,20},{17,... | collective-permute-start | bytes 122888 | tf_op jit(solution)/shard_map/ppermute | solution.py:359
  151.4 0.7 copy.12
  152.1 1.3 collective-permute-start
  153.3 1.0 copy.30
  154.3 1.4 collective-permute-start.2
  155.7 2.3 fusion.14
  158.1 1.8 copy.33
  159.9 1.5 copy.32
  161.4 10.9 %all_gather.3 = f32[5,32,1024]{2,1,0:T(8,128)S(1)} all-gather(f32[5,8,1024]{2,1,0:T(8,128)S(1)} %bitcast.10), channel_id=1, replica_groups=mesh['az'=4,'rad'=2,'ax'=4] {'ax'}, dimensions={1}, use_global_device_ids=true | all-gather | bytes 819200 | tf_op jit(solution)/shard_map/all_gather | solution.py:406
  172.2 0.0 collective-permute-done.3
  172.3 0.1 bitcast_select_fusion.3
  172.4 0.0 collective-permute-done.1
  172.4 0.0 collective-permute-done
  172.4 0.0 collective-permute-done.2
  172.4 2.4 multiply_add_fusion.2
  174.9 0.1 fusion.13
  175.0 3.4 %collective-permute-start.7 = (f32[5,32,1,1024]{3,1,0,2:T(8,128)S(1)}, f32[5,32,1,1024]{3,1,0,2:T(8,128)S(1)}, u32[]{:S(2)}, u32[]{:S(2)}) collective-permute-start(f32[5,32,1,1024]{3,1,0,2:T(8,128)S(1)} %get-tuple-element.32), channel_id=1, source_target_pairs={{0,1},{1,2},{2,3},{4,5},{5,6},{6,7},{8,9},{9,10},{10,11},{12,13},{... | collective-permute-start | bytes 1966088 | tf_op jit(solution)/shard_map/ppermute | solution.py:359
  178.4 1.3 collective-permute-start.6
  179.7 0.1 fusion.12
  179.8 1.3 collective-permute-start.4
  181.1 4.7 %collective-permute-start.5 = (f32[5,1,2,1024]{3,1,0,2:T(1,128)S(1)}, f32[5,1,2,1024]{3,1,0,2:T(1,128)S(1)}, u32[]{:S(2)}, u32[]{:S(2)}) collective-permute-start(f32[5,1,2,1024]{3,1,0,2:T(1,128)S(1)} %get-tuple-element.31), channel_id=1, source_target_pairs={{0,4},{1,5},{2,6},{3,7},{8,12},{9,13},{10,14},{11,15},{16,20},{17,... | collective-permute-start | bytes 122888 | tf_op jit(solution)/shard_map/ppermute | solution.py:359
  185.8 0.3 fusion.11
  186.1 0.0 collective-permute-done.7
  186.1 0.1 bitcast_select_fusion.2
  186.2 0.0 collective-permute-done.4
  186.2 1.2 collective-permute-done.5
  187.4 1.5 multiply_add_fusion.1
  188.9 0.1 fusion.10
  189.0 5.2 %collective-permute-start.11 = (f32[5,32,1,1024]{3,1,0,2:T(8,128)S(1)}, f32[5,32,1,1024]{3,1,0,2:T(8,128)S(1)}, u32[]{:S(2)}, u32[]{:S(2)}) collective-permute-start(f32[5,32,1,1024]{3,1,0,2:T(8,128)S(1)} %get-tuple-element.26), channel_id=1, source_target_pairs={{0,1},{1,2},{2,3},{4,5},{5,6},{6,7},{8,9},{9,10},{10,11},{12,13},{... | collective-permute-start | bytes 1966088 | tf_op jit(solution)/shard_map/ppermute | solution.py:359
  194.2 1.3 collective-permute-start.10
  195.5 0.1 fusion.9
  195.6 1.3 collective-permute-start.8
  196.9 4.5 %collective-permute-start.9 = (f32[5,1,2,1024]{3,1,0,2:T(1,128)S(1)}, f32[5,1,2,1024]{3,1,0,2:T(1,128)S(1)}, u32[]{:S(2)}, u32[]{:S(2)}) collective-permute-start(f32[5,1,2,1024]{3,1,0,2:T(1,128)S(1)} %get-tuple-element.25), channel_id=1, source_target_pairs={{0,4},{1,5},{2,6},{3,7},{8,12},{9,13},{10,14},{11,15},{16,20},{17,... | collective-permute-start | bytes 122888 | tf_op jit(solution)/shard_map/ppermute | solution.py:359
  201.5 0.3 fusion.8
  201.8 0.0 collective-permute-done.11
  201.8 0.1 bitcast_select_fusion.1
  201.9 1.4 collective-permute-done.9
  203.3 1.4 copy_add_fusion
  204.7 0.1 fusion.7
  204.9 5.2 %collective-permute-start.15 = (f32[5,32,1,1024]{3,1,0,2:T(8,128)S(1)}, f32[5,32,1,1024]{3,1,0,2:T(8,128)S(1)}, u32[]{:S(2)}, u32[]{:S(2)}) collective-permute-start(f32[5,32,1,1024]{3,1,0,2:T(8,128)S(1)} %get-tuple-element.20), channel_id=1, source_target_pairs={{0,1},{1,2},{2,3},{4,5},{5,6},{6,7},{8,9},{9,10},{10,11},{12,13},{... | collective-permute-start | bytes 1966088 | tf_op jit(solution)/shard_map/ppermute | solution.py:359
  210.0 1.3 collective-permute-start.14
  211.3 0.1 fusion.6
  211.4 1.3 collective-permute-start.12
  212.7 4.5 %collective-permute-start.13 = (f32[5,1,2,1024]{3,1,0,2:T(1,128)S(1)}, f32[5,1,2,1024]{3,1,0,2:T(1,128)S(1)}, u32[]{:S(2)}, u32[]{:S(2)}) collective-permute-start(f32[5,1,2,1024]{3,1,0,2:T(1,128)S(1)} %get-tuple-element.19), channel_id=1, source_target_pairs={{0,4},{1,5},{2,6},{3,7},{8,12},{9,13},{10,14},{11,15},{16,20},{17,... | collective-permute-start | bytes 122888 | tf_op jit(solution)/shard_map/ppermute | solution.py:359
  217.3 0.3 fusion.5
  217.6 0.0 collective-permute-done.15
  217.6 0.1 bitcast_select_fusion
  217.7 1.4 collective-permute-done.13
  219.1 0.0 collective-permute-done.14
  219.1 1.8 multiply_add_fusion
  220.9 2.1 copy.22
  223.0 37.0 %all-to-all-done = f32[4,5,64,1024]{3,2,1,0:T(8,128)} async-done(((f32[4,5,64,1024]{3,2,1,0:T(8,128)}), f32[4,5,64,1024]{3,2,1,0:T(8,128)}, u32[]{:S(2)}, u32[]{:S(2)}) %all-to-all-start) | async-done | bytes 5242912 | tf_op jit(solution)/shard_map/all_to_all | solution.py:403
  259.9 5.7 %copy.37 = f32[4,5,64,1024]{3,2,1,0:T(8,128)} copy(f32[4,5,64,1024]{3,2,1,0:T(8,128)} %all-to-all-done) | data formatting | bytes 10485760
  (18 shorter events, 0.1 us)
Async XLA Ops:
  2.1 1.0 copy-start
  3.2 0.8 copy-start.1
  135.5 8.6 %copy-start.2 = (f32[5,32,2,1024]{3,2,1,0:T(2,128)S(1)}, f32[5,32,2,1024]{3,2,1,0:T(2,128)}, u32[]{:S(2)}) copy-start(f32[5,32,2,1024]{3,2,1,0:T(2,128)} %param.9) | copy-start | bytes 3932164
  135.5 124.4 %all-to-all-start = ((f32[4,5,64,1024]{3,2,1,0:T(8,128)}), f32[4,5,64,1024]{3,2,1,0:T(8,128)}, u32[]{:S(2)}, u32[]{:S(2)}) async-start(f32[4,5,64,1024]{3,2,1,0:T(8,128)} %bitcast.11), calls=%async_computation | async-start | bytes 10485760 | tf_op jit(solution)/shard_map/all_to_all | solution.py:403
  145.2 27.0 %collective-permute-start.3 = (f32[5,32,1,1024]{3,1,0,2:T(8,128)S(1)}, f32[5,32,1,1024]{3,1,0,2:T(8,128)}, u32[]{:S(2)}, u32[]{:S(2)}) collective-permute-start(f32[5,32,1,1024]{3,1,0,2:T(8,128)S(1)} %copy.31), channel_id=1, source_target_pairs={{0,1},{1,2},{2,3},{4,5},{5,6},{6,7},{8,9},{9,10},{10,11},{12,13},{... | collective-permute-start | bytes 1966088 | tf_op jit(solution)/shard_map/ppermute | solution.py:359
  148.0 24.3 %collective-permute-start.1 = (f32[5,1,2,1024]{3,1,0,2:T(1,128)}, f32[5,1,2,1024]{3,1,0,2:T(1,128)S(1)}, u32[]{:S(2)}, u32[]{:S(2)}) collective-permute-start(f32[5,1,2,1024]{3,1,0,2:T(1,128)} %copy.13), channel_id=1, source_target_pairs={{0,4},{1,5},{2,6},{3,7},{8,12},{9,13},{10,14},{11,15},{16,20},{17,... | collective-permute-start | bytes 122888 | tf_op jit(solution)/shard_map/ppermute | solution.py:359
  152.1 20.3 %collective-permute-start = (f32[5,1,2,1024]{3,1,0,2:T(1,128)}, f32[5,1,2,1024]{3,1,0,2:T(1,128)S(1)}, u32[]{:S(2)}, u32[]{:S(2)}) collective-permute-start(f32[5,1,2,1024]{3,1,0,2:T(1,128)} %copy.12), channel_id=1, source_target_pairs={{4,0},{5,1},{6,2},{7,3},{12,8},{13,9},{14,10},{15,11},{20,16},{21,... | collective-permute-start | bytes 122888 | tf_op jit(solution)/shard_map/ppermute | solution.py:359
  154.3 3.7 %copy-start.6 = (s32[32,2]{0,1:T(2,128)S(1)}, s32[32,2]{0,1:T(2,128)}, u32[]{:S(2)}) copy-start(s32[32,2]{0,1:T(2,128)} %param.11) | copy-start | bytes 772
  154.3 18.1 %collective-permute-start.2 = (f32[5,32,1,1024]{3,1,0,2:T(8,128)}, f32[5,32,1,1024]{3,1,0,2:T(8,128)}, u32[]{:S(2)}, u32[]{:S(2)}) collective-permute-start(f32[5,32,1,1024]{3,1,0,2:T(8,128)} %copy.30), channel_id=1, source_target_pairs={{1,0},{2,1},{3,2},{5,4},{6,5},{7,6},{9,8},{10,9},{11,10},{13,12},{... | collective-permute-start | bytes 1966088 | tf_op jit(solution)/shard_map/ppermute | solution.py:359
  158.0 1.8 copy-start.4
  161.4 11.0 %copy-start.3 = (f32[5,31,2,1024]{3,1,0,2:T(8,128)S(1)}, f32[5,31,2,1024]{3,1,0,2:T(8,128)}, u32[]{:S(2)}) copy-start(f32[5,31,2,1024]{3,1,0,2:T(8,128)} %copy.32) | copy-start | bytes 3809284
  161.4 11.0 %copy-start.5 = (f32[5]{0:T(128)S(1)}, f32[5]{0:T(128)}, u32[]{:S(2)}) copy-start(f32[5]{0:T(128)} %constant.50) | copy-start | bytes 64
  175.0 11.1 %collective-permute-start.7 = (f32[5,32,1,1024]{3,1,0,2:T(8,128)S(1)}, f32[5,32,1,1024]{3,1,0,2:T(8,128)S(1)}, u32[]{:S(2)}, u32[]{:S(2)}) collective-permute-start(f32[5,32,1,1024]{3,1,0,2:T(8,128)S(1)} %get-tuple-element.32), channel_id=1, source_target_pairs={{0,1},{1,2},{2,3},{4,5},{5,6},{6,7},{8,9},{9,10},{10,11},{12,13},{... | collective-permute-start | bytes 1966088 | tf_op jit(solution)/shard_map/ppermute | solution.py:359
  178.4 9.0 %collective-permute-start.6 = (f32[5,32,1,1024]{3,1,0,2:T(8,128)S(1)}, f32[5,32,1,1024]{3,1,0,2:T(8,128)S(1)}, u32[]{:S(2)}, u32[]{:S(2)}) collective-permute-start(f32[5,32,1,1024]{3,1,0,2:T(8,128)S(1)} %get-tuple-element.33), channel_id=1, source_target_pairs={{1,0},{2,1},{3,2},{5,4},{6,5},{7,6},{9,8},{10,9},{11,10},{13,12},{... | collective-permute-start | bytes 1966088 | tf_op jit(solution)/shard_map/ppermute | solution.py:359
  179.8 6.5 %collective-permute-start.4 = (f32[5,1,2,1024]{3,1,0,2:T(1,128)S(1)}, f32[5,1,2,1024]{3,1,0,2:T(1,128)S(1)}, u32[]{:S(2)}, u32[]{:S(2)}) collective-permute-start(f32[5,1,2,1024]{3,1,0,2:T(1,128)S(1)} %get-tuple-element.30), channel_id=1, source_target_pairs={{4,0},{5,1},{6,2},{7,3},{12,8},{13,9},{14,10},{15,11},{20,16},{21,... | collective-permute-start | bytes 122888 | tf_op jit(solution)/shard_map/ppermute | solution.py:359
  181.1 6.4 %collective-permute-start.5 = (f32[5,1,2,1024]{3,1,0,2:T(1,128)S(1)}, f32[5,1,2,1024]{3,1,0,2:T(1,128)S(1)}, u32[]{:S(2)}, u32[]{:S(2)}) collective-permute-start(f32[5,1,2,1024]{3,1,0,2:T(1,128)S(1)} %get-tuple-element.31), channel_id=1, source_target_pairs={{0,4},{1,5},{2,6},{3,7},{8,12},{9,13},{10,14},{11,15},{16,20},{17,... | collective-permute-start | bytes 122888 | tf_op jit(solution)/shard_map/ppermute | solution.py:359
  189.0 12.7 %collective-permute-start.11 = (f32[5,32,1,1024]{3,1,0,2:T(8,128)S(1)}, f32[5,32,1,1024]{3,1,0,2:T(8,128)S(1)}, u32[]{:S(2)}, u32[]{:S(2)}) collective-permute-start(f32[5,32,1,1024]{3,1,0,2:T(8,128)S(1)} %get-tuple-element.26), channel_id=1, source_target_pairs={{0,1},{1,2},{2,3},{4,5},{5,6},{6,7},{8,9},{9,10},{10,11},{12,13},{... | collective-permute-start | bytes 1966088 | tf_op jit(solution)/shard_map/ppermute | solution.py:359
  194.2 9.1 %collective-permute-start.10 = (f32[5,32,1,1024]{3,1,0,2:T(8,128)S(1)}, f32[5,32,1,1024]{3,1,0,2:T(8,128)S(1)}, u32[]{:S(2)}, u32[]{:S(2)}) collective-permute-start(f32[5,32,1,1024]{3,1,0,2:T(8,128)S(1)} %get-tuple-element.27), channel_id=1, source_target_pairs={{1,0},{2,1},{3,2},{5,4},{6,5},{7,6},{9,8},{10,9},{11,10},{13,12},{... | collective-permute-start | bytes 1966088 | tf_op jit(solution)/shard_map/ppermute | solution.py:359
  195.6 6.3 %collective-permute-start.8 = (f32[5,1,2,1024]{3,1,0,2:T(1,128)S(1)}, f32[5,1,2,1024]{3,1,0,2:T(1,128)S(1)}, u32[]{:S(2)}, u32[]{:S(2)}) collective-permute-start(f32[5,1,2,1024]{3,1,0,2:T(1,128)S(1)} %get-tuple-element.24), channel_id=1, source_target_pairs={{4,0},{5,1},{6,2},{7,3},{12,8},{13,9},{14,10},{15,11},{20,16},{21,... | collective-permute-start | bytes 122888 | tf_op jit(solution)/shard_map/ppermute | solution.py:359
  196.9 6.4 %collective-permute-start.9 = (f32[5,1,2,1024]{3,1,0,2:T(1,128)S(1)}, f32[5,1,2,1024]{3,1,0,2:T(1,128)S(1)}, u32[]{:S(2)}, u32[]{:S(2)}) collective-permute-start(f32[5,1,2,1024]{3,1,0,2:T(1,128)S(1)} %get-tuple-element.25), channel_id=1, source_target_pairs={{0,4},{1,5},{2,6},{3,7},{8,12},{9,13},{10,14},{11,15},{16,20},{17,... | collective-permute-start | bytes 122888 | tf_op jit(solution)/shard_map/ppermute | solution.py:359
  204.9 12.7 %collective-permute-start.15 = (f32[5,32,1,1024]{3,1,0,2:T(8,128)S(1)}, f32[5,32,1,1024]{3,1,0,2:T(8,128)S(1)}, u32[]{:S(2)}, u32[]{:S(2)}) collective-permute-start(f32[5,32,1,1024]{3,1,0,2:T(8,128)S(1)} %get-tuple-element.20), channel_id=1, source_target_pairs={{0,1},{1,2},{2,3},{4,5},{5,6},{6,7},{8,9},{9,10},{10,11},{12,13},{... | collective-permute-start | bytes 1966088 | tf_op jit(solution)/shard_map/ppermute | solution.py:359
  210.0 9.1 %collective-permute-start.14 = (f32[5,32,1,1024]{3,1,0,2:T(8,128)S(1)}, f32[5,32,1,1024]{3,1,0,2:T(8,128)S(1)}, u32[]{:S(2)}, u32[]{:S(2)}) collective-permute-start(f32[5,32,1,1024]{3,1,0,2:T(8,128)S(1)} %get-tuple-element.21), channel_id=1, source_target_pairs={{1,0},{2,1},{3,2},{5,4},{6,5},{7,6},{9,8},{10,9},{11,10},{13,12},{... | collective-permute-start | bytes 1966088 | tf_op jit(solution)/shard_map/ppermute | solution.py:359
  211.4 6.3 %collective-permute-start.12 = (f32[5,1,2,1024]{3,1,0,2:T(1,128)S(1)}, f32[5,1,2,1024]{3,1,0,2:T(1,128)S(1)}, u32[]{:S(2)}, u32[]{:S(2)}) collective-permute-start(f32[5,1,2,1024]{3,1,0,2:T(1,128)S(1)} %get-tuple-element.18), channel_id=1, source_target_pairs={{4,0},{5,1},{6,2},{7,3},{12,8},{13,9},{14,10},{15,11},{20,16},{21,... | collective-permute-start | bytes 122888 | tf_op jit(solution)/shard_map/ppermute | solution.py:359
  212.7 6.4 %collective-permute-start.13 = (f32[5,1,2,1024]{3,1,0,2:T(1,128)S(1)}, f32[5,1,2,1024]{3,1,0,2:T(1,128)S(1)}, u32[]{:S(2)}, u32[]{:S(2)}) collective-permute-start(f32[5,1,2,1024]{3,1,0,2:T(1,128)S(1)} %get-tuple-element.19), channel_id=1, source_target_pairs={{0,4},{1,5},{2,6},{3,7},{8,12},{9,13},{10,14},{11,15},{16,20},{17,... | collective-permute-start | bytes 122888 | tf_op jit(solution)/shard_map/ppermute | solution.py:359
